TPU v7x, 256 devices: a whole 4x4x8 slice. The times are simulated.
256 devices in a mesh: tm: 8 (over x_hi, y), rows: 32 (over z, x_lo, core).
Axes of the slice: x: 4 (x_hi: 2, x_lo: 2; x = x_hi * 2 + x_lo), y: 4, z: 8, core: 2. Of those that a mesh axis runs over, the one named last changes fastest.
Arguments:
- features: bfloat16 [32, 64, 64, 384], P('tm', 'rows'), may hold values from -6 to 6
- first_weight: bfloat16 [3, 3, 3, 384, 192], replicated, may hold values from -0.0625 to 0.0625
- first_bias: float32 [192], replicated, may hold values from -1.5 to 1.5
- first_gain: float32 [384], replicated, may hold values from 0.25 to 1.75
- second_weight: bfloat16 [3, 3, 3, 192, 192], replicated, may hold values from -0.078125 to 0.078125
- second_bias: float32 [192], replicated, may hold values from -1.5 to 1.5
- second_gain: float32 [192], replicated, may hold values from 0.25 to 1.75
- skip_weight: bfloat16 [384, 192], replicated, may hold values from -0.3125 to 0.3125
- skip_bias: float32 [192], replicated, may hold values from -1.5 to 1.5
Outputs:
- block_out: bfloat16 [32, 64, 64, 192], P('tm', 'rows')
All inputs are finite; a program needn't handle non-finite values.
Results may differ from a plain program's by a relative error of at most 0.01.
Values may be sent and summed in bfloat16 or wider, within the bound.
No kernel may reach another device: no remote copies, remote signals or barrier semaphores. Data moves between devices by JAX's collectives and lax.ppermute only.
A program may use at most 64 MiB of HBM per device.

v0:
```python
import jax
import jax.numpy as jnp
from jax import lax
from jax.sharding import PartitionSpec as P


def extended(cells, sides, width):
    for axis, dim in sides:
        count = lax.axis_size(axis)
        ends = count - 1
        head = lax.slice_in_dim(cells, 0, width, axis=dim)
        tail = lax.slice_in_dim(cells, cells.shape[dim] - width, cells.shape[dim], axis=dim)
        cells = jnp.concatenate(
            [
                lax.ppermute(tail, axis, [(i, (i + 1) % count) for i in range(ends)]),
                cells,
                lax.ppermute(head, axis, [((i + 1) % count, i) for i in range(ends)]),
            ],
            axis=dim,
        )
    return cells


def from_behind(value, axis, steps):
    count = lax.axis_size(axis)
    initial, last = (max(0, -steps), min(count, count - steps))
    return lax.ppermute(value, axis, [(source, source + steps) for source in range(initial, last)])


def activate(values, gain):
    floats = values.astype(jnp.float32)
    scaled = floats * lax.rsqrt(jnp.mean(floats * floats, axis=-1, keepdims=True) + 1e-06) * gain
    return jax.nn.silu(scaled).astype(jnp.bfloat16)


def convolve(padded, weight, bias):
    frames = padded.shape[0] - 2
    height = padded.shape[1] - 2
    across = padded.shape[2]
    channels = padded.shape[3]
    outputs = weight.shape[4]
    widened = jnp.pad(padded, ((0, 0), (0, 0), (1, 1), (0, 0)))
    summed = jnp.zeros((frames * height * across, outputs), jnp.float32)
    for time_tap in range(3):
        for row_tap in range(3):
            stacked = jnp.concatenate(
                [
                    widened[
                        time_tap : time_tap + frames,
                        row_tap : row_tap + height,
                        col_tap : col_tap + across,
                    ]
                    for col_tap in range(3)
                ],
                axis=-1,
            )
            summed = summed + jnp.dot(
                stacked.reshape(-1, 3 * channels),
                weight[time_tap, row_tap].reshape(3 * channels, outputs),
                preferred_element_type=jnp.float32,
            )
    return summed.reshape(frames, height, across, outputs) + bias


def per_device(
    features,
    first_weight,
    first_bias,
    first_gain,
    second_weight,
    second_bias,
    second_gain,
    skip_weight,
    skip_bias,
):
    frames = features.shape[0]
    first_act = activate(features, first_gain)
    rimmed = extended(first_act, (("rows", 1),), 1)
    earlier = from_behind(rimmed[frames - 2 :], "tm", 1)
    hidden = convolve(jnp.concatenate([earlier, rimmed], 0), first_weight, first_bias).astype(
        jnp.bfloat16
    )
    second_act = activate(hidden, second_gain)
    rimmed = extended(second_act, (("rows", 1),), 1)
    earlier = from_behind(rimmed[frames - 2 :], "tm", 1)
    branch = convolve(jnp.concatenate([earlier, rimmed], 0), second_weight, second_bias)
    skipped = jnp.dot(
        features.reshape(-1, features.shape[-1]), skip_weight, preferred_element_type=jnp.float32
    )
    skipped = skipped.reshape(branch.shape)
    return (branch + skipped + skip_bias).astype(jnp.bfloat16)


def solution(mesh):
    return jax.shard_map(
        per_device,
        mesh=mesh,
        in_specs=(P("tm", "rows", None, None), P(), P(), P(), P(), P(), P(), P(), P()),
        out_specs=P("tm", "rows", None, None),
        check_vma=False,
    )
```

profile of v0, /device:TPU:132, one launch (start us, length us, event | category | flops | bytes accessed | tf_op | source)
XLA Modules:
  0.0 70.0 jit_solution(10249403080349559298)
XLA Ops:
  0.0 1.2 %fusion.6 = f32[4,2,64]{2,1,0:T(2,128)S(1)} fusion(bf16[4,2,64,384]{3,2,1,0:T(8,128)(2,1)} %param.9), kind=kLoop, calls=%fused_computation.35 | loop fusion | flops 589312 | bytes 395264 | tf_op jit(solution)/shard_map/reduce_sum | solution.py:32
  1.2 1.3 %fusion.13 = bf16[4,2,64,384]{3,2,1,0:T(8,128)(2,1)S(1)} fusion(bf16[4,2,64,384]{3,2,1,0:T(8,128)(2,1)} %param.9, f32[384]{0:T(512)} %param.12, f32[4,2,64]{2,1,0:T(2,128)S(1)} %add_rsqrt_fusion), kind=kLoop, calls=%fused_computation.42 | loop fusion | flops 1572864 | bytes 790016 | tf_op jit(solution)/shard_map/convert_element_type | solution.py:33
  2.6 2.1 %collective-permute-start.1 = (bf16[4,1,64,384]{3,2,1,0:T(8,128)(2,1)S(1)}, bf16[4,1,64,384]{3,2,1,0:T(8,128)(2,1)S(1)}, u32[]{:S(2)}, u32[]{:S(2)}) collective-permute-start(bf16[4,1,64,384]{3,2,1,0:T(8,128)(2,1)S(1)} %get-tuple-element.75), channel_id=1, source_target_pairs={{1,0},{2,1},{3,2},{4,3},{5,4},{6,5},{7,6},{8,7},{9,8},{10,9},{11,1... | collective-permute-start | bytes 589832 | tf_op jit(solution)/shard_map/ppermute | solution.py:17
  4.7 2.2 %collective-permute-start = (bf16[4,1,64,384]{3,2,1,0:T(8,128)(2,1)S(1)}, bf16[4,1,64,384]{3,2,1,0:T(8,128)(2,1)S(1)}, u32[]{:S(2)}, u32[]{:S(2)}) collective-permute-start(bf16[4,1,64,384]{3,2,1,0:T(8,128)(2,1)S(1)} %get-tuple-element.74), channel_id=1, source_target_pairs={{0,1},{1,2},{2,3},{3,4},{4,5},{5,6},{6,7},{7,8},{8,9},{9,10},{10,1... | collective-permute-start | bytes 589832 | tf_op jit(solution)/shard_map/ppermute | solution.py:15
  6.9 0.9 %collective-permute-done.1 = bf16[4,1,64,384]{3,2,1,0:T(8,128)(2,1)S(1)} collective-permute-done((bf16[4,1,64,384]{3,2,1,0:T(8,128)(2,1)S(1)}, bf16[4,1,64,384]{3,2,1,0:T(8,128)(2,1)S(1)}, u32[]{:S(2)}, u32[]{:S(2)}) %collective-permute-start.1) | collective-permute-done | bytes 196640 | tf_op jit(solution)/shard_map/ppermute | solution.py:17
  7.8 5.9 %collective-permute-done = bf16[4,1,64,384]{3,2,1,0:T(8,128)(2,1)S(1)} collective-permute-done((bf16[4,1,64,384]{3,2,1,0:T(8,128)(2,1)S(1)}, bf16[4,1,64,384]{3,2,1,0:T(8,128)(2,1)S(1)}, u32[]{:S(2)}, u32[]{:S(2)}) %collective-permute-start) | collective-permute-done | bytes 196640 | tf_op jit(solution)/shard_map/ppermute | solution.py:15
  13.8 3.5 %collective-permute-start.2 = (bf16[2,4,64,384]{3,2,1,0:T(8,128)(2,1)S(1)}, bf16[2,4,64,384]{3,2,1,0:T(8,128)(2,1)S(1)}, u32[]{:S(2)}, u32[]{:S(2)}) collective-permute-start(bf16[2,4,64,384]{3,2,1,0:T(8,128)(2,1)S(1)} %pad_maximum_fusion.18), channel_id=1, source_target_pairs={{0,32},{32,64},{64,96},{96,128},{128,160},{160,192},{192,224},{1,3... | collective-permute-start | bytes 1179656 | tf_op jit(solution)/shard_map/ppermute | solution.py:27
  17.3 2.5 %fusion.19 = (bf16[1,1,3,384,192]{3,4,2,1,0:T(8,128)(2,1)S(1)}, bf16[1,1,3,384,192]{3,4,2,1,0:T(8,128)(2,1)S(1)}, bf16[1,1,3,384,192]{3,4,2,1,0:T(8,128)(2,1)S(1...) fusion(bf16[3,3,3,384,192]{3,4,2,1,0:T(8,128)(2,1)} %param.10), kind=kLoop, calls=%fused_computation.104 | loop fusion | bytes 7962624 | tf_op jit(solution)/shard_map/slice | solution.py:59
  19.8 0.4 copy.11
  20.3 0.4 copy.12
  20.8 0.4 copy.13
  21.2 0.4 copy.14
  21.7 0.4 copy.15
  22.1 0.4 copy.16
  22.6 0.4 copy.17
  23.1 0.4 copy.18
  23.5 0.4 copy.19
  24.0 4.0 %collective-permute-done.2 = bf16[2,4,64,384]{3,2,1,0:T(8,128)(2,1)S(1)} collective-permute-done((bf16[2,4,64,384]{3,2,1,0:T(8,128)(2,1)S(1)}, bf16[2,4,64,384]{3,2,1,0:T(8,128)(2,1)S(1)}, u32[]{:S(2)}, u32[]{:S(2)}) %collective-permute-start.2) | collective-permute-done | bytes 393248 | tf_op jit(solution)/shard_map/ppermute | solution.py:27
  28.0 0.2 maximum_maximum_fusion
  28.2 0.8 %pad_slice_fusion.19 = (bf16[4,2,64,384]{3,2,1,0:T(8,128)(2,1)S(1)}, bf16[4,2,64,384]{3,2,1,0:T(8,128)(2,1)S(1)}, bf16[4,2,64,384]{3,2,1,0:T(8,128)(2,1)S(1)}, b...) fusion(bf16[6,4,64,384]{3,2,1,0:T(8,128)(2,1)S(1)} %maximum_max, ...), kind=kLoop, calls=%fused_computation.87 | loop fusion | bytes 5505024 | tf_op jit(solution)/shard_map/slice | solution.py:48
  29.0 0.2 fusion.21
  29.2 0.8 %pad_slice_fusion.18 = (bf16[4,2,64,384]{3,2,1,0:T(8,128)(2,1)S(1)}, bf16[4,2,64,384]{3,2,1,0:T(8,128)(2,1)S(1)}, bf16[4,2,64,384]{3,2,1,0:T(8,128)(2,1)S(1)}, b...) fusion(bf16[6,4,64,384]{3,2,1,0:T(8,128)(2,1)S(1)} %maximum_max, ...), kind=kLoop, calls=%fused_computation.86 | loop fusion | bytes 6684672 | tf_op jit(solution)/shard_map/slice | solution.py:48
  30.1 0.3 pad_maximum_fusion.2
  30.4 0.5 fusion.25
  31.0 0.5 convolution_add_fusion.8
  31.5 0.3 pad_maximum_fusion.4
  31.9 0.5 convolution_add_fusion.7
  32.4 0.5 convolution_add_fusion.6
  33.0 0.3 pad_maximum_fusion.6
  33.3 0.5 convolution_add_fusion.5
  33.9 0.5 convolution_add_fusion.4
  34.4 0.4 fusion.3
  34.9 0.6 convolution_add_fusion.3
  35.4 0.6 convolution_add_fusion.2
  36.1 1.3 %multiply_reduce_fusion = (f32[512]{0:T(512)S(1)}, f32[512,192]{0,1:T(8,128)}) fusion(f32[192]{0:T(256)S(1)} %copy-done.3, f32[512,192]{0,1:T(8,128)S(1)} %convolution_add_fusion.2, bf16[512,1152]{1,0:T(8,128)(2,1)S(1)} %bitcast.116, bf16[1152,192]{0,1:T(8,128)(2,1)S(1)} %bitcast.145), kind=kOutput, calls=%fused_computation.61 | convolution fusion | flops 227081728 | bytes 2411264 | tf_op jit(solution)/shard_map/dot_general | solution.py:57
  37.4 1.3 %copy.20 = f32[512,192]{1,0:T(8,128)S(1)} copy(f32[512,192]{0,1:T(8,128)} %get-tuple-element.82) | data formatting | bytes 786432 | tf_op jit(solution)/shard_map/add | solution.py:57
  38.9 0.2 multiply_convert_fusion
  39.1 1.9 %collective-permute-start.4 = (bf16[4,1,64,192]{3,2,1,0:T(8,128)(2,1)S(1)}, bf16[4,1,64,192]{3,2,1,0:T(8,128)(2,1)S(1)}, u32[]{:S(2)}, u32[]{:S(2)}) collective-permute-start(bf16[4,1,64,192]{3,2,1,0:T(8,128)(2,1)S(1)} %get-tuple-element.80), channel_id=1, source_target_pairs={{1,0},{2,1},{3,2},{4,3},{5,4},{6,5},{7,6},{8,7},{9,8},{10,9},{11,1... | collective-permute-start | bytes 294920 | tf_op jit(solution)/shard_map/ppermute | solution.py:17
  41.0 2.4 %collective-permute-start.3 = (bf16[4,1,64,192]{3,2,1,0:T(8,128)(2,1)S(1)}, bf16[4,1,64,192]{3,2,1,0:T(8,128)(2,1)S(1)}, u32[]{:S(2)}, u32[]{:S(2)}) collective-permute-start(bf16[4,1,64,192]{3,2,1,0:T(8,128)(2,1)S(1)} %get-tuple-element.79), channel_id=1, source_target_pairs={{0,1},{1,2},{2,3},{3,4},{4,5},{5,6},{6,7},{7,8},{8,9},{9,10},{10,1... | collective-permute-start | bytes 294920 | tf_op jit(solution)/shard_map/ppermute | solution.py:15
  43.5 5.9 %collective-permute-done.3 = bf16[4,1,64,192]{3,2,1,0:T(8,128)(2,1)S(1)} collective-permute-done((bf16[4,1,64,192]{3,2,1,0:T(8,128)(2,1)S(1)}, bf16[4,1,64,192]{3,2,1,0:T(8,128)(2,1)S(1)}, u32[]{:S(2)}, u32[]{:S(2)}) %collective-permute-start.3) | collective-permute-done | bytes 98336 | tf_op jit(solution)/shard_map/ppermute | solution.py:15
  49.5 2.1 %collective-permute-start.5 = (bf16[2,4,64,192]{3,2,1,0:T(8,128)(2,1)S(1)}, bf16[2,4,64,192]{3,2,1,0:T(8,128)(2,1)S(1)}, u32[]{:S(2)}, u32[]{:S(2)}) collective-permute-start(bf16[2,4,64,192]{3,2,1,0:T(8,128)(2,1)S(1)} %pad_maximum_fusion.20), channel_id=1, source_target_pairs={{0,32},{32,64},{64,96},{96,128},{128,160},{160,192},{192,224},{1,3... | collective-permute-start | bytes 589832 | tf_op jit(solution)/shard_map/ppermute | solution.py:27
  51.6 0.2 fusion.20
  51.8 9.6 %collective-permute-done.5 = bf16[2,4,64,192]{3,2,1,0:T(8,128)(2,1)S(1)} collective-permute-done((bf16[2,4,64,192]{3,2,1,0:T(8,128)(2,1)S(1)}, bf16[2,4,64,192]{3,2,1,0:T(8,128)(2,1)S(1)}, u32[]{:S(2)}, u32[]{:S(2)}) %collective-permute-start.5) | collective-permute-done | bytes 196640 | tf_op jit(solution)/shard_map/ppermute | solution.py:27
  61.5 0.5 pad_slice_fusion.1
  62.2 0.5 pad_slice_fusion
  62.6 0.2 pad_maximum_fusion.11
  62.9 0.4 fusion.26
  63.3 0.2 pad_maximum_fusion.12
  63.5 0.4 convolution_add_fusion.16
  63.9 0.2 pad_maximum_fusion.13
  64.1 0.4 convolution_add_fusion.15
  64.5 0.2 pad_maximum_fusion.14
  64.7 0.4 convolution_add_fusion.14
  65.1 0.2 pad_maximum_fusion.15
  65.4 0.4 convolution_add_fusion.13
  65.8 0.2 pad_maximum_fusion.16
  66.0 0.4 convolution_add_fusion.12
  66.4 0.8 %fusion.15 = (bf16[4,2,64,576]{3,2,1,0:T(8,128)(2,1)S(1)}, bf16[4,2,64,576]{3,2,1,0:T(8,128)(2,1)S(1)}, bf16[4,2,64,576]{3,2,1,0:T(8,128)(2,1)S(1)}) fusion(bf16[4,1,64,192]{3,2,1,0:T(8,128)(2,1)S(1)} %collective-permute-done.4, bf16[4,2,64,192]{3,2,1,0:T(8,128)(2,1)S(1)} %multiply_convert_fusion, bf16[4,2,64,192]{3,2,1,0:T(8,128)(2,1)S(1)} %get-tuple-element.57, ...), kind=kLoop, calls=%fused_computation.46 | loop fusion | flops 6488064 | bytes 3342336 | tf_op jit(solution)/shard_map/concatenate | solution.py:46
  67.2 0.4 convolution_add_fusion.11
  67.6 0.4 convolution_add_fusion.10
  68.0 0.4 convolution_add_fusion.9
  68.4 0.2 copy.21
  68.6 0.3 copy-done.1
  69.0 1.0 %fusion.1 = bf16[4,2,64,192]{3,2,1,0:T(8,128)(2,1)} fusion(bf16[4,2,64,384]{3,2,1,0:T(8,128)(2,1)S(1)} %copy-done.1, f32[4,2,64,192]{3,2,1,0:T(8,128)S(1)} %bitcast.144, f32[192]{0:T(256)S(1)} %copy-done.5, f32[192]{0:T(256)S(1)} %copy-done.6, bf16[384,192]{0,1:T(8,128)(2,1)S(1)} %copy-done), kind=kOutput, calls=%fused_computation.2 | convolution fusion | flops 75890688 | bytes 1132032 | tf_op jit(solution)/shard_map/dot_general | solution.py:87
  (32 shorter events, 1.3 us)
Async XLA Ops:
  0.0 68.6 %copy-start = (bf16[384,192]{0,1:T(8,128)(2,1)S(1)}, bf16[384,192]{0,1:T(8,128)(2,1)}, u32[]{:S(2)}) copy-start(bf16[384,192]{0,1:T(8,128)(2,1)} %param.16) | copy-start | bytes 442372
  2.6 5.3 %collective-permute-start.1 = (bf16[4,1,64,384]{3,2,1,0:T(8,128)(2,1)S(1)}, bf16[4,1,64,384]{3,2,1,0:T(8,128)(2,1)S(1)}, u32[]{:S(2)}, u32[]{:S(2)}) collective-permute-start(bf16[4,1,64,384]{3,2,1,0:T(8,128)(2,1)S(1)} %get-tuple-element.75), channel_id=1, source_target_pairs={{1,0},{2,1},{3,2},{4,3},{5,4},{6,5},{7,6},{8,7},{9,8},{10,9},{11,1... | collective-permute-start | bytes 589832 | tf_op jit(solution)/shard_map/ppermute | solution.py:17
  4.7 9.1 %collective-permute-start = (bf16[4,1,64,384]{3,2,1,0:T(8,128)(2,1)S(1)}, bf16[4,1,64,384]{3,2,1,0:T(8,128)(2,1)S(1)}, u32[]{:S(2)}, u32[]{:S(2)}) collective-permute-start(bf16[4,1,64,384]{3,2,1,0:T(8,128)(2,1)S(1)} %get-tuple-element.74), channel_id=1, source_target_pairs={{0,1},{1,2},{2,3},{3,4},{4,5},{5,6},{6,7},{7,8},{8,9},{9,10},{10,1... | collective-permute-start | bytes 589832 | tf_op jit(solution)/shard_map/ppermute | solution.py:15
  13.8 14.2 %collective-permute-start.2 = (bf16[2,4,64,384]{3,2,1,0:T(8,128)(2,1)S(1)}, bf16[2,4,64,384]{3,2,1,0:T(8,128)(2,1)S(1)}, u32[]{:S(2)}, u32[]{:S(2)}) collective-permute-start(bf16[2,4,64,384]{3,2,1,0:T(8,128)(2,1)S(1)} %pad_maximum_fusion.18), channel_id=1, source_target_pairs={{0,32},{32,64},{64,96},{96,128},{128,160},{160,192},{192,224},{1,3... | collective-permute-start | bytes 1179656 | tf_op jit(solution)/shard_map/ppermute | solution.py:27
  35.4 0.7 copy-start.3
  36.1 2.8 %copy-start.4 = (f32[192]{0:T(256)S(1)}, f32[192]{0:T(256)}, u32[]{:S(2)}) copy-start(f32[192]{0:T(256)} %param.15) | copy-start | bytes 2308
  37.4 14.2 %copy-start.2 = (bf16[3,3,3,192,192]{4,3,2,1,0:T(8,128)(2,1)S(1)}, bf16[3,3,3,192,192]{4,3,2,1,0:T(8,128)(2,1)}, u32[]{:S(2)}) copy-start(bf16[3,3,3,192,192]{4,3,2,1,0:T(8,128)(2,1)} %param.13) | copy-start | bytes 5971972
  39.1 4.4 %collective-permute-start.4 = (bf16[4,1,64,192]{3,2,1,0:T(8,128)(2,1)S(1)}, bf16[4,1,64,192]{3,2,1,0:T(8,128)(2,1)S(1)}, u32[]{:S(2)}, u32[]{:S(2)}) collective-permute-start(bf16[4,1,64,192]{3,2,1,0:T(8,128)(2,1)S(1)} %get-tuple-element.80), channel_id=1, source_target_pairs={{1,0},{2,1},{3,2},{4,3},{5,4},{6,5},{7,6},{8,7},{9,8},{10,9},{11,1... | collective-permute-start | bytes 294920 | tf_op jit(solution)/shard_map/ppermute | solution.py:17
  41.0 8.4 %collective-permute-start.3 = (bf16[4,1,64,192]{3,2,1,0:T(8,128)(2,1)S(1)}, bf16[4,1,64,192]{3,2,1,0:T(8,128)(2,1)S(1)}, u32[]{:S(2)}, u32[]{:S(2)}) collective-permute-start(bf16[4,1,64,192]{3,2,1,0:T(8,128)(2,1)S(1)} %get-tuple-element.79), channel_id=1, source_target_pairs={{0,1},{1,2},{2,3},{3,4},{4,5},{5,6},{6,7},{7,8},{8,9},{9,10},{10,1... | collective-permute-start | bytes 294920 | tf_op jit(solution)/shard_map/ppermute | solution.py:15
  49.5 11.9 %collective-permute-start.5 = (bf16[2,4,64,192]{3,2,1,0:T(8,128)(2,1)S(1)}, bf16[2,4,64,192]{3,2,1,0:T(8,128)(2,1)S(1)}, u32[]{:S(2)}, u32[]{:S(2)}) collective-permute-start(bf16[2,4,64,192]{3,2,1,0:T(8,128)(2,1)S(1)} %pad_maximum_fusion.20), channel_id=1, source_target_pairs={{0,32},{32,64},{64,96},{96,128},{128,160},{160,192},{192,224},{1,3... | collective-permute-start | bytes 589832 | tf_op jit(solution)/shard_map/ppermute | solution.py:27
  68.0 1.0 %copy-start.1 = (bf16[4,2,64,384]{3,2,1,0:T(8,128)(2,1)S(1)}, bf16[4,2,64,384]{3,2,1,0:T(8,128)(2,1)}, u32[]{:S(2)}) copy-start(bf16[4,2,64,384]{3,2,1,0:T(8,128)(2,1)} %param.9) | copy-start | bytes 1179652
  68.0 1.0 %copy-start.5 = (f32[192]{0:T(256)S(1)}, f32[192]{0:T(256)}, u32[]{:S(2)}) copy-start(f32[192]{0:T(256)} %param.17) | copy-start | bytes 2308
  68.0 1.0 %copy-start.6 = (f32[192]{0:T(256)S(1)}, f32[192]{0:T(256)}, u32[]{:S(2)}) copy-start(f32[192]{0:T(256)} %param.14) | copy-start | bytes 2308
where the time goes:
time: 71.1 us; the launch traced here: 70 us
  waiting for transfers between devices  26.4 us (37%)
  starting transfers between devices  14.2 us (20%)
  local copies, waits for them, and re-layouts  11.8 us (17%)
  matrix products  10.2 us (14%)
  other arithmetic  6.7 us (9%)
    ppermute x2, waiting for transfers between devices, from_behind(): lax.ppermute(value, axis, [(source, source + steps) for source in range(i...  13.6 us
    ppermute x2, waiting for transfers between devices, extended(): lax.ppermute(tail, axis, [(i, (i + 1) % count) for i in range(ends)])  11.8 us
    dot_general x18, matrix products, convolve(): jnp.dot(stacked.reshape(-1, 3 * channels), weight[time_tap, row_tap].resh...  9.22 us
    slice x11, local copies, waits for them, and re-layouts, convolve(): weight[time_tap, row_tap].reshape(3 * channels, outputs)  6.14 us
    ppermute x2, starting transfers between devices, from_behind(): lax.ppermute(value, axis, [(source, source + steps) for source in range(i...  5.59 us
    ppermute x2, starting transfers between devices, extended(): lax.ppermute(tail, axis, [(i, (i + 1) % count) for i in range(ends)])  4.64 us
    ppermute x2, starting transfers between devices, extended(): lax.ppermute(head, axis, [((i + 1) % count, i) for i in range(ends)])  4.01 us
    concatenate x11, other arithmetic, convolve(): jnp.concatenate([widened[time_tap:time_tap + frames, row_tap:row_tap + he...  3.53 us
  transfers between devices with their start and end apart: 6, of which 6 were waited for; matrix products, arithmetic and copies ran while one was open for 10% of the time, Pallas kernels for 0%

commit v1 on v0

v1 whole, which is shorter than its diff:
```python
import jax
import jax.numpy as jnp
from jax import lax
from jax.experimental import pallas as pl
from jax.experimental.pallas import tpu as pltpu
from jax.sharding import PartitionSpec as P

F32 = jnp.float32
BF16 = jnp.bfloat16
COLS = 64
VMEM = pl.BlockSpec(memory_space=pltpu.VMEM)


def call(body, outs, *args, flops=0, scratch=(), limit=8):
    moved = sum(a.size * a.dtype.itemsize for a in args) + sum(o.size * o.dtype.itemsize for o in outs)
    return pl.pallas_call(
        body,
        out_shape=outs,
        in_specs=[VMEM] * len(args),
        out_specs=[VMEM] * len(outs),
        scratch_shapes=list(scratch),
        compiler_params=pltpu.CompilerParams(vmem_limit_bytes=limit << 20),
        cost_estimate=pl.CostEstimate(flops=flops, bytes_accessed=moved, transcendentals=0),
    )(*args)


def act(values, gain):
    mean = jnp.mean(values * values, axis=-1, keepdims=True)
    scaled = values * lax.rsqrt(mean + 1e-06) * gain
    return scaled / (1.0 + jnp.exp(-scaled))


def taps(values):
    count = values.shape[0]
    col = lax.broadcasted_iota(jnp.int32, values.shape, 0) % COLS
    left = jnp.where(col == 0, 0.0, pltpu.roll(values, 1, 0))
    right = jnp.where(col == COLS - 1, 0.0, pltpu.roll(values, count - 1, 0))
    return left, values, right


def dot_nt(a, w):
    return lax.dot_general(a, w, (((1,), (1,)), ((), ())), preferred_element_type=F32)


def dot_nn(a, w):
    return jnp.dot(a, w, preferred_element_type=F32)


def act_kernel(x_ref, g_ref, fa_ref, a_ref, b_ref):
    odd = lax.axis_index("rows") % 2
    gain = g_ref[...]
    for row in range(2):
        for t in range(4):
            values = act(x_ref[t, row].astype(F32), gain)
            left, mid, right = taps(values)
            mid = mid.astype(BF16)
            fa_ref[row, t, :, 0:384] = left.astype(BF16)
            fa_ref[row, t, :, 384:768] = mid
            fa_ref[row, t, :, 768:1152] = right.astype(BF16)

            @pl.when(odd == row)
            def _():
                b_ref[t] = mid

            @pl.when(odd != row)
            def _():
                a_ref[t] = mid


def first_own_kernel(fa_ref, w_ref, acc_ref):
    acc_ref[...] = jnp.zeros_like(acc_ref)
    for i in range(3):
        for j in (1, 0, 2):
            w = jnp.concatenate([w_ref[i, j, k] for k in range(3)], axis=-1)
            if j == 1:
                out = dot_nt(fa_ref[...].reshape(512, 1152), w).reshape(2, 4, COLS, 192)
                acc_ref[:, 2 - i : 6 - i] += out
            else:
                source = 0 if j == 0 else 1
                out = dot_nt(fa_ref[source].reshape(256, 1152), w).reshape(4, COLS, 192)
                acc_ref[1 - source, 2 - i : 6 - i] += out


def rims(ra_ref, rb_ref):
    rows = lax.axis_index("rows")
    odd = rows % 2 == 1
    count = lax.axis_size("rows")
    a = ra_ref[...].astype(F32)
    edge = jnp.logical_or(rows == 0, rows == count - 1)
    b = jnp.where(edge, 0.0, rb_ref[...].astype(F32))
    return jnp.where(odd, a, b), jnp.where(odd, b, a)


def first_rim_kernel(own_ref, ra_ref, rb_ref, w_ref, bias_ref, gain_ref, p_ref, s_ref, t_ref, acc_ref):
    acc_ref[...] = own_ref[...]
    for row, rim in enumerate(rims(ra_ref, rb_ref)):
        stacked = jnp.concatenate([v.astype(BF16) for v in taps(rim.reshape(256, 384))], axis=-1)
        for i in range(3):
            w = jnp.concatenate([w_ref[i, 2 * row, k] for k in range(3)], axis=-1)
            acc_ref[row, 2 - i : 6 - i] += dot_nt(stacked, w).reshape(4, COLS, 192)
    p_ref[...] = acc_ref[:, 0:2]
    hidden = (acc_ref[:, 2:4] + bias_ref[...]).astype(BF16).astype(F32)
    second = act(hidden, gain_ref[...])
    s_ref[...] = second.astype(BF16)
    t_ref[...] = jnp.concatenate([acc_ref[:, 4:6], second], axis=-1).astype(BF16)


def second_act_kernel(p_ref, t_ref, s_ref, bias_ref, gain_ref, sa_ref, a_ref, b_ref):
    first = lax.axis_index("tm") == 0
    odd = lax.axis_index("rows") % 2
    came = jnp.where(first, 0.0, t_ref[...].astype(F32))
    hidden = (p_ref[...] + came[..., :192] + bias_ref[...]).astype(BF16).astype(F32)
    second = act(hidden, gain_ref[...])
    for row in range(2):
        frames = jnp.concatenate([came[row, :, :, 192:], second[row], s_ref[row].astype(F32)], axis=0)
        left, mid, right = taps(frames.reshape(384, 192))
        stacked = jnp.concatenate([left, mid, right], axis=-1).astype(BF16)
        sa_ref[row] = stacked.reshape(6, COLS, 576)
        packed = jnp.concatenate([frames[0:3], frames[3:6]], axis=-1).astype(BF16)

        @pl.when(odd == row)
        def _():
            b_ref[...] = packed

        @pl.when(odd != row)
        def _():
            a_ref[...] = packed


def second_own_kernel(sa_ref, w_ref, x_ref, sw_ref, bias_ref, sbias_ref, acc_ref):
    bias = bias_ref[...] + sbias_ref[...]
    for row in range(2):
        acc_ref[row] = dot_nt(x_ref[:, row].reshape(256, 384), sw_ref[...]).reshape(4, COLS, 192) + bias
    for i in range(3):
        for j in (1, 0, 2):
            w = w_ref[i, j].reshape(576, 192)
            if j == 1:
                out = dot_nn(sa_ref[:, i : i + 4].reshape(512, 576), w).reshape(2, 4, COLS, 192)
                acc_ref[...] += out
            else:
                source = 0 if j == 0 else 1
                out = dot_nn(sa_ref[source, i : i + 4].reshape(256, 576), w)
                acc_ref[1 - source] += out.reshape(4, COLS, 192)


def second_rim_kernel(acc_ref, ra_ref, rb_ref, w_ref, out_ref):
    for row, rim in enumerate(rims(ra_ref, rb_ref)):
        frames = jnp.concatenate([rim[..., :192], rim[..., 192:]], axis=0)
        left, mid, right = taps(frames.reshape(384, 192))
        stacked = jnp.concatenate([left, mid, right], axis=-1).astype(BF16).reshape(6, COLS, 576)
        total = acc_ref[row]
        for i in range(3):
            w = w_ref[i, 2 * row].reshape(576, 192)
            total += dot_nn(stacked[i : i + 4].reshape(256, 576), w).reshape(4, COLS, 192)
        out_ref[:, row] = total.astype(BF16)


def swap_pairs(count):
    inner = [(i, i ^ 1) for i in range(count)]
    outer = [(0, 0), (count - 1, count - 1)]
    for i in range(1, count - 1, 2):
        outer += [(i, i + 1), (i + 1, i)]
    return inner, outer


def shape(dims, dtype):
    return jax.ShapeDtypeStruct(dims, dtype)


def per_device(x, w1, b1, g1, w2, b2, g2, sw, sb):
    inner, outer = swap_pairs(lax.axis_size("rows"))
    steps = lax.axis_size("tm")
    ring = [(i, (i + 1) % steps) for i in range(steps)]
    w1 = jnp.swapaxes(w1, 3, 4)
    sw = jnp.swapaxes(sw, 0, 1)
    b1, g1, b2, g2, sb = (v.reshape(1, -1) for v in (b1, g1, b2, g2, sb))

    fa, send_a, send_b = call(
        act_kernel,
        [shape((2, 4, COLS, 1152), BF16), shape((4, COLS, 384), BF16), shape((4, COLS, 384), BF16)],
        x, g1,
    )
    rim_b = lax.ppermute(send_b, "rows", outer)
    rim_a = lax.ppermute(send_a, "rows", inner)
    acc = call(first_own_kernel, [shape((2, 6, COLS, 192), F32)], fa, w1, flops=10**9)[0]
    p01, s23, send_t = call(
        first_rim_kernel,
        [shape((2, 2, COLS, 192), F32), shape((2, 2, COLS, 192), BF16), shape((2, 2, COLS, 384), BF16)],
        acc, rim_a, rim_b, w1, b1, g2, flops=10**9, scratch=[pltpu.VMEM((2, 6, COLS, 192), F32)],
    )
    came = lax.ppermute(send_t, "tm", ring)
    sa, send_a, send_b = call(
        second_act_kernel,
        [shape((2, 6, COLS, 576), BF16), shape((3, COLS, 384), BF16), shape((3, COLS, 384), BF16)],
        p01, came, s23, b1, g2,
    )
    rim_b = lax.ppermute(send_b, "rows", outer)
    rim_a = lax.ppermute(send_a, "rows", inner)
    acc = call(second_own_kernel, [shape((2, 4, COLS, 192), F32)], sa, w2, x, sw, b2, sb, flops=10**9)[0]
    return call(second_rim_kernel, [shape((4, 2, COLS, 192), BF16)], acc, rim_a, rim_b, w2, flops=10**9)[0]


def solution(mesh):
    return jax.shard_map(
        per_device,
        mesh=mesh,
        in_specs=(P("tm", "rows", None, None), P(), P(), P(), P(), P(), P(), P(), P()),
        out_specs=P("tm", "rows", None, None),
        check_vma=False,
    )
```

time: 71.1 us -> 36.1 us (0.51)
  matrix products: 10.2 us -> 0 us
  waiting for transfers between devices: 26.4 us -> 16.2 us
  Pallas kernels: 0 us -> 8.86 us
  local copies, waits for them, and re-layouts: 11.8 us -> 3.84 us
  starting transfers between devices: 14.2 us -> 6.52 us
  other arithmetic: 6.7 us -> 0 us
    dot_general x19 -> x0, matrix products: 10.2 us -> none  [the longest x18 9.22 us: convolve(): jnp.dot(stacked.reshape(-1, 3 * channels), weight[time_tap, row_tap].resh...]
    ppermute x6 -> x5, waiting for transfers between devices: 26.4 us -> 16.2 us  [the longest x1 9.2 us: per_device(): came = lax.ppermute(send_t, 'tm', ring)]
    slice x19 -> x0, local copies, waits for them, and re-layouts: 9.13 us -> none  [the longest x11 6.14 us: convolve(): weight[time_tap, row_tap].reshape(3 * channels, outputs)]
    pallas_call x0 -> x6, Pallas kernels: none -> 8.86 us  [call(): pl.pallas_call(body, out_shape=outs, in_specs=[VMEM] * len(args), out_spe...]
    ppermute x6 -> x5, starting transfers between devices: 14.2 us -> 6.52 us  [the longest x2 4.66 us: per_device(): rim_b = lax.ppermute(send_b, 'rows', outer)]
    concatenate x15 -> x0, other arithmetic: 3.98 us -> none  [the longest x11 3.53 us: convolve(): jnp.concatenate([widened[time_tap:time_tap + frames, row_tap:row_tap + he...]
    unnamed x23 -> x20, local copies, waits for them, and re-layouts: 1.04 us -> 3.16 us
    add x2 -> x0, local copies, waits for them, and re-layouts: 1.54 us -> none  [convolve(): summed + jnp.dot(stacked.reshape(-1, 3 * channels), weight[time_tap, row_...]
  transfers between devices with their start and end apart: 6 -> 5, of which waited for: 6 -> 3; matrix products, arithmetic and copies ran while one was open for 10% -> 0% of each run, Pallas kernels for 0% -> 11%
where the time goes in v1:
time: 36.1 us; the launch traced here: 35.6 us
  waiting for transfers between devices  16.2 us (45%)
  Pallas kernels  8.86 us (25%)
  starting transfers between devices  6.52 us (18%)
  local copies, waits for them, and re-layouts  3.84 us (11%)
    ppermute x1, waiting for transfers between devices, per_device(): came = lax.ppermute(send_t, 'tm', ring)  9.2 us
    pallas_call x6, Pallas kernels, call(): pl.pallas_call(body, out_shape=outs, in_specs=[VMEM] * len(args), out_spe...  8.86 us
    ppermute x2, waiting for transfers between devices, per_device(): rim_b = lax.ppermute(send_b, 'rows', outer)  7.04 us
    ppermute x2, starting transfers between devices, per_device(): rim_b = lax.ppermute(send_b, 'rows', outer)  4.66 us
    unnamed x20, local copies, waits for them, and re-layouts  3.16 us
    ppermute x1, starting transfers between devices, per_device(): came = lax.ppermute(send_t, 'tm', ring)  1.67 us
  transfers between devices with their start and end apart: 5, of which 3 were waited for; matrix products, arithmetic and copies ran while one was open for 0% of the time, Pallas kernels for 11%

profile of v1, /device:TPU:132, one launch (start us, length us, event | category | flops | bytes accessed | tf_op | source)
XLA Modules:
  0.0 35.6 jit_solution(4038741345505217551)
XLA Ops:
  0.0 0.7 %reshape.15.g_ref = f32[1,384]{1,0:T(1,128)S(1)} reshape(f32[384]{0:T(512)} %param.12) | data formatting | bytes 3072 | tf_op jit(solution)/shard_map/reshape | solution.py:176
  0.7 0.0 copy-start.3
  0.7 1.0 %copy-done.3 = bf16[4,2,64,384]{3,2,1,0:T(8,128)(2,1)S(1)} copy-done((bf16[4,2,64,384]{3,2,1,0:T(8,128)(2,1)S(1)}, bf16[4,2,64,384]{3,2,1,0:T(8,128)(2,1)}, u32[]{:S(2)}) %copy-start.3) | copy-done | bytes 393240
  1.7 1.2 %shard_map.91 = (bf16[2,4,64,1152]{3,2,1,0:T(8,128)(2,1)S(1)}, bf16[4,64,384]{2,1,0:T(8,128)(2,1)S(1)}, bf16[4,64,384]{2,1,0:T(8,128)(2,1)S(1)}) custom-call(bf16[4,2,64,384]{3,2,1,0:T(8,128)(2,1)S(1)} %copy-done.3, f32[1,384]{1,0:T(1,128)S(1)} %reshape.15.g_ref), custom_call_target="tpu_custom_call" | custom-call | bytes 1967616 | tf_op jit(solution)/shard_map/pallas_call | solution.py:16
  2.9 0.1 collective-permute-start
  3.0 2.7 %collective-permute-start.1 = (bf16[4,64,384]{2,1,0:T(8,128)(2,1)S(1)}, bf16[4,64,384]{2,1,0:T(8,128)(2,1)S(1)}, u32[]{:S(2)}, u32[]{:S(2)}) collective-permute-start(bf16[4,64,384]{2,1,0:T(8,128)(2,1)S(1)} %get-tuple-element.16), channel_id=1, source_target_pairs={{0,0},{31,31},{1,2},{2,1},{3,4},{4,3},{5,6},{6,5},{7,8},{8,7},{9,1... | collective-permute-start | bytes 589832 | tf_op jit(solution)/shard_map/ppermute | solution.py:183
  5.7 0.0 copy-start
  5.7 2.1 %copy-done = bf16[3,3,3,384,192]{3,4,2,1,0:T(8,128)(2,1)S(1)} copy-done((bf16[3,3,3,384,192]{3,4,2,1,0:T(8,128)(2,1)S(1)}, bf16[3,3,3,384,192]{3,4,2,1,0:T(8,128)(2,1)}, u32[]{:S(2)}) %copy-start) | copy-done | bytes 3981336
  7.8 0.0 copy-start.1
  7.8 0.0 copy-start.6
  7.8 0.0 copy-start.7
  7.9 2.3 %shard_map.92.own_ref = f32[2,6,64,192]{3,2,1,0:T(8,128)S(1)} custom-call(bf16[2,4,64,1152]{3,2,1,0:T(8,128)(2,1)S(1)} %get-tuple-element.14.fa_ref, bf16[3,3,3,192,384]{4,3,2,1,0:T(8,128)(2,1)S(1)} %bitcast.6), custom_call_target="tpu_custom_call" | custom-call | flops 1000000000 | bytes 5750784 | tf_op jit(solution)/shard_map/pallas_call | solution.py:16
  10.1 0.0 collective-permute-done.ra_ref
  10.2 2.0 %collective-permute-done.1.rb_ref = bf16[4,64,384]{2,1,0:T(8,128)(2,1)S(1)} collective-permute-done((bf16[4,64,384]{2,1,0:T(8,128)(2,1)S(1)}, bf16[4,64,384]{2,1,0:T(8,128)(2,1)S(1)}, u32[]{:S(2)}, u32[]{:S(2)}) %collective-permute-start.1) | collective-permute-done | bytes 196640 | tf_op jit(solution)/shard_map/ppermute | solution.py:183
  12.2 0.0 copy-done.1
  12.2 0.0 copy-done.6
  12.2 0.0 copy-done.7
  12.2 0.0 copy-start.2
  12.2 0.0 copy-start.4
  12.2 0.0 copy-start.5
  12.2 0.0 copy-start.8
  12.2 0.0 copy-start.9
  12.2 1.5 %shard_map.93 = (f32[2,2,64,192]{3,2,1,0:T(8,128)S(1)}, bf16[2,2,64,192]{3,2,1,0:T(8,128)(2,1)S(1)}, bf16[2,2,64,384]{3,2,1,0:T(8,128)(2,1)S(1)}) custom-call(f32[2,6,64,192]{3,2,1,0:T(8,128)S(1)} %shard_map.92.own_ref, bf16[4,64,384]{2,1,0:T(8,128)(2,1)S(1)} %collective-permute-done.ra_ref, bf16[4,64,384]{2,1,0:T(8,128)(2,1)S(1)} %collective-permute-done.1.rb_ref, ...), custom_call_target="tpu_custom_call" | custom-call | flops 1000000000 | bytes 5457408 | tf_op jit(solution)/shard_map/pallas_call | solution.py:16
  13.7 1.7 %collective-permute-start.2 = (bf16[2,2,64,384]{3,2,1,0:T(8,128)(2,1)S(1)}, bf16[2,2,64,384]{3,2,1,0:T(8,128)(2,1)S(1)}, u32[]{:S(2)}, u32[]{:S(2)}) collective-permute-start(bf16[2,2,64,384]{3,2,1,0:T(8,128)(2,1)S(1)} %get-tuple-element.18), channel_id=1, source_target_pairs={{0,32},{32,64},{64,96},{96,128},{128,160},{160,192},{192,224},{224... | collective-permute-start | bytes 589832 | tf_op jit(solution)/shard_map/ppermute | solution.py:191
  15.4 9.2 %collective-permute-done.2.t_ref = bf16[2,2,64,384]{3,2,1,0:T(8,128)(2,1)S(1)} collective-permute-done((bf16[2,2,64,384]{3,2,1,0:T(8,128)(2,1)S(1)}, bf16[2,2,64,384]{3,2,1,0:T(8,128)(2,1)S(1)}, u32[]{:S(2)}, u32[]{:S(2)}) %collective-permute-start.2) | collective-permute-done | bytes 196640 | tf_op jit(solution)/shard_map/ppermute | solution.py:191
  24.6 0.6 %shard_map.94 = (bf16[2,6,64,576]{3,2,1,0:T(8,128)(2,1)S(1)}, bf16[3,64,384]{2,1,0:T(8,128)(2,1)S(1)}, bf16[3,64,384]{2,1,0:T(8,128)(2,1)S(1)}) custom-call(f32[2,2,64,192]{3,2,1,0:T(8,128)S(1)} %get-tuple-element.17.p_ref, bf16[2,2,64,384]{3,2,1,0:T(8,128)(2,1)S(1)} %collective-permute-done.2.t_ref, bf16[2,2,64,192]{3,2,1,0:T(8,128)(2,1)S(1)} %get-tuple-element.19.s_ref, ...), custom_call_target="tpu_custom_call" | custom-call | bytes 1672704 | tf_op jit(solution)/shard_map/pallas_call | solution.py:16
  25.2 0.1 collective-permute-start.3
  25.3 1.9 %collective-permute-start.4 = (bf16[3,64,384]{2,1,0:T(8,128)(2,1)S(1)}, bf16[3,64,384]{2,1,0:T(8,128)(2,1)S(1)}, u32[]{:S(2)}, u32[]{:S(2)}) collective-permute-start(bf16[3,64,384]{2,1,0:T(8,128)(2,1)S(1)} %get-tuple-element.22), channel_id=1, source_target_pairs={{0,0},{31,31},{1,2},{2,1},{3,4},{4,3},{5,6},{6,5},{7,8},{8,7},{9,1... | collective-permute-start | bytes 442376 | tf_op jit(solution)/shard_map/ppermute | solution.py:197
  27.2 0.0 copy-done.2
  27.2 0.0 copy-done.4
  27.3 0.0 copy-done.5
  27.3 0.0 copy-done.8
  27.3 0.0 copy-done.9
  27.3 1.7 %shard_map.95.acc_ref = f32[2,4,64,192]{3,2,1,0:T(8,128)S(1)} custom-call(bf16[2,6,64,576]{3,2,1,0:T(8,128)(2,1)S(1)} %get-tuple-element.20.sa_ref, bf16[3,3,3,192,192]{4,3,2,1,0:T(8,128)(2,1)S(1)} %copy-done.2, bf16[4,2,64,384]{3,2,1,0:T(8,128)(2,1)S(1)} %copy-done.4, bf16[192,384]{1,0:T(8,128)(2,1)S(1)} %bitcast.8, f32[1,192]{1,0:T(1,128)S(1)} %bitcast.13, ...), custom_call_target="tpu_custom_call" | custom-call | flops 1000000000 | bytes 3810816 | tf_op jit(solution)/shard_map/pallas_call | solution.py:16
  28.9 0.0 collective-permute-done.3.ra_ref
  29.0 5.0 %collective-permute-done.4.rb_ref = bf16[3,64,384]{2,1,0:T(8,128)(2,1)S(1)} collective-permute-done((bf16[3,64,384]{2,1,0:T(8,128)(2,1)S(1)}, bf16[3,64,384]{2,1,0:T(8,128)(2,1)S(1)}, u32[]{:S(2)}, u32[]{:S(2)}) %collective-permute-start.4) | collective-permute-done | bytes 147488 | tf_op jit(solution)/shard_map/ppermute | solution.py:197
  34.0 1.7 %shard_map.96 = bf16[4,2,64,192]{3,2,1,0:T(8,128)(2,1)} custom-call(f32[2,4,64,192]{3,2,1,0:T(8,128)S(1)} %shard_map.95.acc_ref, bf16[3,64,384]{2,1,0:T(8,128)(2,1)S(1)} %collective-permute-done.3.ra_ref, bf16[3,64,384]{2,1,0:T(8,128)(2,1)S(1)} %collective-permute-done.4.rb_ref, bf16[3,3,3,192,192]{4,3,2,1,0:T(8,128)(2,1)S(1)} %copy-done.2), custom_call_target="tpu_custom_call" | custom-call | flops 1000000000 | bytes 2875392 | tf_op jit(solution)/shard_map/pallas_call | solution.py:16
Async XLA Ops:
  0.7 1.0 %copy-start.3 = (bf16[4,2,64,384]{3,2,1,0:T(8,128)(2,1)S(1)}, bf16[4,2,64,384]{3,2,1,0:T(8,128)(2,1)}, u32[]{:S(2)}) copy-start(bf16[4,2,64,384]{3,2,1,0:T(8,128)(2,1)} %x_ref.3) | copy-start | bytes 1179652
  2.9 7.3 %collective-permute-start = (bf16[4,64,384]{2,1,0:T(8,128)(2,1)S(1)}, bf16[4,64,384]{2,1,0:T(8,128)(2,1)S(1)}, u32[]{:S(2)}, u32[]{:S(2)}) collective-permute-start(bf16[4,64,384]{2,1,0:T(8,128)(2,1)S(1)} %get-tuple-element.15), channel_id=1, source_target_pairs={{0,1},{1,0},{2,3},{3,2},{4,5},{5,4},{6,7},{7,6},{8,9},{9,8},{10,11... | collective-permute-start | bytes 589832 | tf_op jit(solution)/shard_map/ppermute | solution.py:184
  3.0 9.2 %collective-permute-start.1 = (bf16[4,64,384]{2,1,0:T(8,128)(2,1)S(1)}, bf16[4,64,384]{2,1,0:T(8,128)(2,1)S(1)}, u32[]{:S(2)}, u32[]{:S(2)}) collective-permute-start(bf16[4,64,384]{2,1,0:T(8,128)(2,1)S(1)} %get-tuple-element.16), channel_id=1, source_target_pairs={{0,0},{31,31},{1,2},{2,1},{3,4},{4,3},{5,6},{6,5},{7,8},{8,7},{9,1... | collective-permute-start | bytes 589832 | tf_op jit(solution)/shard_map/ppermute | solution.py:183
  5.7 2.1 %copy-start = (bf16[3,3,3,384,192]{3,4,2,1,0:T(8,128)(2,1)S(1)}, bf16[3,3,3,384,192]{3,4,2,1,0:T(8,128)(2,1)}, u32[]{:S(2)}) copy-start(bf16[3,3,3,384,192]{3,4,2,1,0:T(8,128)(2,1)} %param.10) | copy-start | bytes 11943940
  7.8 4.3 %copy-start.1 = (bf16[3,3,3,384,192]{3,4,2,1,0:T(8,128)(2,1)S(1)}, bf16[3,3,3,384,192]{3,4,2,1,0:T(8,128)(2,1)}, u32[]{:S(2)}) copy-start(bf16[3,3,3,384,192]{3,4,2,1,0:T(8,128)(2,1)} %param.10) | copy-start | bytes 11943940
  7.8 4.3 %copy-start.6 = (f32[192]{0:T(256)S(1)}, f32[192]{0:T(256)}, u32[]{:S(2)}) copy-start(f32[192]{0:T(256)} %param.11) | copy-start | bytes 2308
  7.8 4.3 %copy-start.7 = (f32[192]{0:T(256)S(1)}, f32[192]{0:T(256)}, u32[]{:S(2)}) copy-start(f32[192]{0:T(256)} %param.15) | copy-start | bytes 2308
  12.2 15.1 %copy-start.2 = (bf16[3,3,3,192,192]{4,3,2,1,0:T(8,128)(2,1)S(1)}, bf16[3,3,3,192,192]{4,3,2,1,0:T(8,128)(2,1)}, u32[]{:S(2)}) copy-start(bf16[3,3,3,192,192]{4,3,2,1,0:T(8,128)(2,1)} %w_ref.3) | copy-start | bytes 5971972
  12.2 15.0 %copy-start.4 = (bf16[4,2,64,384]{3,2,1,0:T(8,128)(2,1)S(1)}, bf16[4,2,64,384]{3,2,1,0:T(8,128)(2,1)}, u32[]{:S(2)}) copy-start(bf16[4,2,64,384]{3,2,1,0:T(8,128)(2,1)} %x_ref.3) | copy-start | bytes 1179652
  12.2 15.0 %copy-start.5 = (bf16[384,192]{0,1:T(8,128)(2,1)S(1)}, bf16[384,192]{0,1:T(8,128)(2,1)}, u32[]{:S(2)}) copy-start(bf16[384,192]{0,1:T(8,128)(2,1)} %param.16) | copy-start | bytes 442372
  12.2 15.0 %copy-start.8 = (f32[192]{0:T(256)S(1)}, f32[192]{0:T(256)}, u32[]{:S(2)}) copy-start(f32[192]{0:T(256)} %param.14) | copy-start | bytes 2308
  12.2 15.0 %copy-start.9 = (f32[192]{0:T(256)S(1)}, f32[192]{0:T(256)}, u32[]{:S(2)}) copy-start(f32[192]{0:T(256)} %param.17) | copy-start | bytes 2308
  13.7 10.9 %collective-permute-start.2 = (bf16[2,2,64,384]{3,2,1,0:T(8,128)(2,1)S(1)}, bf16[2,2,64,384]{3,2,1,0:T(8,128)(2,1)S(1)}, u32[]{:S(2)}, u32[]{:S(2)}) collective-permute-start(bf16[2,2,64,384]{3,2,1,0:T(8,128)(2,1)S(1)} %get-tuple-element.18), channel_id=1, source_target_pairs={{0,32},{32,64},{64,96},{96,128},{128,160},{160,192},{192,224},{224... | collective-permute-start | bytes 589832 | tf_op jit(solution)/shard_map/ppermute | solution.py:191
  25.2 3.8 %collective-permute-start.3 = (bf16[3,64,384]{2,1,0:T(8,128)(2,1)S(1)}, bf16[3,64,384]{2,1,0:T(8,128)(2,1)S(1)}, u32[]{:S(2)}, u32[]{:S(2)}) collective-permute-start(bf16[3,64,384]{2,1,0:T(8,128)(2,1)S(1)} %get-tuple-element.21), channel_id=1, source_target_pairs={{0,1},{1,0},{2,3},{3,2},{4,5},{5,4},{6,7},{7,6},{8,9},{9,8},{10,11... | collective-permute-start | bytes 442376 | tf_op jit(solution)/shard_map/ppermute | solution.py:198
  25.3 8.7 %collective-permute-start.4 = (bf16[3,64,384]{2,1,0:T(8,128)(2,1)S(1)}, bf16[3,64,384]{2,1,0:T(8,128)(2,1)S(1)}, u32[]{:S(2)}, u32[]{:S(2)}) collective-permute-start(bf16[3,64,384]{2,1,0:T(8,128)(2,1)S(1)} %get-tuple-element.22), channel_id=1, source_target_pairs={{0,0},{31,31},{1,2},{2,1},{3,4},{4,3},{5,6},{6,5},{7,8},{8,7},{9,1... | collective-permute-start | bytes 442376 | tf_op jit(solution)/shard_map/ppermute | solution.py:197

commit v2 on v1

v2 whole, which is shorter than its diff:
```python
import jax
import jax.numpy as jnp
from jax import lax
from jax.experimental import pallas as pl
from jax.experimental.pallas import tpu as pltpu
from jax.sharding import PartitionSpec as P

F32 = jnp.float32
BF16 = jnp.bfloat16
COLS = 64
VMEM = pl.BlockSpec(memory_space=pltpu.VMEM)
HBM = pl.BlockSpec(memory_space=pltpu.HBM)


def call(body, outs, *args, flops=0, scratch=(), limit=8, in_hbm=(), out_hbm=()):
    args = [pltpu.with_memory_space_constraint(a, pltpu.HBM) if n in in_hbm else a for n, a in enumerate(args)]
    moved = sum(a.size * a.dtype.itemsize for a in args) + sum(o.size * o.dtype.itemsize for o in outs)
    return pl.pallas_call(
        body,
        out_shape=outs,
        in_specs=[HBM if n in in_hbm else VMEM for n in range(len(args))],
        out_specs=[HBM if n in out_hbm else VMEM for n in range(len(outs))],
        scratch_shapes=list(scratch),
        compiler_params=pltpu.CompilerParams(vmem_limit_bytes=limit << 20),
        cost_estimate=pl.CostEstimate(flops=flops, bytes_accessed=moved, transcendentals=0),
    )(*args)


def shape(dims, dtype=BF16):
    return jax.ShapeDtypeStruct(dims, dtype)


def act(values, gain):
    mean = jnp.mean(values * values, axis=-1, keepdims=True)
    scaled = values * lax.rsqrt(mean + 1e-06) * gain
    return scaled / (1.0 + jnp.exp(-scaled))


def taps(values):
    count = values.shape[0]
    col = lax.broadcasted_iota(jnp.int32, values.shape, 0) % COLS
    left = jnp.where(col == 0, 0.0, pltpu.roll(values, 1, 0))
    right = jnp.where(col == COLS - 1, 0.0, pltpu.roll(values, count - 1, 0))
    return left, values, right


def first_dot(a, w_ref, i, j):
    frames = a.shape[0]
    w = jnp.concatenate([w_ref[i, j, k] for k in range(3)], axis=-1)
    out = lax.dot_general(
        a.reshape(frames * COLS, 1152), w, (((1,), (1,)), ((), ())), preferred_element_type=F32
    )
    return out.reshape(frames, COLS, 192)


def second_dot(a, w_ref, i, j):
    frames = a.shape[0]
    out = jnp.dot(a.reshape(frames * COLS, 576), w_ref[i, j].reshape(576, 192), preferred_element_type=F32)
    return out.reshape(frames, COLS, 192)


def store_for_pairs(above, below, a_ref, b_ref):
    odd = lax.axis_index("rows") % 2 == 1
    a_ref[...] = jnp.where(odd, above, below).astype(BF16)
    b_ref[...] = jnp.where(odd, below, above).astype(BF16)


def from_pairs(ra_ref, rb_ref):
    rows = lax.axis_index("rows")
    odd = rows % 2 == 1
    edge = jnp.logical_or(rows == 0, rows == lax.axis_size("rows") - 1)
    a = ra_ref[...].astype(F32)
    b = jnp.where(edge, 0.0, rb_ref[...].astype(F32))
    return jnp.where(odd, a, b), jnp.where(odd, b, a)


def pack(values):
    half = values.shape[0] // 2
    return jnp.concatenate([values[:half], values[half:]], axis=-1)


def unpack(values):
    return jnp.concatenate([values[..., :192], values[..., 192:]], axis=0)


def act_kernel(x_hbm, g_hbm, w_hbm, fa_ref, w_ref, a_ref, b_ref, x_ref, g_ref, acc_ref, gsem, xsem, wsem):
    gain_load = pltpu.make_async_copy(g_hbm, g_ref, gsem)
    gain_load.start()
    loads = [pltpu.make_async_copy(x_hbm.at[t], x_ref.at[t], xsem.at[t]) for t in range(4)]
    weights = [pltpu.make_async_copy(w_hbm.at[:, j], w_ref.at[:, j], wsem.at[j]) for j in range(3)]
    for load in loads:
        load.start()
    for j in (0, 2, 1):
        weights[j].start()
    gain_load.wait()
    gain = g_ref[...].reshape(1, 384)
    for t in range(4):
        loads[t].wait()
        for row in range(2):
            left, mid, right = taps(act(x_ref[t, row].astype(F32), gain))
            fa_ref[row, t, :, 0:384] = left.astype(BF16)
            fa_ref[row, t, :, 384:768] = mid.astype(BF16)
            fa_ref[row, t, :, 768:1152] = right.astype(BF16)
    weights[0].wait()
    weights[2].wait()
    sums = []
    for side, j in ((0, 2), (1, 0)):
        acc_ref[side, 2:6] = first_dot(fa_ref[side], w_ref, 0, j)
        acc_ref[side, 0:2] = jnp.zeros((2, COLS, 192), F32)
        for i in (1, 2):
            acc_ref[side, 2 - i : 6 - i] += first_dot(fa_ref[side], w_ref, i, j)
        sums.append(pack(acc_ref[side]))
    store_for_pairs(sums[0], sums[1], a_ref, b_ref)
    weights[1].wait()


def first_own_kernel(fa_ref, w_ref, acc_ref):
    for i in range(3):
        outs = [first_dot(fa_ref[row], w_ref, i, 1) for row in range(2)]
        outs[1] += first_dot(fa_ref[0], w_ref, i, 0)
        outs[0] += first_dot(fa_ref[1], w_ref, i, 2)
        for row in range(2):
            if i == 0:
                acc_ref[row, 0:2] = jnp.zeros((2, COLS, 192), F32)
                acc_ref[row, 2:6] = outs[row]
            else:
                acc_ref[row, 2 - i : 6 - i] += outs[row]


def first_rim_kernel(own_ref, ra_ref, rb_ref, bias_ref, gain_ref, p_ref, s_ref, t_ref):
    for row, rim in enumerate(from_pairs(ra_ref, rb_ref)):
        total = own_ref[row] + unpack(rim)
        p_ref[row] = total[0:2] + bias_ref[...]
        hidden = (total[2:4] + bias_ref[...]).astype(BF16).astype(F32)
        second = act(hidden, gain_ref[...])
        s_ref[row] = second.astype(BF16)
        t_ref[row] = jnp.concatenate([total[4:6], second], axis=-1).astype(BF16)


def meanwhile_kernel(s_ref, x_ref, w_ref, bias_ref, sbias_ref, sa_ref, acc_ref):
    bias = bias_ref[...] + sbias_ref[...]
    for row in range(2):
        stacked = jnp.concatenate(taps(s_ref[row].astype(F32).reshape(128, 192)), axis=-1)
        sa_ref[row] = stacked.astype(BF16).reshape(2, COLS, 576)
        out = lax.dot_general(
            x_ref[:, row].reshape(256, 384), w_ref[...], (((1,), (1,)), ((), ())), preferred_element_type=F32
        )
        acc_ref[row] = out.reshape(4, COLS, 192) + bias


def second_act_kernel(p_ref, t_ref, last_ref, gain_ref, w_ref, sa_ref, a_ref, b_ref):
    first = lax.axis_index("tm") == 0
    for row in range(2):
        came = jnp.where(first, 0.0, t_ref[row].astype(F32))
        hidden = (p_ref[row] + came[..., :192]).astype(BF16).astype(F32)
        second = act(hidden, gain_ref[...])
        frames = jnp.concatenate([came[..., 192:], second], axis=0)
        stacked = jnp.concatenate(taps(frames.reshape(256, 192)), axis=-1)
        sa_ref[row, 0:4] = stacked.astype(BF16).reshape(4, COLS, 576)
        sa_ref[row, 4:6] = last_ref[row]
    sums = []
    for side, j in ((0, 2), (1, 0)):
        total = second_dot(sa_ref[side, 0:4], w_ref, 0, j)
        total += second_dot(sa_ref[side, 1:5], w_ref, 1, j)
        total += second_dot(sa_ref[side, 2:6], w_ref, 2, j)
        sums.append(pack(total))
    store_for_pairs(sums[0], sums[1], a_ref, b_ref)


def second_own_kernel(sa_ref, w_ref, skip_ref, acc_ref):
    for i in range(3):
        outs = [second_dot(sa_ref[row, i : i + 4], w_ref, i, 1) for row in range(2)]
        outs[1] += second_dot(sa_ref[0, i : i + 4], w_ref, i, 0)
        outs[0] += second_dot(sa_ref[1, i : i + 4], w_ref, i, 2)
        for row in range(2):
            if i == 0:
                acc_ref[row] = skip_ref[row] + outs[row]
            else:
                acc_ref[row] += outs[row]


def second_rim_kernel(acc_ref, ra_ref, rb_ref, out_ref):
    for row, rim in enumerate(from_pairs(ra_ref, rb_ref)):
        out_ref[:, row] = (acc_ref[row] + unpack(rim)).astype(BF16)


def swap_pairs(count):
    inner = [(i, i ^ 1) for i in range(count)]
    outer = [(0, 0), (count - 1, count - 1)]
    for i in range(1, count - 1, 2):
        outer += [(i, i + 1), (i + 1, i)]
    return inner, outer


def per_device(x, w1, b1, g1, w2, b2, g2, sw, sb):
    inner, outer = swap_pairs(lax.axis_size("rows"))
    steps = lax.axis_size("tm")
    ring = [(i, (i + 1) % steps) for i in range(steps)]
    w1 = jnp.swapaxes(w1, 3, 4)
    sw = jnp.swapaxes(sw, 0, 1)
    b1, b2, g2, sb = (v.reshape(1, -1) for v in (b1, b2, g2, sb))

    def swap(a, b):
        return lax.ppermute(a, "rows", inner), lax.ppermute(b, "rows", outer)

    fa, w1, send_a, send_b = call(
        act_kernel,
        [shape((2, 4, COLS, 1152)), shape(w1.shape), shape((3, COLS, 384)), shape((3, COLS, 384))],
        x, g1, w1, flops=10**9, in_hbm=(0, 1, 2),
        scratch=[
            pltpu.VMEM((4, 2, COLS, 384), BF16), pltpu.VMEM((384,), F32), pltpu.VMEM((2, 6, COLS, 192), F32),
            pltpu.SemaphoreType.DMA(()), pltpu.SemaphoreType.DMA((4,)), pltpu.SemaphoreType.DMA((3,)),
        ],
    )
    rims = swap(send_a, send_b)
    own = call(first_own_kernel, [shape((2, 6, COLS, 192), F32)], fa, w1, flops=10**9)[0]
    p01, s23, send_t = call(
        first_rim_kernel,
        [shape((2, 2, COLS, 192), F32), shape((2, 2, COLS, 192)), shape((2, 2, COLS, 384))],
        own, *rims, b1, g2, flops=10**8,
    )
    came = lax.ppermute(send_t, "tm", ring)
    last, skip = call(
        meanwhile_kernel,
        [shape((2, 2, COLS, 576)), shape((2, 4, COLS, 192), F32)],
        s23, x, sw, b2, sb, flops=10**8,
    )
    sa, send_a, send_b = call(
        second_act_kernel,
        [shape((2, 6, COLS, 576)), shape((2, COLS, 384)), shape((2, COLS, 384))],
        p01, came, last, g2, w2, flops=10**9,
    )
    rims = swap(send_a, send_b)
    own = call(second_own_kernel, [shape((2, 4, COLS, 192), F32)], sa, w2, skip, flops=10**9)[0]
    return call(second_rim_kernel, [shape((4, 2, COLS, 192))], own, *rims, flops=10**8)[0]


def solution(mesh):
    return jax.shard_map(
        per_device,
        mesh=mesh,
        in_specs=(P("tm", "rows", None, None), P(), P(), P(), P(), P(), P(), P(), P()),
        out_specs=P("tm", "rows", None, None),
        check_vma=False,
    )
```

time: 36.1 us -> 33.5 us (0.928)
  the two profiles are of different devices: /device:TPU:132 before, /device:TPU:197 now
where the time goes in v2:
time: 33.5 us; the launch traced here: 33.3 us
  waiting for transfers between devices  15.2 us (45%)
  Pallas kernels  10.1 us (30%)
  starting transfers between devices  7.8 us (23%)
    pallas_call x7, Pallas kernels, call(): pl.pallas_call(body, out_shape=outs, in_specs=[HBM if n in in_hbm else VM...  10.1 us
    ppermute x1, waiting for transfers between devices, per_device(): came = lax.ppermute(send_t, 'tm', ring)  8.86 us
    ppermute x4, starting transfers between devices, swap(): return (lax.ppermute(a, 'rows', inner), lax.ppermute(b, 'rows', outer))  6.42 us
    ppermute x4, waiting for transfers between devices, swap(): return (lax.ppermute(a, 'rows', inner), lax.ppermute(b, 'rows', outer))  6.36 us
    ppermute x1, starting transfers between devices, per_device(): came = lax.ppermute(send_t, 'tm', ring)  1.37 us
  transfers between devices with their start and end apart: 5, of which 3 were waited for; matrix products, arithmetic and copies ran while one was open for 0% of the time, Pallas kernels for 12%

profile of v2, /device:TPU:197, one launch (start us, length us, event | category | flops | bytes accessed | tf_op | source)
XLA Modules:
  0.0 33.3 jit_solution(8574537411377294894)
XLA Ops:
  0.0 3.8 %shard_map.91 = (bf16[2,4,64,1152]{3,2,1,0:T(8,128)(2,1)S(1)}, bf16[3,3,3,192,384]{4,3,2,1,0:T(8,128)(2,1)S(1)}, bf16[3,64,384]{2,1,0:T(8,128)(2,1)S(1)}, bf16[3,64,384]{2,1,0:T(8,128)(2,1)S(1)}) custom-call(bf16[4,2,64,384]{3,2,1,0:T(8,128)(2,1)} %x_ref.1, f32[384]{0:T(512)} %g_hbm.1, bf16[3,3,3,192,384]{4,3,2,1,0:T(8,128)(2,1)} %bitcast.12), custom_call_target="tpu_custom_call" | custom-call | flops 1000000000 | bytes 9831936 | tf_op jit(solution)/shard_map/pallas_call | solution.py:18
  3.9 0.0 copy-start.5
  3.9 0.0 copy-start.6
  3.9 0.0 copy-start.1
  3.9 0.0 copy-start.2
  3.9 0.0 copy-start.3
  3.9 0.0 copy-start.4
  3.9 0.0 copy-start
  3.9 0.8 %collective-permute-start = (bf16[3,64,384]{2,1,0:T(8,128)(2,1)S(1)}, bf16[3,64,384]{2,1,0:T(8,128)(2,1)S(1)}, u32[]{:S(2)}, u32[]{:S(2)}) collective-permute-start(bf16[3,64,384]{2,1,0:T(8,128)(2,1)S(1)} %get-tuple-element.19), channel_id=1, source_target_pairs={{0,1},{1,0},{2,3},{3,2},{4,5},{5,4},{6,7},{7,6},{8,9},{9,8},{10,11... | collective-permute-start | bytes 442376 | tf_op jit(solution)/shard_map/ppermute | solution.py:204
  4.7 3.0 %collective-permute-start.1 = (bf16[3,64,384]{2,1,0:T(8,128)(2,1)S(1)}, bf16[3,64,384]{2,1,0:T(8,128)(2,1)S(1)}, u32[]{:S(2)}, u32[]{:S(2)}) collective-permute-start(bf16[3,64,384]{2,1,0:T(8,128)(2,1)S(1)} %get-tuple-element.20), channel_id=1, source_target_pairs={{0,0},{31,31},{1,2},{2,1},{3,4},{4,3},{5,6},{6,5},{7,8},{8,7},{9,1... | collective-permute-start | bytes 442376 | tf_op jit(solution)/shard_map/ppermute | solution.py:204
  7.7 2.2 %shard_map.92.own_ref = f32[2,6,64,192]{3,2,1,0:T(8,128)S(1)} custom-call(bf16[2,4,64,1152]{3,2,1,0:T(8,128)(2,1)S(1)} %get-tuple-element.17.fa_ref, bf16[3,3,3,192,384]{4,3,2,1,0:T(8,128)(2,1)S(1)} %get-tuple-element.18.w_ref), custom_call_target="tpu_custom_call" | custom-call | flops 1000000000 | bytes 5750784 | tf_op jit(solution)/shard_map/pallas_call | solution.py:18
  9.9 0.0 collective-permute-done.ra_ref
  9.9 2.9 %collective-permute-done.1.rb_ref = bf16[3,64,384]{2,1,0:T(8,128)(2,1)S(1)} collective-permute-done((bf16[3,64,384]{2,1,0:T(8,128)(2,1)S(1)}, bf16[3,64,384]{2,1,0:T(8,128)(2,1)S(1)}, u32[]{:S(2)}, u32[]{:S(2)}) %collective-permute-start.1) | collective-permute-done | bytes 147488 | tf_op jit(solution)/shard_map/ppermute | solution.py:204
  12.9 0.0 copy-done.5
  12.9 0.0 copy-done.6
  12.9 0.4 %shard_map.93 = (f32[2,2,64,192]{3,2,1,0:T(8,128)S(1)}, bf16[2,2,64,192]{3,2,1,0:T(8,128)(2,1)S(1)}, bf16[2,2,64,384]{3,2,1,0:T(8,128)(2,1)S(1)}) custom-call(f32[2,6,64,192]{3,2,1,0:T(8,128)S(1)} %shard_map.92.own_ref, bf16[3,64,384]{2,1,0:T(8,128)(2,1)S(1)} %collective-permute-done.ra_ref, bf16[3,64,384]{2,1,0:T(8,128)(2,1)S(1)} %collective-permute-done.1.rb_ref, ...), custom_call_target="tpu_custom_call" | custom-call | flops 100000000 | bytes 1377792 | tf_op jit(solution)/shard_map/pallas_call | solution.py:18
  13.2 1.4 %collective-permute-start.2 = (bf16[2,2,64,384]{3,2,1,0:T(8,128)(2,1)S(1)}, bf16[2,2,64,384]{3,2,1,0:T(8,128)(2,1)S(1)}, u32[]{:S(2)}, u32[]{:S(2)}) collective-permute-start(bf16[2,2,64,384]{3,2,1,0:T(8,128)(2,1)S(1)} %get-tuple-element.22), channel_id=1, source_target_pairs={{0,32},{32,64},{64,96},{96,128},{128,160},{160,192},{192,224},{224... | collective-permute-start | bytes 589832 | tf_op jit(solution)/shard_map/ppermute | solution.py:222
  14.6 0.0 copy-done.1
  14.6 0.0 copy-done.2
  14.6 0.0 copy-done.3
  14.6 0.0 copy-done.4
  14.6 0.3 shard_map.94
  14.9 8.9 %collective-permute-done.2.t_ref = bf16[2,2,64,384]{3,2,1,0:T(8,128)(2,1)S(1)} collective-permute-done((bf16[2,2,64,384]{3,2,1,0:T(8,128)(2,1)S(1)}, bf16[2,2,64,384]{3,2,1,0:T(8,128)(2,1)S(1)}, u32[]{:S(2)}, u32[]{:S(2)}) %collective-permute-start.2) | collective-permute-done | bytes 196640 | tf_op jit(solution)/shard_map/ppermute | solution.py:222
  23.8 0.0 copy-done
  23.8 1.2 %shard_map.95 = (bf16[2,6,64,576]{3,2,1,0:T(8,128)(2,1)S(1)}, bf16[2,64,384]{2,1,0:T(8,128)(2,1)S(1)}, bf16[2,64,384]{2,1,0:T(8,128)(2,1)S(1)}) custom-call(f32[2,2,64,192]{3,2,1,0:T(8,128)S(1)} %get-tuple-element.21.p_ref, bf16[2,2,64,384]{3,2,1,0:T(8,128)(2,1)S(1)} %collective-permute-done.2.t_ref, bf16[2,2,64,576]{3,2,1,0:T(8,128)(2,1)S(1)} %get-tuple-element.24.last_ref, ...), custom_call_target="tpu_custom_call" | custom-call | flops 1000000000 | bytes 3760896 | tf_op jit(solution)/shard_map/pallas_call | solution.py:18
  25.0 0.5 %collective-permute-start.3 = (bf16[2,64,384]{2,1,0:T(8,128)(2,1)S(1)}, bf16[2,64,384]{2,1,0:T(8,128)(2,1)S(1)}, u32[]{:S(2)}, u32[]{:S(2)}) collective-permute-start(bf16[2,64,384]{2,1,0:T(8,128)(2,1)S(1)} %get-tuple-element.27), channel_id=1, source_target_pairs={{0,1},{1,0},{2,3},{3,2},{4,5},{5,4},{6,7},{7,6},{8,9},{9,8},{10,11... | collective-permute-start | bytes 294920 | tf_op jit(solution)/shard_map/ppermute | solution.py:204
  25.5 2.1 %collective-permute-start.4 = (bf16[2,64,384]{2,1,0:T(8,128)(2,1)S(1)}, bf16[2,64,384]{2,1,0:T(8,128)(2,1)S(1)}, u32[]{:S(2)}, u32[]{:S(2)}) collective-permute-start(bf16[2,64,384]{2,1,0:T(8,128)(2,1)S(1)} %get-tuple-element.28), channel_id=1, source_target_pairs={{0,0},{31,31},{1,2},{2,1},{3,4},{4,3},{5,6},{6,5},{7,8},{8,7},{9,1... | collective-permute-start | bytes 294920 | tf_op jit(solution)/shard_map/ppermute | solution.py:204
  27.7 1.4 %shard_map.96.acc_ref = f32[2,4,64,192]{3,2,1,0:T(8,128)S(1)} custom-call(bf16[2,6,64,576]{3,2,1,0:T(8,128)(2,1)S(1)} %get-tuple-element.25.sa_ref, bf16[3,3,3,192,192]{4,3,2,1,0:T(8,128)(2,1)S(1)} %copy-done, f32[2,4,64,192]{3,2,1,0:T(8,128)S(1)} %get-tuple-element.26.skip_ref), custom_call_target="tpu_custom_call" | custom-call | flops 1000000000 | bytes 3661824 | tf_op jit(solution)/shard_map/pallas_call | solution.py:18
  29.1 0.0 collective-permute-done.3.ra_ref
  29.1 3.4 %collective-permute-done.4.rb_ref = bf16[2,64,384]{2,1,0:T(8,128)(2,1)S(1)} collective-permute-done((bf16[2,64,384]{2,1,0:T(8,128)(2,1)S(1)}, bf16[2,64,384]{2,1,0:T(8,128)(2,1)S(1)}, u32[]{:S(2)}, u32[]{:S(2)}) %collective-permute-start.4) | collective-permute-done | bytes 98336 | tf_op jit(solution)/shard_map/ppermute | solution.py:204
  32.5 0.8 %shard_map.97 = bf16[4,2,64,192]{3,2,1,0:T(8,128)(2,1)} custom-call(f32[2,4,64,192]{3,2,1,0:T(8,128)S(1)} %shard_map.96.acc_ref, bf16[2,64,384]{2,1,0:T(8,128)(2,1)S(1)} %collective-permute-done.3.ra_ref, bf16[2,64,384]{2,1,0:T(8,128)(2,1)S(1)} %collective-permute-done.4.rb_ref), custom_call_target="tpu_custom_call" | custom-call | flops 100000000 | bytes 786432 | tf_op jit(solution)/shard_map/pallas_call | solution.py:18
Async XLA Ops:
  3.9 9.0 %copy-start.5 = (f32[192]{0:T(256)S(1)}, f32[192]{0:T(256)}, u32[]{:S(2)}) copy-start(f32[192]{0:T(256)} %param.11) | copy-start | bytes 2308
  3.9 9.0 %copy-start.6 = (f32[192]{0:T(256)S(1)}, f32[192]{0:T(256)}, u32[]{:S(2)}) copy-start(f32[192]{0:T(256)} %param.15) | copy-start | bytes 2308
  3.9 10.7 %copy-start.1 = (bf16[4,2,64,384]{3,2,1,0:T(8,128)(2,1)S(1)}, bf16[4,2,64,384]{3,2,1,0:T(8,128)(2,1)}, u32[]{:S(2)}) copy-start(bf16[4,2,64,384]{3,2,1,0:T(8,128)(2,1)} %x_ref.1) | copy-start | bytes 1179652
  3.9 10.7 %copy-start.2 = (bf16[384,192]{0,1:T(8,128)(2,1)S(1)}, bf16[384,192]{0,1:T(8,128)(2,1)}, u32[]{:S(2)}) copy-start(bf16[384,192]{0,1:T(8,128)(2,1)} %param.16) | copy-start | bytes 442372
  3.9 10.7 %copy-start.3 = (f32[192]{0:T(256)S(1)}, f32[192]{0:T(256)}, u32[]{:S(2)}) copy-start(f32[192]{0:T(256)} %param.14) | copy-start | bytes 2308
  3.9 10.7 %copy-start.4 = (f32[192]{0:T(256)S(1)}, f32[192]{0:T(256)}, u32[]{:S(2)}) copy-start(f32[192]{0:T(256)} %param.17) | copy-start | bytes 2308
  3.9 19.9 %copy-start = (bf16[3,3,3,192,192]{4,3,2,1,0:T(8,128)(2,1)S(1)}, bf16[3,3,3,192,192]{4,3,2,1,0:T(8,128)(2,1)}, u32[]{:S(2)}) copy-start(bf16[3,3,3,192,192]{4,3,2,1,0:T(8,128)(2,1)} %w_ref.3) | copy-start | bytes 5971972
  3.9 6.0 %collective-permute-start = (bf16[3,64,384]{2,1,0:T(8,128)(2,1)S(1)}, bf16[3,64,384]{2,1,0:T(8,128)(2,1)S(1)}, u32[]{:S(2)}, u32[]{:S(2)}) collective-permute-start(bf16[3,64,384]{2,1,0:T(8,128)(2,1)S(1)} %get-tuple-element.19), channel_id=1, source_target_pairs={{0,1},{1,0},{2,3},{3,2},{4,5},{5,4},{6,7},{7,6},{8,9},{9,8},{10,11... | collective-permute-start | bytes 442376 | tf_op jit(solution)/shard_map/ppermute | solution.py:204
  4.7 8.2 %collective-permute-start.1 = (bf16[3,64,384]{2,1,0:T(8,128)(2,1)S(1)}, bf16[3,64,384]{2,1,0:T(8,128)(2,1)S(1)}, u32[]{:S(2)}, u32[]{:S(2)}) collective-permute-start(bf16[3,64,384]{2,1,0:T(8,128)(2,1)S(1)} %get-tuple-element.20), channel_id=1, source_target_pairs={{0,0},{31,31},{1,2},{2,1},{3,4},{4,3},{5,6},{6,5},{7,8},{8,7},{9,1... | collective-permute-start | bytes 442376 | tf_op jit(solution)/shard_map/ppermute | solution.py:204
  13.2 10.6 %collective-permute-start.2 = (bf16[2,2,64,384]{3,2,1,0:T(8,128)(2,1)S(1)}, bf16[2,2,64,384]{3,2,1,0:T(8,128)(2,1)S(1)}, u32[]{:S(2)}, u32[]{:S(2)}) collective-permute-start(bf16[2,2,64,384]{3,2,1,0:T(8,128)(2,1)S(1)} %get-tuple-element.22), channel_id=1, source_target_pairs={{0,32},{32,64},{64,96},{96,128},{128,160},{160,192},{192,224},{224... | collective-permute-start | bytes 589832 | tf_op jit(solution)/shard_map/ppermute | solution.py:222
  25.0 4.1 %collective-permute-start.3 = (bf16[2,64,384]{2,1,0:T(8,128)(2,1)S(1)}, bf16[2,64,384]{2,1,0:T(8,128)(2,1)S(1)}, u32[]{:S(2)}, u32[]{:S(2)}) collective-permute-start(bf16[2,64,384]{2,1,0:T(8,128)(2,1)S(1)} %get-tuple-element.27), channel_id=1, source_target_pairs={{0,1},{1,0},{2,3},{3,2},{4,5},{5,4},{6,7},{7,6},{8,9},{9,8},{10,11... | collective-permute-start | bytes 294920 | tf_op jit(solution)/shard_map/ppermute | solution.py:204
  25.5 7.0 %collective-permute-start.4 = (bf16[2,64,384]{2,1,0:T(8,128)(2,1)S(1)}, bf16[2,64,384]{2,1,0:T(8,128)(2,1)S(1)}, u32[]{:S(2)}, u32[]{:S(2)}) collective-permute-start(bf16[2,64,384]{2,1,0:T(8,128)(2,1)S(1)} %get-tuple-element.28), channel_id=1, source_target_pairs={{0,0},{31,31},{1,2},{2,1},{3,4},{4,3},{5,6},{6,5},{7,8},{8,7},{9,1... | collective-permute-start | bytes 294920 | tf_op jit(solution)/shard_map/ppermute | solution.py:204

commit v3 on v0

v3 whole, which is shorter than its diff:
```python
import jax
import jax.numpy as jnp
from jax import lax
from jax.experimental import pallas as pl
from jax.experimental.pallas import tpu as pltpu
from jax.sharding import PartitionSpec as P

F32 = jnp.float32
BF16 = jnp.bfloat16
COLS = 64
VMEM = pl.BlockSpec(memory_space=pltpu.VMEM)
HBM = pl.BlockSpec(memory_space=pltpu.HBM)


def call(body, outs, *args, flops=0, scratch=(), limit=8, in_hbm=()):
    args = [pltpu.with_memory_space_constraint(a, pltpu.HBM) if n in in_hbm else a for n, a in enumerate(args)]
    moved = sum(a.size * a.dtype.itemsize for a in args) + sum(o.size * o.dtype.itemsize for o in outs)
    return pl.pallas_call(
        body,
        out_shape=outs,
        in_specs=[HBM if n in in_hbm else VMEM for n in range(len(args))],
        out_specs=[VMEM] * len(outs),
        scratch_shapes=list(scratch),
        compiler_params=pltpu.CompilerParams(vmem_limit_bytes=limit << 20),
        cost_estimate=pl.CostEstimate(flops=flops, bytes_accessed=moved, transcendentals=0),
    )(*args)


def shape(dims, dtype=BF16):
    return jax.ShapeDtypeStruct(dims, dtype)


def act(values, gain):
    mean = jnp.mean(values * values, axis=-1, keepdims=True)
    scaled = values * lax.rsqrt(mean + 1e-06) * gain
    return scaled / (1.0 + jnp.exp(-scaled))


def taps(values):
    frames, _, channels = values.shape
    flat = values.reshape(frames * COLS, channels)
    col = lax.broadcasted_iota(jnp.int32, flat.shape, 0) % COLS
    left = jnp.where(col == 0, 0.0, pltpu.roll(flat, 1, 0))
    right = jnp.where(col == COLS - 1, 0.0, pltpu.roll(flat, frames * COLS - 1, 0))
    return jnp.concatenate([left, flat, right], axis=-1).astype(BF16).reshape(frames, COLS, 3 * channels)


def first_sums(fa_ref, w_ref, acc_ref):
    acc_ref[...] = jnp.zeros_like(acc_ref)
    for i in range(3):
        a = fa_ref[:, i : i + 2].reshape(4 * COLS, 1152)
        for j in range(3):
            w = jnp.concatenate([w_ref[i, j, k] for k in range(3)], axis=-1)
            out = lax.dot_general(a, w, (((1,), (1,)), ((), ())), preferred_element_type=F32)
            acc_ref[2 - j : 4 - j] += out.reshape(2, 2, COLS, 192)


def send_rows(acc_ref, a_ref, b_ref):
    odd = lax.axis_index("rows") % 2 == 1
    up = jnp.concatenate([acc_ref[0], acc_ref[1]], axis=-1)
    down = jnp.concatenate([acc_ref[2], acc_ref[3]], axis=-1)
    a_ref[...] = jnp.where(odd, up, down).astype(BF16)
    b_ref[...] = jnp.where(odd, down, up).astype(BF16)


def second_act(own_ref, rb_ref, ra_ref, bias_ref, gain_ref, sa_ref):
    rows = lax.axis_index("rows")
    odd = rows % 2 == 1
    a, b = ra_ref[...].astype(F32), rb_ref[...].astype(F32)
    above, below = jnp.where(odd, a, b), jnp.where(odd, b, a)
    top, bottom = rows == 0, rows == lax.axis_size("rows") - 1
    above, below = jnp.where(top, 0.0, above), jnp.where(bottom, 0.0, below)
    for row, rim in enumerate((above[..., :192], above[..., 192:], below[..., :192], below[..., 192:])):
        hidden = (own_ref[row] + rim + bias_ref[...]).astype(BF16).astype(F32)
        second = act(hidden, gain_ref[...])
        if row == 0:
            second = jnp.where(top, 0.0, second)
        if row == 3:
            second = jnp.where(bottom, 0.0, second)
        sa_ref[row] = taps(second)


def second_dot(a, w_ref, i, j):
    rows, frames = a.shape[:2]
    a = a.reshape(rows * frames * COLS, 576)
    out = jnp.dot(a, w_ref[i, j].reshape(576, 192), preferred_element_type=F32)
    return out.reshape(rows, frames, COLS, 192)


def act_kernel(x_hbm, g_hbm, fa_ref, t_ref, x_ref, g_ref, gsem, sem):
    gain_load = pltpu.make_async_copy(g_hbm, g_ref, gsem)
    loads = [pltpu.make_async_copy(x_hbm.at[t], x_ref.at[t], sem.at[t]) for t in range(4)]
    for load in [gain_load] + loads:
        load.start()
    gain_load.wait()
    gain = g_ref[...].reshape(1, 384)
    for t in range(4):
        loads[t].wait()
        for row in range(2):
            value = act(x_ref[t, row].astype(F32), gain)
            fa_ref[row, t] = taps(value[None])[0]
            if t >= 2:
                t_ref[row, t - 2] = value.astype(BF16)


def early_kernel(fa_ref, w_ref, own_ref, a_ref, b_ref):
    first_sums(fa_ref, w_ref, own_ref)
    send_rows(own_ref, a_ref, b_ref)


def late_kernel(t_ref, fa_ref, w_ref, own_ref, all_ref):
    first = lax.axis_index("tm") == 0
    for row in range(2):
        all_ref[row, 0:2] = taps(jnp.where(first, 0.0, t_ref[row].astype(F32)))
    all_ref[:, 2:4] = fa_ref[:, 0:2]
    first_sums(all_ref, w_ref, own_ref)


def next_kernel(rb_ref, own_ref, ra_ref, bias_ref, gain_ref, w_ref, late_ref, sa_ref, q_ref, a_ref, b_ref):
    send_rows(late_ref, a_ref, b_ref)
    second_act(own_ref, rb_ref, ra_ref, bias_ref, gain_ref, sa_ref)
    both = jnp.zeros((2, 2, COLS, 192), F32)
    one = jnp.zeros((2, 1, COLS, 192), F32)
    for j in range(3):
        both += second_dot(sa_ref[j : j + 2], w_ref, 0, j)
        one += second_dot(sa_ref[j : j + 2, 1:2], w_ref, 1, j)
    q_ref[0] = jnp.concatenate([both[0, 0] + one[0, 0], both[1, 0] + one[1, 0]], axis=-1).astype(BF16)
    q_ref[1] = jnp.concatenate([both[0, 1], both[1, 1]], axis=-1).astype(BF16)


def rest_kernel(sa_ref, w_ref, x_ref, sw_ref, bias_ref, sbias_ref, acc_ref):
    bias = bias_ref[...] + sbias_ref[...]
    for row in range(2):
        skip = lax.dot_general(
            x_ref[:, row].reshape(4 * COLS, 384), sw_ref[...], (((1,), (1,)), ((), ())), preferred_element_type=F32
        )
        acc_ref[row] = skip.reshape(4, COLS, 192) + bias
    for j in range(3):
        acc_ref[:, 2:4] += second_dot(sa_ref[j : j + 2], w_ref, 2, j)
        acc_ref[:, 3:4] += second_dot(sa_ref[j : j + 2, 0:1], w_ref, 1, j)


def second_kernel(
    q_ref, rb_ref, own_ref, ra_ref, bias_ref, gain_ref, w_ref, rest_ref, out_ref, acc_ref, sa_ref
):
    second_act(own_ref, rb_ref, ra_ref, bias_ref, gain_ref, sa_ref)
    acc_ref[...] = rest_ref[...]
    for i in range(3):
        for j in range(3):
            acc_ref[:, 2 - i : 4 - i] += second_dot(sa_ref[j : j + 2], w_ref, i, j)
    came = jnp.where(lax.axis_index("tm") == 0, 0.0, q_ref[...].astype(F32))
    for row in range(2):
        out_ref[0:2, row] = (acc_ref[row, 0:2] + came[..., 192 * row : 192 * row + 192]).astype(BF16)
        out_ref[2:4, row] = acc_ref[row, 2:4].astype(BF16)


def swap_pairs(count):
    inner = [(i, i ^ 1) for i in range(count)]
    outer = [(0, 0), (count - 1, count - 1)]
    for i in range(1, count - 1, 2):
        outer += [(i, i + 1), (i + 1, i)]
    return inner, outer


def per_device(x, w1, b1, g1, w2, b2, g2, sw, sb):
    inner, outer = swap_pairs(lax.axis_size("rows"))
    steps = lax.axis_size("tm")
    ring = [(i, (i + 1) % steps) for i in range(steps)]
    w1 = jnp.swapaxes(w1, 3, 4)
    sw = jnp.swapaxes(sw, 0, 1)
    b1, b2, g2, sb = (v.reshape(1, -1) for v in (b1, b2, g2, sb))
    sums = [shape((4, 2, COLS, 192), F32), shape((2, COLS, 384)), shape((2, COLS, 384))]

    fa, give = call(
        act_kernel, [shape((2, 4, COLS, 1152)), shape((2, 2, COLS, 384))], x, g1, flops=4 * 10**9, in_hbm=(0, 1),
        scratch=[
            pltpu.VMEM((4, 2, COLS, 384), BF16), pltpu.VMEM((384,), F32),
            pltpu.SemaphoreType.DMA(()), pltpu.SemaphoreType.DMA((4,)),
        ],
    )
    came = lax.ppermute(give, "tm", ring)
    own23, edge_a, edge_b = call(early_kernel, sums, fa, w1, flops=10**9)
    b23 = lax.ppermute(edge_b, "rows", outer)
    a23 = lax.ppermute(edge_a, "rows", inner)
    own01 = call(
        late_kernel, sums[:1], came, fa, w1, flops=10**9, scratch=[pltpu.VMEM((2, 4, COLS, 1152), BF16)]
    )[0]
    sa23, give, edge_a, edge_b = call(
        next_kernel, [shape((4, 2, COLS, 576)), shape((2, COLS, 384)), *sums[1:]],
        b23, own23, a23, b1, g2, w2, own01, flops=10**9,
    )
    came = lax.ppermute(give, "tm", ring)
    b01 = lax.ppermute(edge_b, "rows", outer)
    a01 = lax.ppermute(edge_a, "rows", inner)
    rest = call(rest_kernel, [shape((2, 4, COLS, 192), F32)], sa23, w2, x, sw, b2, sb, flops=10**9)[0]
    return call(
        second_kernel, [shape((4, 2, COLS, 192))], came, b01, own01, a01, b1, g2, w2, rest, flops=10**9,
        scratch=[pltpu.VMEM((2, 4, COLS, 192), F32), pltpu.VMEM((4, 2, COLS, 576), BF16)],
    )[0]


def solution(mesh):
    return jax.shard_map(
        per_device,
        mesh=mesh,
        in_specs=(P("tm", "rows", None, None), P(), P(), P(), P(), P(), P(), P(), P()),
        out_specs=P("tm", "rows", None, None),
        check_vma=False,
    )
```

time: 71.1 us -> 28.8 us (0.41)
  the two profiles are of different devices: /device:TPU:132 before, /device:TPU:152 now
where the time goes in v3:
time: 28.8 us; the launch traced here: 28.6 us
  starting transfers between devices  10.4 us (36%)
  Pallas kernels  10 us (35%)
  waiting for transfers between devices  8.01 us (28%)
    pallas_call x6, Pallas kernels, call(): pl.pallas_call(body, out_shape=outs, in_specs=[HBM if n in in_hbm else VM...  10 us
    ppermute x2, starting transfers between devices, per_device(): came = lax.ppermute(give, 'tm', ring)  5.04 us
    ppermute x1, waiting for transfers between devices, per_device(): b01 = lax.ppermute(edge_b, 'rows', outer)  4.48 us
    ppermute x1, waiting for transfers between devices, per_device(): b23 = lax.ppermute(edge_b, 'rows', outer)  3.52 us
    ppermute x1, starting transfers between devices, per_device(): b23 = lax.ppermute(edge_b, 'rows', outer)  1.92 us
    ppermute x1, starting transfers between devices, per_device(): b01 = lax.ppermute(edge_b, 'rows', outer)  1.91 us
    ppermute x1, starting transfers between devices, per_device(): a01 = lax.ppermute(edge_a, 'rows', inner)  0.78 us
    ppermute x1, starting transfers between devices, per_device(): a23 = lax.ppermute(edge_a, 'rows', inner)  0.77 us
  transfers between devices with their start and end apart: 6, of which 2 were waited for; matrix products, arithmetic and copies ran while one was open for 0% of the time, Pallas kernels for 15%

profile of v3, /device:TPU:152, one launch (start us, length us, event | category | flops | bytes accessed | tf_op | source)
XLA Modules:
  0.0 28.6 jit_solution(16575337776670237235)
XLA Ops:
  0.0 0.0 copy-start.1
  0.0 1.9 %shard_map.91 = (bf16[2,4,64,1152]{3,2,1,0:T(8,128)(2,1)S(1)}, bf16[2,2,64,384]{3,2,1,0:T(8,128)(2,1)S(1)}) custom-call(bf16[4,2,64,384]{3,2,1,0:T(8,128)(2,1)} %x_ref.1, f32[384]{0:T(512)} %g_hbm.1), custom_call_target="tpu_custom_call" | custom-call | flops 4000000000 | bytes 1771008 | tf_op jit(solution)/shard_map/pallas_call | solution.py:18
  1.9 2.8 %collective-permute-start.2 = (bf16[2,2,64,384]{3,2,1,0:T(8,128)(2,1)S(1)}, bf16[2,2,64,384]{3,2,1,0:T(8,128)(2,1)S(1)}, u32[]{:S(2)}, u32[]{:S(2)}) collective-permute-start(bf16[2,2,64,384]{3,2,1,0:T(8,128)(2,1)S(1)} %get-tuple-element.18), channel_id=1, source_target_pairs={{0,32},{32,64},{64,96},{96,128},{128,160},{160,192},{192,224},{224... | collective-permute-start | bytes 589832 | tf_op jit(solution)/shard_map/ppermute | solution.py:181
  4.7 0.0 copy-done.1
  4.7 1.8 %shard_map.92 = (f32[4,2,64,192]{3,2,1,0:T(8,128)S(1)}, bf16[2,64,384]{2,1,0:T(8,128)(2,1)S(1)}, bf16[2,64,384]{2,1,0:T(8,128)(2,1)S(1)}) custom-call(bf16[2,4,64,1152]{3,2,1,0:T(8,128)(2,1)S(1)} %get-tuple-element.14.fa_ref, bf16[3,3,3,192,384]{4,3,2,1,0:T(8,128)(2,1)S(1)} %bitcast.6), custom_call_target="tpu_custom_call" | custom-call | flops 1000000000 | bytes 5750784 | tf_op jit(solution)/shard_map/pallas_call | solution.py:18
  6.5 1.9 %collective-permute-start = (bf16[2,64,384]{2,1,0:T(8,128)(2,1)S(1)}, bf16[2,64,384]{2,1,0:T(8,128)(2,1)S(1)}, u32[]{:S(2)}, u32[]{:S(2)}) collective-permute-start(bf16[2,64,384]{2,1,0:T(8,128)(2,1)S(1)} %get-tuple-element.15), channel_id=1, source_target_pairs={{0,0},{31,31},{1,2},{2,1},{3,4},{4,3},{5,6},{6,5},{7,8},{8,7},{9,1... | collective-permute-start | bytes 294920 | tf_op jit(solution)/shard_map/ppermute | solution.py:183
  8.4 0.0 copy-start
  8.4 0.0 copy-start.4
  8.5 0.0 copy-start.5
  8.5 0.8 %collective-permute-start.1 = (bf16[2,64,384]{2,1,0:T(8,128)(2,1)S(1)}, bf16[2,64,384]{2,1,0:T(8,128)(2,1)S(1)}, u32[]{:S(2)}, u32[]{:S(2)}) collective-permute-start(bf16[2,64,384]{2,1,0:T(8,128)(2,1)S(1)} %get-tuple-element.17), channel_id=1, source_target_pairs={{0,1},{1,0},{2,3},{3,2},{4,5},{5,4},{6,7},{7,6},{8,9},{9,8},{10,11... | collective-permute-start | bytes 294920 | tf_op jit(solution)/shard_map/ppermute | solution.py:184
  9.2 0.0 collective-permute-done.2.t_ref
  9.2 1.7 %shard_map.93.late_ref.own_ref = f32[4,2,64,192]{3,2,1,0:T(8,128)S(1)} custom-call(bf16[2,2,64,384]{3,2,1,0:T(8,128)(2,1)S(1)} %collective-permute-done.2.t_ref, bf16[2,4,64,1152]{3,2,1,0:T(8,128)(2,1)S(1)} %get-tuple-element.14.fa_ref, bf16[3,3,3,192,384]{4,3,2,1,0:T(8,128)(2,1)S(1)} %bitcast.7), custom_call_target="tpu_custom_call" | custom-call | flops 1000000000 | bytes 5750784 | tf_op jit(solution)/shard_map/pallas_call | solution.py:18
  11.0 0.0 copy-start.2
  11.0 0.0 copy-start.3
  11.0 0.0 copy-start.6
  11.0 0.0 copy-start.7
  11.0 3.5 %collective-permute-done.rb_ref = bf16[2,64,384]{2,1,0:T(8,128)(2,1)S(1)} collective-permute-done((bf16[2,64,384]{2,1,0:T(8,128)(2,1)S(1)}, bf16[2,64,384]{2,1,0:T(8,128)(2,1)S(1)}, u32[]{:S(2)}, u32[]{:S(2)}) %collective-permute-start) | collective-permute-done | bytes 98336 | tf_op jit(solution)/shard_map/ppermute | solution.py:183
  14.5 0.0 collective-permute-done.1.ra_ref
  14.6 0.0 copy-done
  14.6 0.0 copy-done.4
  14.6 0.0 copy-done.5
  14.6 1.2 %shard_map.94 = (bf16[4,2,64,576]{3,2,1,0:T(8,128)(2,1)S(1)}, bf16[2,64,384]{2,1,0:T(8,128)(2,1)S(1)}, bf16[2,64,384]{2,1,0:T(8,128)(2,1)S(1)}, bf16[2,64,384]{2,1,0:T(8,128)(2,1)S(1)}) custom-call(bf16[2,64,384]{2,1,0:T(8,128)(2,1)S(1)} %collective-permute-done.rb_ref, f32[4,2,64,192]{3,2,1,0:T(8,128)S(1)} %get-tuple-element.16.own_ref, ...), custom_call_target="tpu_custom_call" | custom-call | flops 1000000000 | bytes 3859968 | tf_op jit(solution)/shard_map/pallas_call | solution.py:18
  15.8 2.3 %collective-permute-start.3 = (bf16[2,64,384]{2,1,0:T(8,128)(2,1)S(1)}, bf16[2,64,384]{2,1,0:T(8,128)(2,1)S(1)}, u32[]{:S(2)}, u32[]{:S(2)}) collective-permute-start(bf16[2,64,384]{2,1,0:T(8,128)(2,1)S(1)} %get-tuple-element.19), channel_id=1, source_target_pairs={{0,32},{32,64},{64,96},{96,128},{128,160},{160,192},{192,224},{224... | collective-permute-start | bytes 294920 | tf_op jit(solution)/shard_map/ppermute | solution.py:192
  18.1 1.9 %collective-permute-start.4 = (bf16[2,64,384]{2,1,0:T(8,128)(2,1)S(1)}, bf16[2,64,384]{2,1,0:T(8,128)(2,1)S(1)}, u32[]{:S(2)}, u32[]{:S(2)}) collective-permute-start(bf16[2,64,384]{2,1,0:T(8,128)(2,1)S(1)} %get-tuple-element.20), channel_id=1, source_target_pairs={{0,0},{31,31},{1,2},{2,1},{3,4},{4,3},{5,6},{6,5},{7,8},{8,7},{9,1... | collective-permute-start | bytes 294920 | tf_op jit(solution)/shard_map/ppermute | solution.py:193
  20.0 0.8 %collective-permute-start.5 = (bf16[2,64,384]{2,1,0:T(8,128)(2,1)S(1)}, bf16[2,64,384]{2,1,0:T(8,128)(2,1)S(1)}, u32[]{:S(2)}, u32[]{:S(2)}) collective-permute-start(bf16[2,64,384]{2,1,0:T(8,128)(2,1)S(1)} %get-tuple-element.21), channel_id=1, source_target_pairs={{0,1},{1,0},{2,3},{3,2},{4,5},{5,4},{6,7},{7,6},{8,9},{9,8},{10,11... | collective-permute-start | bytes 294920 | tf_op jit(solution)/shard_map/ppermute | solution.py:194
  20.8 0.0 copy-done.2
  20.8 0.0 copy-done.3
  20.8 0.0 copy-done.6
  20.8 0.0 copy-done.7
  20.8 0.8 %shard_map.95.rest_ref = f32[2,4,64,192]{3,2,1,0:T(8,128)S(1)} custom-call(bf16[4,2,64,576]{3,2,1,0:T(8,128)(2,1)S(1)} %get-tuple-element.22.sa_ref, bf16[3,3,3,192,192]{4,3,2,1,0:T(8,128)(2,1)S(1)} %copy-done, bf16[4,2,64,384]{3,2,1,0:T(8,128)(2,1)S(1)} %copy-done.2, bf16[192,384]{1,0:T(8,128)(2,1)S(1)} %bitcast.8, f32[1,192]{1,0:T(1,128)S(1)} %bitcast.13, ...), custom_call_target="tpu_custom_call" | custom-call | flops 1000000000 | bytes 3515904 | tf_op jit(solution)/shard_map/pallas_call | solution.py:18
  21.6 0.0 collective-permute-done.3.q_ref
  21.7 4.5 %collective-permute-done.4.rb_ref = bf16[2,64,384]{2,1,0:T(8,128)(2,1)S(1)} collective-permute-done((bf16[2,64,384]{2,1,0:T(8,128)(2,1)S(1)}, bf16[2,64,384]{2,1,0:T(8,128)(2,1)S(1)}, u32[]{:S(2)}, u32[]{:S(2)}) %collective-permute-start.4) | collective-permute-done | bytes 98336 | tf_op jit(solution)/shard_map/ppermute | solution.py:193
  26.1 0.0 collective-permute-done.5.ra_ref
  26.1 2.5 %shard_map.96 = bf16[4,2,64,192]{3,2,1,0:T(8,128)(2,1)} custom-call(bf16[2,64,384]{2,1,0:T(8,128)(2,1)S(1)} %collective-permute-done.3.q_ref, bf16[2,64,384]{2,1,0:T(8,128)(2,1)S(1)} %collective-permute-done.4.rb_ref, f32[4,2,64,192]{3,2,1,0:T(8,128)S(1)} %shard_map.93.late_ref.own_ref, bf16[2,64,384]{2,1,0:T(8,128)(2,1)S(1)} %collective-permute-done.5.ra_ref, ...), custom_call_target="tpu_custom_call" | custom-call | flops 1000000000 | bytes 3270144 | tf_op jit(solution)/shard_map/pallas_call | solution.py:18
Async XLA Ops:
  0.0 4.7 %copy-start.1 = (bf16[3,3,3,384,192]{3,4,2,1,0:T(8,128)(2,1)S(1)}, bf16[3,3,3,384,192]{3,4,2,1,0:T(8,128)(2,1)}, u32[]{:S(2)}) copy-start(bf16[3,3,3,384,192]{3,4,2,1,0:T(8,128)(2,1)} %param.10) | copy-start | bytes 11943940
  1.9 7.3 %collective-permute-start.2 = (bf16[2,2,64,384]{3,2,1,0:T(8,128)(2,1)S(1)}, bf16[2,2,64,384]{3,2,1,0:T(8,128)(2,1)S(1)}, u32[]{:S(2)}, u32[]{:S(2)}) collective-permute-start(bf16[2,2,64,384]{3,2,1,0:T(8,128)(2,1)S(1)} %get-tuple-element.18), channel_id=1, source_target_pairs={{0,32},{32,64},{64,96},{96,128},{128,160},{160,192},{192,224},{224... | collective-permute-start | bytes 589832 | tf_op jit(solution)/shard_map/ppermute | solution.py:181
  6.5 8.0 %collective-permute-start = (bf16[2,64,384]{2,1,0:T(8,128)(2,1)S(1)}, bf16[2,64,384]{2,1,0:T(8,128)(2,1)S(1)}, u32[]{:S(2)}, u32[]{:S(2)}) collective-permute-start(bf16[2,64,384]{2,1,0:T(8,128)(2,1)S(1)} %get-tuple-element.15), channel_id=1, source_target_pairs={{0,0},{31,31},{1,2},{2,1},{3,4},{4,3},{5,6},{6,5},{7,8},{8,7},{9,1... | collective-permute-start | bytes 294920 | tf_op jit(solution)/shard_map/ppermute | solution.py:183
  8.4 6.1 %copy-start = (bf16[3,3,3,192,192]{4,3,2,1,0:T(8,128)(2,1)S(1)}, bf16[3,3,3,192,192]{4,3,2,1,0:T(8,128)(2,1)}, u32[]{:S(2)}) copy-start(bf16[3,3,3,192,192]{4,3,2,1,0:T(8,128)(2,1)} %w_ref.5) | copy-start | bytes 5971972
  8.4 6.1 %copy-start.4 = (f32[192]{0:T(256)S(1)}, f32[192]{0:T(256)}, u32[]{:S(2)}) copy-start(f32[192]{0:T(256)} %param.11) | copy-start | bytes 2308
  8.5 6.1 %copy-start.5 = (f32[192]{0:T(256)S(1)}, f32[192]{0:T(256)}, u32[]{:S(2)}) copy-start(f32[192]{0:T(256)} %param.15) | copy-start | bytes 2308
  8.5 6.1 %collective-permute-start.1 = (bf16[2,64,384]{2,1,0:T(8,128)(2,1)S(1)}, bf16[2,64,384]{2,1,0:T(8,128)(2,1)S(1)}, u32[]{:S(2)}, u32[]{:S(2)}) collective-permute-start(bf16[2,64,384]{2,1,0:T(8,128)(2,1)S(1)} %get-tuple-element.17), channel_id=1, source_target_pairs={{0,1},{1,0},{2,3},{3,2},{4,5},{5,4},{6,7},{7,6},{8,9},{9,8},{10,11... | collective-permute-start | bytes 294920 | tf_op jit(solution)/shard_map/ppermute | solution.py:184
  11.0 9.8 %copy-start.2 = (bf16[4,2,64,384]{3,2,1,0:T(8,128)(2,1)S(1)}, bf16[4,2,64,384]{3,2,1,0:T(8,128)(2,1)}, u32[]{:S(2)}) copy-start(bf16[4,2,64,384]{3,2,1,0:T(8,128)(2,1)} %x_ref.1) | copy-start | bytes 1179652
  11.0 9.8 %copy-start.3 = (bf16[384,192]{0,1:T(8,128)(2,1)S(1)}, bf16[384,192]{0,1:T(8,128)(2,1)}, u32[]{:S(2)}) copy-start(bf16[384,192]{0,1:T(8,128)(2,1)} %param.16) | copy-start | bytes 442372
  11.0 9.8 %copy-start.6 = (f32[192]{0:T(256)S(1)}, f32[192]{0:T(256)}, u32[]{:S(2)}) copy-start(f32[192]{0:T(256)} %param.14) | copy-start | bytes 2308
  11.0 9.8 %copy-start.7 = (f32[192]{0:T(256)S(1)}, f32[192]{0:T(256)}, u32[]{:S(2)}) copy-start(f32[192]{0:T(256)} %param.17) | copy-start | bytes 2308
  15.8 5.8 %collective-permute-start.3 = (bf16[2,64,384]{2,1,0:T(8,128)(2,1)S(1)}, bf16[2,64,384]{2,1,0:T(8,128)(2,1)S(1)}, u32[]{:S(2)}, u32[]{:S(2)}) collective-permute-start(bf16[2,64,384]{2,1,0:T(8,128)(2,1)S(1)} %get-tuple-element.19), channel_id=1, source_target_pairs={{0,32},{32,64},{64,96},{96,128},{128,160},{160,192},{192,224},{224... | collective-permute-start | bytes 294920 | tf_op jit(solution)/shard_map/ppermute | solution.py:192
  18.1 8.0 %collective-permute-start.4 = (bf16[2,64,384]{2,1,0:T(8,128)(2,1)S(1)}, bf16[2,64,384]{2,1,0:T(8,128)(2,1)S(1)}, u32[]{:S(2)}, u32[]{:S(2)}) collective-permute-start(bf16[2,64,384]{2,1,0:T(8,128)(2,1)S(1)} %get-tuple-element.20), channel_id=1, source_target_pairs={{0,0},{31,31},{1,2},{2,1},{3,4},{4,3},{5,6},{6,5},{7,8},{8,7},{9,1... | collective-permute-start | bytes 294920 | tf_op jit(solution)/shard_map/ppermute | solution.py:193
  20.0 6.1 %collective-permute-start.5 = (bf16[2,64,384]{2,1,0:T(8,128)(2,1)S(1)}, bf16[2,64,384]{2,1,0:T(8,128)(2,1)S(1)}, u32[]{:S(2)}, u32[]{:S(2)}) collective-permute-start(bf16[2,64,384]{2,1,0:T(8,128)(2,1)S(1)} %get-tuple-element.21), channel_id=1, source_target_pairs={{0,1},{1,0},{2,3},{3,2},{4,5},{5,4},{6,7},{7,6},{8,9},{9,8},{10,11... | collective-permute-start | bytes 294920 | tf_op jit(solution)/shard_map/ppermute | solution.py:194

commit v4 on v3

--- a/solution.py
+++ b/solution.py
@@ -45,22 +45,21 @@
     return jnp.concatenate([left, flat, right], axis=-1).astype(BF16).reshape(frames, COLS, 3 * channels)
 
 
-def first_sums(fa_ref, w_ref, acc_ref):
-    acc_ref[...] = jnp.zeros_like(acc_ref)
-    for i in range(3):
-        a = fa_ref[:, i : i + 2].reshape(4 * COLS, 1152)
+def first_sums(parts, w_ref, acc_ref):
+    for i, source, frames in parts:
+        count = source.shape[1]
+        a = source.reshape(2 * count * COLS, 1152)
         for j in range(3):
             w = jnp.concatenate([w_ref[i, j, k] for k in range(3)], axis=-1)
             out = lax.dot_general(a, w, (((1,), (1,)), ((), ())), preferred_element_type=F32)
-            acc_ref[2 - j : 4 - j] += out.reshape(2, 2, COLS, 192)
-
-
-def send_rows(acc_ref, a_ref, b_ref):
+            acc_ref[2 - j : 4 - j, frames] += out.reshape(2, count, COLS, 192)
+
+
+def edge_rows(acc_ref, outer):
     odd = lax.axis_index("rows") % 2 == 1
     up = jnp.concatenate([acc_ref[0], acc_ref[1]], axis=-1)
     down = jnp.concatenate([acc_ref[2], acc_ref[3]], axis=-1)
-    a_ref[...] = jnp.where(odd, up, down).astype(BF16)
-    b_ref[...] = jnp.where(odd, down, up).astype(BF16)
+    return jnp.where(odd, down if outer else up, up if outer else down).astype(BF16)
 
 
 def second_act(own_ref, rb_ref, ra_ref, bias_ref, gain_ref, sa_ref):
@@ -103,21 +102,31 @@
                 t_ref[row, t - 2] = value.astype(BF16)
 
 
-def early_kernel(fa_ref, w_ref, own_ref, a_ref, b_ref):
-    first_sums(fa_ref, w_ref, own_ref)
-    send_rows(own_ref, a_ref, b_ref)
-
-
-def late_kernel(t_ref, fa_ref, w_ref, own_ref, all_ref):
+def early_kernel(fa_ref, w_ref, own_ref, b_ref):
+    own_ref[...] = jnp.zeros_like(own_ref)
+    first_sums([(i, fa_ref[:, i : i + 2], slice(0, 2)) for i in range(3)], w_ref, own_ref)
+    b_ref[...] = edge_rows(own_ref, True)
+
+
+def between_kernel(own_ref, fa_ref, w_ref, part_ref, a_ref):
+    a_ref[...] = edge_rows(own_ref, False)
+    part_ref[...] = jnp.zeros_like(part_ref)
+    parts = [(2, fa_ref[:, 0:2], slice(0, 2)), (1, fa_ref[:, 0:1], slice(1, 2))]
+    first_sums(parts, w_ref, part_ref)
+
+
+def late_kernel(t_ref, part_ref, w_ref, after_ref, own_ref, b_ref, fa_ref):
+    del after_ref
     first = lax.axis_index("tm") == 0
     for row in range(2):
-        all_ref[row, 0:2] = taps(jnp.where(first, 0.0, t_ref[row].astype(F32)))
-    all_ref[:, 2:4] = fa_ref[:, 0:2]
-    first_sums(all_ref, w_ref, own_ref)
-
-
-def next_kernel(rb_ref, own_ref, ra_ref, bias_ref, gain_ref, w_ref, late_ref, sa_ref, q_ref, a_ref, b_ref):
-    send_rows(late_ref, a_ref, b_ref)
+        fa_ref[row] = taps(jnp.where(first, 0.0, t_ref[row].astype(F32)))
+    own_ref[...] = part_ref[...]
+    parts = [(0, fa_ref[...], slice(0, 2)), (1, fa_ref[:, 1:2], slice(0, 1))]
+    first_sums(parts, w_ref, own_ref)
+    b_ref[...] = edge_rows(own_ref, True)
+
+
+def next_kernel(rb_ref, own_ref, ra_ref, bias_ref, gain_ref, w_ref, sa_ref, q_ref):
     second_act(own_ref, rb_ref, ra_ref, bias_ref, gain_ref, sa_ref)
     both = jnp.zeros((2, 2, COLS, 192), F32)
     one = jnp.zeros((2, 1, COLS, 192), F32)
@@ -128,7 +137,8 @@
     q_ref[1] = jnp.concatenate([both[0, 1], both[1, 1]], axis=-1).astype(BF16)
 
 
-def rest_kernel(sa_ref, w_ref, x_ref, sw_ref, bias_ref, sbias_ref, acc_ref):
+def rest_kernel(own_ref, sa_ref, w_ref, x_ref, sw_ref, bias_ref, sbias_ref, acc_ref, a_ref):
+    a_ref[...] = edge_rows(own_ref, False)
     bias = bias_ref[...] + sbias_ref[...]
     for row in range(2):
         skip = lax.dot_general(
@@ -154,22 +164,26 @@
         out_ref[2:4, row] = acc_ref[row, 2:4].astype(BF16)
 
 
-def swap_pairs(count):
+def swap_pairs(steps, count):
     inner = [(i, i ^ 1) for i in range(count)]
-    outer = [(0, 0), (count - 1, count - 1)]
-    for i in range(1, count - 1, 2):
-        outer += [(i, i + 1), (i + 1, i)]
+    outer = []
+    for t in range(steps):
+        base = t * count
+        for i in range(1, count - 1, 2):
+            outer += [(base + i, base + i + 1), (base + i + 1, base + i)]
+        for i in (0, count - 1):
+            outer.append((base + i, (t ^ 1) * count + i))
     return inner, outer
 
 
 def per_device(x, w1, b1, g1, w2, b2, g2, sw, sb):
-    inner, outer = swap_pairs(lax.axis_size("rows"))
     steps = lax.axis_size("tm")
+    inner, outer = swap_pairs(steps, lax.axis_size("rows"))
     ring = [(i, (i + 1) % steps) for i in range(steps)]
     w1 = jnp.swapaxes(w1, 3, 4)
     sw = jnp.swapaxes(sw, 0, 1)
     b1, b2, g2, sb = (v.reshape(1, -1) for v in (b1, b2, g2, sb))
-    sums = [shape((4, 2, COLS, 192), F32), shape((2, COLS, 384)), shape((2, COLS, 384))]
+    sums, edges = shape((4, 2, COLS, 192), F32), shape((2, COLS, 384))
 
     fa, give = call(
         act_kernel, [shape((2, 4, COLS, 1152)), shape((2, 2, COLS, 384))], x, g1, flops=4 * 10**9, in_hbm=(0, 1),
@@ -179,22 +193,24 @@
         ],
     )
     came = lax.ppermute(give, "tm", ring)
-    own23, edge_a, edge_b = call(early_kernel, sums, fa, w1, flops=10**9)
-    b23 = lax.ppermute(edge_b, "rows", outer)
-    a23 = lax.ppermute(edge_a, "rows", inner)
-    own01 = call(
-        late_kernel, sums[:1], came, fa, w1, flops=10**9, scratch=[pltpu.VMEM((2, 4, COLS, 1152), BF16)]
-    )[0]
-    sa23, give, edge_a, edge_b = call(
-        next_kernel, [shape((4, 2, COLS, 576)), shape((2, COLS, 384)), *sums[1:]],
-        b23, own23, a23, b1, g2, w2, own01, flops=10**9,
-    )
-    came = lax.ppermute(give, "tm", ring)
-    b01 = lax.ppermute(edge_b, "rows", outer)
-    a01 = lax.ppermute(edge_a, "rows", inner)
-    rest = call(rest_kernel, [shape((2, 4, COLS, 192), F32)], sa23, w2, x, sw, b2, sb, flops=10**9)[0]
+    own23, edge = call(early_kernel, [sums, edges], fa, w1, flops=10**9)
+    b23 = lax.optimization_barrier(lax.ppermute(edge, ("tm", "rows"), outer))
+    part, edge = call(between_kernel, [sums, edges], own23, fa, w1, flops=10**9)
+    a23 = lax.ppermute(edge, "rows", inner)
+    sa23, give = call(
+        next_kernel, [shape((4, 2, COLS, 576)), edges], b23, own23, a23, b1, g2, w2, flops=10**9
+    )
+    q = lax.ppermute(give, "tm", ring)
+    own01, edge = call(
+        late_kernel, [sums, edges], came, part, w1, sa23, flops=10**9, scratch=[pltpu.VMEM((2, 2, COLS, 1152), BF16)]
+    )
+    b01 = lax.optimization_barrier(lax.ppermute(edge, ("tm", "rows"), outer))
+    rest, edge = call(
+        rest_kernel, [shape((2, 4, COLS, 192), F32), edges], own01, sa23, w2, x, sw, b2, sb, flops=10**9
+    )
+    a01 = lax.ppermute(edge, "rows", inner)
     return call(
-        second_kernel, [shape((4, 2, COLS, 192))], came, b01, own01, a01, b1, g2, w2, rest, flops=10**9,
+        second_kernel, [shape((4, 2, COLS, 192))], q, b01, own01, a01, b1, g2, w2, rest, flops=10**9,
         scratch=[pltpu.VMEM((2, 4, COLS, 192), F32), pltpu.VMEM((4, 2, COLS, 576), BF16)],
     )[0]
 

time: 28.8 us -> 25.8 us (0.90)
  the two profiles are of different devices: /device:TPU:152 before, /device:TPU:132 now
where the time goes in v4:
time: 25.8 us; the launch traced here: 25.5 us
  Pallas kernels  10.6 us (41%)
  waiting for transfers between devices  9.57 us (37%)
  starting transfers between devices  5.17 us (20%)
    pallas_call x7, Pallas kernels, call(): pl.pallas_call(body, out_shape=outs, in_specs=[HBM if n in in_hbm else VM...  10.6 us
    ppermute x1, waiting for transfers between devices, per_device(): b01 = lax.optimization_barrier(lax.ppermute(edge, ('tm', 'rows'), outer))  4.96 us
    ppermute x1, waiting for transfers between devices, per_device(): b23 = lax.optimization_barrier(lax.ppermute(edge, ('tm', 'rows'), outer))  3.63 us
    ppermute x1, starting transfers between devices, per_device(): q = lax.ppermute(give, 'tm', ring)  1.66 us
    ppermute x1, starting transfers between devices, per_device(): came = lax.ppermute(give, 'tm', ring)  1.65 us
    ppermute x1, starting transfers between devices, per_device(): a23 = lax.ppermute(edge, 'rows', inner)  1.36 us
    ppermute x1, waiting for transfers between devices, per_device(): q = lax.ppermute(give, 'tm', ring)  0.97 us
  transfers between devices with their start and end apart: 6, of which 3 were waited for; matrix products, arithmetic and copies ran while one was open for 0% of the time, Pallas kernels for 24%

profile of v4, /device:TPU:132, one launch (start us, length us, event | category | flops | bytes accessed | tf_op | source)
XLA Modules:
  0.0 25.5 jit_solution(2247905634480648605)
XLA Ops:
  0.0 0.0 copy-start
  0.0 1.9 %shard_map.91 = (bf16[2,4,64,1152]{3,2,1,0:T(8,128)(2,1)S(1)}, bf16[2,2,64,384]{3,2,1,0:T(8,128)(2,1)S(1)}) custom-call(bf16[4,2,64,384]{3,2,1,0:T(8,128)(2,1)} %x_ref.1, f32[384]{0:T(512)} %g_hbm.1), custom_call_target="tpu_custom_call" | custom-call | flops 4000000000 | bytes 1771008 | tf_op jit(solution)/shard_map/pallas_call | solution.py:18
  1.9 1.7 %collective-permute-start.3 = (bf16[2,2,64,384]{3,2,1,0:T(8,128)(2,1)S(1)}, bf16[2,2,64,384]{3,2,1,0:T(8,128)(2,1)S(1)}, u32[]{:S(2)}, u32[]{:S(2)}) collective-permute-start(bf16[2,2,64,384]{3,2,1,0:T(8,128)(2,1)S(1)} %get-tuple-element.22), channel_id=1, source_target_pairs={{0,32},{32,64},{64,96},{96,128},{128,160},{160,192},{192,224},{224... | collective-permute-start | bytes 589832 | tf_op jit(solution)/shard_map/ppermute | solution.py:195
  3.6 0.0 copy-done
  3.6 1.8 %shard_map.92 = (f32[4,2,64,192]{3,2,1,0:T(8,128)S(1)}, bf16[2,64,384]{2,1,0:T(8,128)(2,1)S(1)}) custom-call(bf16[2,4,64,1152]{3,2,1,0:T(8,128)(2,1)S(1)} %get-tuple-element.17.fa_ref, bf16[3,3,3,192,384]{4,3,2,1,0:T(8,128)(2,1)S(1)} %bitcast.6), custom_call_target="tpu_custom_call" | custom-call | flops 1000000000 | bytes 5652480 | tf_op jit(solution)/shard_map/pallas_call | solution.py:18
  5.4 0.1 collective-permute-start
  5.5 0.0 copy-start.1
  5.5 0.0 copy-start.6
  5.5 0.0 copy-start.7
  5.6 1.1 %shard_map.93 = (f32[4,2,64,192]{3,2,1,0:T(8,128)S(1)}, bf16[2,64,384]{2,1,0:T(8,128)(2,1)S(1)}) custom-call(f32[4,2,64,192]{3,2,1,0:T(8,128)S(1)} %get-tuple-element.19.own_ref, bf16[2,4,64,1152]{3,2,1,0:T(8,128)(2,1)S(1)} %get-tuple-element.17.fa_ref, bf16[3,3,3,192,384]{4,3,2,1,0:T(8,128)(2,1)S(1)} %bitcast.7), custom_call_target="tpu_custom_call" | custom-call | flops 1000000000 | bytes 6045696 | tf_op jit(solution)/shard_map/pallas_call | solution.py:18
  6.7 1.4 %collective-permute-start.1 = (bf16[2,64,384]{2,1,0:T(8,128)(2,1)S(1)}, bf16[2,64,384]{2,1,0:T(8,128)(2,1)S(1)}, u32[]{:S(2)}, u32[]{:S(2)}) collective-permute-start(bf16[2,64,384]{2,1,0:T(8,128)(2,1)S(1)} %get-tuple-element.20), channel_id=1, source_target_pairs={{0,1},{1,0},{2,3},{3,2},{4,5},{5,4},{6,7},{7,6},{8,9},{9,8},{10,11... | collective-permute-start | bytes 294920 | tf_op jit(solution)/shard_map/ppermute | solution.py:199
  8.0 3.6 %collective-permute-done.rb_ref = bf16[2,64,384]{2,1,0:T(8,128)(2,1)S(1)} collective-permute-done((bf16[2,64,384]{2,1,0:T(8,128)(2,1)S(1)}, bf16[2,64,384]{2,1,0:T(8,128)(2,1)S(1)}, u32[]{:S(2)}, u32[]{:S(2)}) %collective-permute-start) | collective-permute-done | bytes 98336 | tf_op jit(solution)/shard_map/ppermute | solution.py:197
  11.7 0.0 collective-permute-done.1.ra_ref
  11.7 0.0 copy-done.1
  11.7 0.0 copy-done.6
  11.7 0.0 copy-done.7
  11.7 1.2 %shard_map.94 = (bf16[4,2,64,576]{3,2,1,0:T(8,128)(2,1)S(1)}, bf16[2,64,384]{2,1,0:T(8,128)(2,1)S(1)}) custom-call(bf16[2,64,384]{2,1,0:T(8,128)(2,1)S(1)} %collective-permute-done.rb_ref, f32[4,2,64,192]{3,2,1,0:T(8,128)S(1)} %get-tuple-element.19.own_ref, bf16[2,64,384]{2,1,0:T(8,128)(2,1)S(1)} %collective-permute-done.1.ra_ref, f32[1,192]{1,0:T(1,128)S(1)} %bitcast.12, ...), custom_call_target="tpu_custom_call" | custom-call | flops 1000000000 | bytes 3270144 | tf_op jit(solution)/shard_map/pallas_call | solution.py:18
  12.9 1.7 %collective-permute-start.2 = (bf16[2,64,384]{2,1,0:T(8,128)(2,1)S(1)}, bf16[2,64,384]{2,1,0:T(8,128)(2,1)S(1)}, u32[]{:S(2)}, u32[]{:S(2)}) collective-permute-start(bf16[2,64,384]{2,1,0:T(8,128)(2,1)S(1)} %get-tuple-element.21), channel_id=1, source_target_pairs={{0,32},{32,64},{64,96},{96,128},{128,160},{160,192},{192,224},{224... | collective-permute-start | bytes 294920 | tf_op jit(solution)/shard_map/ppermute | solution.py:203
  14.6 0.0 collective-permute-done.3.t_ref
  14.6 0.0 copy-start.2
  14.6 0.0 copy-start.3
  14.6 0.0 copy-start.4
  14.6 0.0 copy-start.5
  14.6 1.2 %shard_map.95 = (f32[4,2,64,192]{3,2,1,0:T(8,128)S(1)}, bf16[2,64,384]{2,1,0:T(8,128)(2,1)S(1)}) custom-call(bf16[2,2,64,384]{3,2,1,0:T(8,128)(2,1)S(1)} %collective-permute-done.3.t_ref, f32[4,2,64,192]{3,2,1,0:T(8,128)S(1)} %get-tuple-element.23.part_ref, bf16[3,3,3,192,384]{4,3,2,1,0:T(8,128)(2,1)S(1)} %bitcast.8, ...), custom_call_target="tpu_custom_call" | custom-call | flops 1000000000 | bytes 5652480 | tf_op jit(solution)/shard_map/pallas_call | solution.py:18
  15.8 0.1 collective-permute-start.4
  15.9 0.0 copy-done.2
  15.9 0.0 copy-done.3
  16.0 0.0 copy-done.4
  16.0 0.0 copy-done.5
  16.0 0.8 %shard_map.96 = (f32[2,4,64,192]{3,2,1,0:T(8,128)S(1)}, bf16[2,64,384]{2,1,0:T(8,128)(2,1)S(1)}) custom-call(f32[4,2,64,192]{3,2,1,0:T(8,128)S(1)} %get-tuple-element.26.own_ref, bf16[4,2,64,576]{3,2,1,0:T(8,128)(2,1)S(1)} %get-tuple-element.24.after_ref.sa_ref, bf16[3,3,3,192,192]{4,3,2,1,0:T(8,128)(2,1)S(1)} %copy-done.1, ...), custom_call_target="tpu_custom_call" | custom-call | flops 1000000000 | bytes 4007424 | tf_op jit(solution)/shard_map/pallas_call | solution.py:18
  16.8 0.3 %collective-permute-start.5 = (bf16[2,64,384]{2,1,0:T(8,128)(2,1)S(1)}, bf16[2,64,384]{2,1,0:T(8,128)(2,1)S(1)}, u32[]{:S(2)}, u32[]{:S(2)}) collective-permute-start(bf16[2,64,384]{2,1,0:T(8,128)(2,1)S(1)} %get-tuple-element.27), channel_id=1, source_target_pairs={{0,1},{1,0},{2,3},{3,2},{4,5},{5,4},{6,7},{7,6},{8,9},{9,8},{10,11... | collective-permute-start | bytes 294920 | tf_op jit(solution)/shard_map/ppermute | solution.py:211
  17.1 5.0 %collective-permute-done.4.rb_ref = bf16[2,64,384]{2,1,0:T(8,128)(2,1)S(1)} collective-permute-done((bf16[2,64,384]{2,1,0:T(8,128)(2,1)S(1)}, bf16[2,64,384]{2,1,0:T(8,128)(2,1)S(1)}, u32[]{:S(2)}, u32[]{:S(2)}) %collective-permute-start.4) | collective-permute-done | bytes 98336 | tf_op jit(solution)/shard_map/ppermute | solution.py:207
  22.1 1.0 %collective-permute-done.2.q_ref = bf16[2,64,384]{2,1,0:T(8,128)(2,1)S(1)} collective-permute-done((bf16[2,64,384]{2,1,0:T(8,128)(2,1)S(1)}, bf16[2,64,384]{2,1,0:T(8,128)(2,1)S(1)}, u32[]{:S(2)}, u32[]{:S(2)}) %collective-permute-start.2) | collective-permute-done | bytes 98336 | tf_op jit(solution)/shard_map/ppermute | solution.py:203
  23.0 0.0 collective-permute-done.5.ra_ref
  23.0 2.5 %shard_map.97 = bf16[4,2,64,192]{3,2,1,0:T(8,128)(2,1)} custom-call(bf16[2,64,384]{2,1,0:T(8,128)(2,1)S(1)} %collective-permute-done.2.q_ref, bf16[2,64,384]{2,1,0:T(8,128)(2,1)S(1)} %collective-permute-done.4.rb_ref, f32[4,2,64,192]{3,2,1,0:T(8,128)S(1)} %get-tuple-element.26.own_ref, bf16[2,64,384]{2,1,0:T(8,128)(2,1)S(1)} %collective-permute-done.5.ra_ref, ...), custom_call_target="tpu_custom_call" | custom-call | flops 1000000000 | bytes 3270144 | tf_op jit(solution)/shard_map/pallas_call | solution.py:18
Async XLA Ops:
  0.0 3.6 %copy-start = (bf16[3,3,3,384,192]{3,4,2,1,0:T(8,128)(2,1)S(1)}, bf16[3,3,3,384,192]{3,4,2,1,0:T(8,128)(2,1)}, u32[]{:S(2)}) copy-start(bf16[3,3,3,384,192]{3,4,2,1,0:T(8,128)(2,1)} %param.10) | copy-start | bytes 11943940
  1.9 12.7 %collective-permute-start.3 = (bf16[2,2,64,384]{3,2,1,0:T(8,128)(2,1)S(1)}, bf16[2,2,64,384]{3,2,1,0:T(8,128)(2,1)S(1)}, u32[]{:S(2)}, u32[]{:S(2)}) collective-permute-start(bf16[2,2,64,384]{3,2,1,0:T(8,128)(2,1)S(1)} %get-tuple-element.22), channel_id=1, source_target_pairs={{0,32},{32,64},{64,96},{96,128},{128,160},{160,192},{192,224},{224... | collective-permute-start | bytes 589832 | tf_op jit(solution)/shard_map/ppermute | solution.py:195
  5.4 6.2 %collective-permute-start = (bf16[2,64,384]{2,1,0:T(8,128)(2,1)S(1)}, bf16[2,64,384]{2,1,0:T(8,128)(2,1)S(1)}, u32[]{:S(2)}, u32[]{:S(2)}) collective-permute-start(bf16[2,64,384]{2,1,0:T(8,128)(2,1)S(1)} %get-tuple-element.18), channel_id=1, source_target_pairs={{1,2},{2,1},{3,4},{4,3},{5,6},{6,5},{7,8},{8,7},{9,10},{10,9},{11,... | collective-permute-start | bytes 294920 | tf_op jit(solution)/shard_map/ppermute | solution.py:197
  5.5 6.1 %copy-start.1 = (bf16[3,3,3,192,192]{4,3,2,1,0:T(8,128)(2,1)S(1)}, bf16[3,3,3,192,192]{4,3,2,1,0:T(8,128)(2,1)}, u32[]{:S(2)}) copy-start(bf16[3,3,3,192,192]{4,3,2,1,0:T(8,128)(2,1)} %w_ref.5) | copy-start | bytes 5971972
  5.5 6.1 %copy-start.6 = (f32[192]{0:T(256)S(1)}, f32[192]{0:T(256)}, u32[]{:S(2)}) copy-start(f32[192]{0:T(256)} %param.11) | copy-start | bytes 2308
  5.5 6.1 %copy-start.7 = (f32[192]{0:T(256)S(1)}, f32[192]{0:T(256)}, u32[]{:S(2)}) copy-start(f32[192]{0:T(256)} %param.15) | copy-start | bytes 2308
  6.7 5.0 %collective-permute-start.1 = (bf16[2,64,384]{2,1,0:T(8,128)(2,1)S(1)}, bf16[2,64,384]{2,1,0:T(8,128)(2,1)S(1)}, u32[]{:S(2)}, u32[]{:S(2)}) collective-permute-start(bf16[2,64,384]{2,1,0:T(8,128)(2,1)S(1)} %get-tuple-element.20), channel_id=1, source_target_pairs={{0,1},{1,0},{2,3},{3,2},{4,5},{5,4},{6,7},{7,6},{8,9},{9,8},{10,11... | collective-permute-start | bytes 294920 | tf_op jit(solution)/shard_map/ppermute | solution.py:199
  12.9 10.1 %collective-permute-start.2 = (bf16[2,64,384]{2,1,0:T(8,128)(2,1)S(1)}, bf16[2,64,384]{2,1,0:T(8,128)(2,1)S(1)}, u32[]{:S(2)}, u32[]{:S(2)}) collective-permute-start(bf16[2,64,384]{2,1,0:T(8,128)(2,1)S(1)} %get-tuple-element.21), channel_id=1, source_target_pairs={{0,32},{32,64},{64,96},{96,128},{128,160},{160,192},{192,224},{224... | collective-permute-start | bytes 294920 | tf_op jit(solution)/shard_map/ppermute | solution.py:203
  14.6 1.3 %copy-start.2 = (bf16[4,2,64,384]{3,2,1,0:T(8,128)(2,1)S(1)}, bf16[4,2,64,384]{3,2,1,0:T(8,128)(2,1)}, u32[]{:S(2)}) copy-start(bf16[4,2,64,384]{3,2,1,0:T(8,128)(2,1)} %x_ref.1) | copy-start | bytes 1179652
  14.6 1.4 %copy-start.3 = (bf16[384,192]{0,1:T(8,128)(2,1)S(1)}, bf16[384,192]{0,1:T(8,128)(2,1)}, u32[]{:S(2)}) copy-start(bf16[384,192]{0,1:T(8,128)(2,1)} %param.16) | copy-start | bytes 442372
  14.6 1.4 %copy-start.4 = (f32[192]{0:T(256)S(1)}, f32[192]{0:T(256)}, u32[]{:S(2)}) copy-start(f32[192]{0:T(256)} %param.14) | copy-start | bytes 2308
  14.6 1.4 %copy-start.5 = (f32[192]{0:T(256)S(1)}, f32[192]{0:T(256)}, u32[]{:S(2)}) copy-start(f32[192]{0:T(256)} %param.17) | copy-start | bytes 2308
  15.8 6.2 %collective-permute-start.4 = (bf16[2,64,384]{2,1,0:T(8,128)(2,1)S(1)}, bf16[2,64,384]{2,1,0:T(8,128)(2,1)S(1)}, u32[]{:S(2)}, u32[]{:S(2)}) collective-permute-start(bf16[2,64,384]{2,1,0:T(8,128)(2,1)S(1)} %get-tuple-element.25), channel_id=1, source_target_pairs={{1,2},{2,1},{3,4},{4,3},{5,6},{6,5},{7,8},{8,7},{9,10},{10,9},{11,... | collective-permute-start | bytes 294920 | tf_op jit(solution)/shard_map/ppermute | solution.py:207
  16.8 6.2 %collective-permute-start.5 = (bf16[2,64,384]{2,1,0:T(8,128)(2,1)S(1)}, bf16[2,64,384]{2,1,0:T(8,128)(2,1)S(1)}, u32[]{:S(2)}, u32[]{:S(2)}) collective-permute-start(bf16[2,64,384]{2,1,0:T(8,128)(2,1)S(1)} %get-tuple-element.27), channel_id=1, source_target_pairs={{0,1},{1,0},{2,3},{3,2},{4,5},{5,4},{6,7},{7,6},{8,9},{9,8},{10,11... | collective-permute-start | bytes 294920 | tf_op jit(solution)/shard_map/ppermute | solution.py:211

commit v5 on v4

v5 whole, which is shorter than its diff:
```python
import jax
import jax.numpy as jnp
from jax import lax
from jax.experimental import pallas as pl
from jax.experimental.pallas import tpu as pltpu
from jax.sharding import PartitionSpec as P

F32 = jnp.float32
BF16 = jnp.bfloat16
COLS = 64
VMEM = pl.BlockSpec(memory_space=pltpu.VMEM)
HBM = pl.BlockSpec(memory_space=pltpu.HBM)


def call(body, outs, *args, flops=0, scratch=(), limit=8, in_hbm=()):
    args = [pltpu.with_memory_space_constraint(a, pltpu.HBM) if n in in_hbm else a for n, a in enumerate(args)]
    moved = sum(a.size * a.dtype.itemsize for a in args) + sum(o.size * o.dtype.itemsize for o in outs)
    return pl.pallas_call(
        body,
        out_shape=outs,
        in_specs=[HBM if n in in_hbm else VMEM for n in range(len(args))],
        out_specs=[VMEM] * len(outs),
        scratch_shapes=list(scratch),
        compiler_params=pltpu.CompilerParams(vmem_limit_bytes=limit << 20),
        cost_estimate=pl.CostEstimate(flops=flops // 10, bytes_accessed=moved // 10, transcendentals=0),
    )(*args)


def shape(dims, dtype=BF16):
    return jax.ShapeDtypeStruct(dims, dtype)


def act(values, gain):
    mean = jnp.mean(values * values, axis=-1, keepdims=True)
    scaled = values * lax.rsqrt(mean + 1e-06) * gain
    return scaled / (1.0 + jnp.exp(-scaled))


def taps(values):
    frames, _, channels = values.shape
    flat = values.reshape(frames * COLS, channels)
    col = lax.broadcasted_iota(jnp.int32, flat.shape, 0) % COLS
    left = jnp.where(col == 0, 0.0, pltpu.roll(flat, 1, 0))
    right = jnp.where(col == COLS - 1, 0.0, pltpu.roll(flat, frames * COLS - 1, 0))
    return jnp.concatenate([left, flat, right], axis=-1).astype(BF16).reshape(frames, COLS, 3 * channels)


def first_sums(parts, w_ref, acc_ref):
    for i, source, frames in parts:
        count = source.shape[1]
        a = source.reshape(2 * count * COLS, 1152)
        for j in range(3):
            w = jnp.concatenate([w_ref[i, j, k] for k in range(3)], axis=-1)
            out = lax.dot_general(a, w, (((1,), (1,)), ((), ())), preferred_element_type=F32)
            acc_ref[2 - j : 4 - j, frames] += out.reshape(2, count, COLS, 192)


def edge_rows(acc_ref, outer):
    odd = lax.axis_index("rows") % 2 == 1
    up = jnp.concatenate([acc_ref[0], acc_ref[1]], axis=-1)
    down = jnp.concatenate([acc_ref[2], acc_ref[3]], axis=-1)
    return jnp.where(odd, down if outer else up, up if outer else down).astype(BF16)


def outer_side():
    return lax.axis_index("rows") % 2


def second_act(own_ref, r_ref, bias_ref, gain_ref, side, outer, sa_ref):
    rows = lax.axis_index("rows")
    edge = jnp.logical_or(rows == 0, rows == lax.axis_size("rows") - 1)
    came = r_ref[...].astype(F32)
    if outer:
        came = jnp.where(edge, 0.0, came)
    for n in range(2):
        hidden = own_ref[2 * side + n] + came[..., 192 * n : 192 * n + 192] + bias_ref[...]
        second = act(hidden.astype(BF16).astype(F32), gain_ref[...])
        if outer:
            second = jnp.where(jnp.logical_and(edge, side == n), 0.0, second)
        sa_ref[n] = taps(second)


def second_sums(sa_ref, w_ref, side, parts, acc_ref):
    def dot(a, w):
        count = a.shape[0] * a.shape[1]
        out = jnp.dot(a.reshape(count * COLS, 576), w.reshape(576, 192), preferred_element_type=F32)
        return out.reshape(a.shape[0], a.shape[1], COLS, 192)

    for i, source, frames in parts:
        acc_ref[:, frames] += dot(sa_ref[:, source], w_ref[i, 2 * side])
        acc_ref[pl.ds(side, 1), frames] += dot(sa_ref[pl.ds(1 - side, 1), source], w_ref[i, 1])


def act_kernel(x_hbm, g_hbm, fa_ref, t_ref, x_ref, g_ref, gsem, sem):
    gain_load = pltpu.make_async_copy(g_hbm, g_ref, gsem)
    loads = [pltpu.make_async_copy(x_hbm.at[t], x_ref.at[t], sem.at[t]) for t in range(4)]
    for load in [gain_load] + loads:
        load.start()
    gain_load.wait()
    gain = g_ref[...].reshape(1, 384)
    for t in range(4):
        loads[t].wait()
        for row in range(2):
            value = act(x_ref[t, row].astype(F32), gain)
            fa_ref[row, t] = taps(value[None])[0]
            if t >= 2:
                t_ref[row, t - 2] = value.astype(BF16)


def early_kernel(fa_ref, w_ref, own_ref, a_ref, b_ref):
    own_ref[...] = jnp.zeros_like(own_ref)
    first_sums([(i, fa_ref[:, i : i + 2], slice(0, 2)) for i in range(3)], w_ref, own_ref)
    a_ref[...] = edge_rows(own_ref, False)
    b_ref[...] = edge_rows(own_ref, True)


def between_kernel(fa_ref, w_ref, part_ref):
    part_ref[...] = jnp.zeros_like(part_ref)
    parts = [(2, fa_ref[:, 0:2], slice(0, 2)), (1, fa_ref[:, 0:1], slice(1, 2))]
    first_sums(parts, w_ref, part_ref)


def late_kernel(t_ref, part_ref, w_ref, after_ref, own_ref, a_ref, b_ref, fa_ref):
    del after_ref
    first = lax.axis_index("tm") == 0
    for row in range(2):
        fa_ref[row] = taps(jnp.where(first, 0.0, t_ref[row].astype(F32)))
    own_ref[...] = part_ref[...]
    parts = [(0, fa_ref[...], slice(0, 2)), (1, fa_ref[:, 1:2], slice(0, 1))]
    first_sums(parts, w_ref, own_ref)
    a_ref[...] = edge_rows(own_ref, False)
    b_ref[...] = edge_rows(own_ref, True)


NEXT = [(0, slice(0, 2), slice(0, 2)), (1, slice(1, 2), slice(0, 1))]
REST = [(2, slice(0, 2), slice(2, 4)), (1, slice(0, 1), slice(3, 4))]
FIRST = [(i, slice(0, 2), slice(2 - i, 4 - i)) for i in range(3)]


def near_kernel(ra_ref, own_ref, bias_ref, gain_ref, w_ref, sa_ref, q_ref):
    side = 1 - outer_side()
    second_act(own_ref, ra_ref, bias_ref, gain_ref, side, False, sa_ref)
    q_ref[...] = jnp.zeros_like(q_ref)
    second_sums(sa_ref, w_ref, side, NEXT, q_ref)


def next_kernel(rb_ref, own_ref, part_ref, bias_ref, gain_ref, w_ref, sa_ref, q_ref, acc_ref):
    side = outer_side()
    second_act(own_ref, rb_ref, bias_ref, gain_ref, side, True, sa_ref)
    acc_ref[...] = part_ref[...]
    second_sums(sa_ref, w_ref, side, NEXT, acc_ref)
    q_ref[...] = jnp.concatenate([acc_ref[0], acc_ref[1]], axis=-1).astype(BF16)


def rest_kernel(near_ref, far_ref, w_ref, x_ref, sw_ref, bias_ref, sbias_ref, acc_ref):
    bias = bias_ref[...] + sbias_ref[...]
    for row in range(2):
        skip = lax.dot_general(
            x_ref[:, row].reshape(4 * COLS, 384), sw_ref[...], (((1,), (1,)), ((), ())), preferred_element_type=F32
        )
        acc_ref[row] = skip.reshape(4, COLS, 192) + bias
    second_sums(near_ref, w_ref, 1 - outer_side(), REST, acc_ref)
    second_sums(far_ref, w_ref, outer_side(), REST, acc_ref)


def second_near_kernel(ra_ref, own_ref, bias_ref, gain_ref, w_ref, rest_ref, acc_ref, sa_ref):
    side = 1 - outer_side()
    second_act(own_ref, ra_ref, bias_ref, gain_ref, side, False, sa_ref)
    acc_ref[...] = rest_ref[...]
    second_sums(sa_ref, w_ref, side, FIRST, acc_ref)


def second_kernel(q_ref, rb_ref, own_ref, part_ref, bias_ref, gain_ref, w_ref, out_ref, acc_ref, sa_ref):
    side = outer_side()
    second_act(own_ref, rb_ref, bias_ref, gain_ref, side, True, sa_ref)
    acc_ref[...] = part_ref[...]
    second_sums(sa_ref, w_ref, side, FIRST, acc_ref)
    came = jnp.where(lax.axis_index("tm") == 0, 0.0, q_ref[...].astype(F32))
    for row in range(2):
        out_ref[0:2, row] = (acc_ref[row, 0:2] + came[..., 192 * row : 192 * row + 192]).astype(BF16)
        out_ref[2:4, row] = acc_ref[row, 2:4].astype(BF16)


def swap_pairs(steps, count):
    inner = [(i, i ^ 1) for i in range(count)]
    outer = []
    for t in range(steps):
        base = t * count
        for i in range(1, count - 1, 2):
            outer += [(base + i, base + i + 1), (base + i + 1, base + i)]
        for i in (0, count - 1):
            outer.append((base + i, (t ^ 1) * count + i))
    return inner, outer


def per_device(x, w1, b1, g1, w2, b2, g2, sw, sb):
    steps = lax.axis_size("tm")
    inner, outer = swap_pairs(steps, lax.axis_size("rows"))
    ring = [(i, (i + 1) % steps) for i in range(steps)]
    w1 = jnp.swapaxes(w1, 3, 4)
    sw = jnp.swapaxes(sw, 0, 1)
    b1, b2, g2, sb = (v.reshape(1, -1) for v in (b1, b2, g2, sb))
    half = shape((2, 2, COLS, 576))
    sums, edges = shape((4, 2, COLS, 192), F32), shape((2, COLS, 384))

    fa, give = call(
        act_kernel, [shape((2, 4, COLS, 1152)), shape((2, 2, COLS, 384))], x, g1, flops=4 * 10**10, in_hbm=(0, 1),
        scratch=[
            pltpu.VMEM((4, 2, COLS, 384), BF16), pltpu.VMEM((384,), F32),
            pltpu.SemaphoreType.DMA(()), pltpu.SemaphoreType.DMA((4,)),
        ],
    )
    came = lax.ppermute(give, "tm", ring)
    own23, edge_a, edge_b = call(early_kernel, [sums, edges, edges], fa, w1, flops=10**9)
    b23 = lax.ppermute(edge_b, ("tm", "rows"), outer)
    a23 = lax.ppermute(edge_a, "rows", inner)
    part = call(between_kernel, [sums], fa, w1, flops=10**9)[0]
    near, part_q = call(near_kernel, [half, shape((2, 2, COLS, 192), F32)], a23, own23, b1, g2, w2, flops=10**9)
    far, give = call(
        next_kernel, [half, edges], b23, own23, part_q, b1, g2, w2, flops=10**9,
        scratch=[pltpu.VMEM((2, 2, COLS, 192), F32)],
    )
    q = lax.optimization_barrier(lax.ppermute(give, "tm", ring))
    own01, edge_a, edge_b = call(
        late_kernel, [sums, edges, edges], came, part, w1, far, flops=10**9,
        scratch=[pltpu.VMEM((2, 2, COLS, 1152), BF16)],
    )
    b01 = lax.ppermute(edge_b, ("tm", "rows"), outer)
    a01 = lax.ppermute(edge_a, "rows", inner)
    rest = call(rest_kernel, [shape((2, 4, COLS, 192), F32)], near, far, w2, x, sw, b2, sb, flops=10**9)[0]
    total = call(
        second_near_kernel, [shape((2, 4, COLS, 192), F32)], a01, own01, b1, g2, w2, rest, flops=10**9,
        scratch=[pltpu.VMEM((2, 2, COLS, 576), BF16)],
    )[0]
    return call(
        second_kernel, [shape((4, 2, COLS, 192))], q, b01, own01, total, b1, g2, w2, flops=10**9,
        scratch=[pltpu.VMEM((2, 4, COLS, 192), F32), pltpu.VMEM((2, 2, COLS, 576), BF16)],
    )[0]


def solution(mesh):
    return jax.shard_map(
        per_device,
        mesh=mesh,
        in_specs=(P("tm", "rows", None, None), P(), P(), P(), P(), P(), P(), P(), P()),
        out_specs=P("tm", "rows", None, None),
        check_vma=False,
    )
```

time: 25.8 us -> 24.9 us (0.965)
  the two profiles are of different devices: /device:TPU:132 before, /device:TPU:152 now
where the time goes in v5:
time: 24.9 us; the launch traced here: 24.8 us
  Pallas kernels  11.4 us (46%)
  waiting for transfers between devices  7.9 us (32%)
  starting transfers between devices  4.94 us (20%)
  local copies, waits for them, and re-layouts  0.45 us (2%)
    pallas_call x9, Pallas kernels, call(): pl.pallas_call(body, out_shape=outs, in_specs=[HBM if n in in_hbm else VM...  11.4 us
    ppermute x1, waiting for transfers between devices, per_device(): b23 = lax.ppermute(edge_b, ('tm', 'rows'), outer)  3.81 us
    ppermute x1, waiting for transfers between devices, per_device(): b01 = lax.ppermute(edge_b, ('tm', 'rows'), outer)  3.45 us
    ppermute x1, starting transfers between devices, per_device(): came = lax.ppermute(give, 'tm', ring)  2.76 us
    ppermute x1, starting transfers between devices, per_device(): q = lax.optimization_barrier(lax.ppermute(give, 'tm', ring))  1.65 us
    ppermute x1, waiting for transfers between devices, per_device(): q = lax.optimization_barrier(lax.ppermute(give, 'tm', ring))  0.63 us
  transfers between devices with their start and end apart: 6, of which 3 were waited for; matrix products, arithmetic and copies ran while one was open for 0% of the time, Pallas kernels for 31%

profile of v5, /device:TPU:152, one launch (start us, length us, event | category | flops | bytes accessed | tf_op | source)
XLA Modules:
  0.0 24.8 jit_solution(11038932030166268867)
XLA Ops:
  0.0 0.0 copy-start.1
  0.0 1.9 %shard_map.91 = (bf16[2,4,64,1152]{3,2,1,0:T(8,128)(2,1)S(1)}, bf16[2,2,64,384]{3,2,1,0:T(8,128)(2,1)S(1)}) custom-call(bf16[4,2,64,384]{3,2,1,0:T(8,128)(2,1)} %x_ref.1, f32[384]{0:T(512)} %g_hbm.1), custom_call_target="tpu_custom_call" | custom-call | flops 4000000000 | bytes 177100 | tf_op jit(solution)/shard_map/pallas_call | solution.py:18
  1.9 2.8 %collective-permute-start.3 = (bf16[2,2,64,384]{3,2,1,0:T(8,128)(2,1)S(1)}, bf16[2,2,64,384]{3,2,1,0:T(8,128)(2,1)S(1)}, u32[]{:S(2)}, u32[]{:S(2)}) collective-permute-start(bf16[2,2,64,384]{3,2,1,0:T(8,128)(2,1)S(1)} %get-tuple-element.23), channel_id=1, source_target_pairs={{0,32},{32,64},{64,96},{96,128},{128,160},{160,192},{192,224},{224... | collective-permute-start | bytes 589832 | tf_op jit(solution)/shard_map/ppermute | solution.py:213
  4.7 0.0 copy-done.1
  4.7 1.8 %shard_map.92 = (f32[4,2,64,192]{3,2,1,0:T(8,128)S(1)}, bf16[2,64,384]{2,1,0:T(8,128)(2,1)S(1)}, bf16[2,64,384]{2,1,0:T(8,128)(2,1)S(1)}) custom-call(bf16[2,4,64,1152]{3,2,1,0:T(8,128)(2,1)S(1)} %get-tuple-element.17.fa_ref, bf16[3,3,3,192,384]{4,3,2,1,0:T(8,128)(2,1)S(1)} %bitcast.6), custom_call_target="tpu_custom_call" | custom-call | flops 100000000 | bytes 575078 | tf_op jit(solution)/shard_map/pallas_call | solution.py:18
  6.5 0.1 collective-permute-start.1
  6.6 0.0 copy-start
  6.6 0.0 copy-start.4
  6.6 0.0 copy-start.5
  6.6 0.2 collective-permute-start
  6.9 1.1 %shard_map.95.part_ref = f32[4,2,64,192]{3,2,1,0:T(8,128)S(1)} custom-call(bf16[2,4,64,1152]{3,2,1,0:T(8,128)(2,1)S(1)} %get-tuple-element.17.fa_ref, bf16[3,3,3,192,384]{4,3,2,1,0:T(8,128)(2,1)S(1)} %bitcast.7), custom_call_target="tpu_custom_call" | custom-call | flops 100000000 | bytes 555417 | tf_op jit(solution)/shard_map/pallas_call | solution.py:18
  7.9 0.0 collective-permute-done.1.ra_ref
  8.0 0.4 %copy-done = bf16[3,3,3,192,192]{4,3,2,1,0:T(8,128)(2,1)S(1)} copy-done((bf16[3,3,3,192,192]{4,3,2,1,0:T(8,128)(2,1)S(1)}, bf16[3,3,3,192,192]{4,3,2,1,0:T(8,128)(2,1)}, u32[]{:S(2)}) %copy-start) | copy-done | bytes 1990680
  8.4 0.0 copy-done.4
  8.4 0.0 copy-done.5
  8.4 0.7 %shard_map.93 = (bf16[2,2,64,576]{3,2,1,0:T(8,128)(2,1)S(1)}, f32[2,2,64,192]{3,2,1,0:T(8,128)S(1)}) custom-call(bf16[2,64,384]{2,1,0:T(8,128)(2,1)S(1)} %collective-permute-done.1.ra_ref, f32[4,2,64,192]{3,2,1,0:T(8,128)S(1)} %get-tuple-element.19.own_ref, f32[1,192]{1,0:T(1,128)S(1)} %bitcast.10, f32[1,192]{1,0:T(1,128)S(1)} %bitcast.14, ...), custom_call_target="tpu_custom_call" | custom-call | flops 100000000 | bytes 297523 | tf_op jit(solution)/shard_map/pallas_call | solution.py:18
  9.1 3.8 %collective-permute-done.rb_ref = bf16[2,64,384]{2,1,0:T(8,128)(2,1)S(1)} collective-permute-done((bf16[2,64,384]{2,1,0:T(8,128)(2,1)S(1)}, bf16[2,64,384]{2,1,0:T(8,128)(2,1)S(1)}, u32[]{:S(2)}, u32[]{:S(2)}) %collective-permute-start) | collective-permute-done | bytes 98336 | tf_op jit(solution)/shard_map/ppermute | solution.py:215
  12.9 0.9 %shard_map.94 = (bf16[2,2,64,576]{3,2,1,0:T(8,128)(2,1)S(1)}, bf16[2,64,384]{2,1,0:T(8,128)(2,1)S(1)}) custom-call(bf16[2,64,384]{2,1,0:T(8,128)(2,1)S(1)} %collective-permute-done.rb_ref, f32[4,2,64,192]{3,2,1,0:T(8,128)S(1)} %get-tuple-element.19.own_ref, f32[2,2,64,192]{3,2,1,0:T(8,128)S(1)} %get-tuple-element.21.part_ref, f32[1,192]{1,0:T(1,128)S(1)} %bitcast.11, ...), custom_call_target="tpu_custom_call" | custom-call | flops 100000000 | bytes 307353 | tf_op jit(solution)/shard_map/pallas_call | solution.py:18
  13.7 0.0 copy-start.2
  13.8 0.0 copy-start.3
  13.8 0.0 copy-start.6
  13.8 0.0 copy-start.7
  13.8 1.6 %collective-permute-start.2 = (bf16[2,64,384]{2,1,0:T(8,128)(2,1)S(1)}, bf16[2,64,384]{2,1,0:T(8,128)(2,1)S(1)}, u32[]{:S(2)}, u32[]{:S(2)}) collective-permute-start(bf16[2,64,384]{2,1,0:T(8,128)(2,1)S(1)} %get-tuple-element.22), channel_id=1, source_target_pairs={{0,32},{32,64},{64,96},{96,128},{128,160},{160,192},{192,224},{224... | collective-permute-start | bytes 294920 | tf_op jit(solution)/shard_map/ppermute | solution.py:223
  15.4 0.0 collective-permute-done.3.t_ref
  15.4 1.2 %shard_map.96 = (f32[4,2,64,192]{3,2,1,0:T(8,128)S(1)}, bf16[2,64,384]{2,1,0:T(8,128)(2,1)S(1)}, bf16[2,64,384]{2,1,0:T(8,128)(2,1)S(1)}) custom-call(bf16[2,2,64,384]{3,2,1,0:T(8,128)(2,1)S(1)} %collective-permute-done.3.t_ref, f32[4,2,64,192]{3,2,1,0:T(8,128)S(1)} %shard_map.95.part_ref, bf16[3,3,3,192,384]{4,3,2,1,0:T(8,128)(2,1)S(1)} %bitcast.8, ...), custom_call_target="tpu_custom_call" | custom-call | flops 100000000 | bytes 545587 | tf_op jit(solution)/shard_map/pallas_call | solution.py:18
  16.7 0.1 collective-permute-start.5
  16.8 0.1 collective-permute-start.4
  16.9 0.0 copy-done.2
  16.9 0.0 copy-done.3
  16.9 0.0 copy-done.6
  16.9 0.0 copy-done.7
  16.9 0.9 %shard_map.97.rest_ref = f32[2,4,64,192]{3,2,1,0:T(8,128)S(1)} custom-call(bf16[2,2,64,576]{3,2,1,0:T(8,128)(2,1)S(1)} %get-tuple-element.28.near_ref, bf16[2,2,64,576]{3,2,1,0:T(8,128)(2,1)S(1)} %get-tuple-element.24.after_ref.far_ref, bf16[3,3,3,192,192]{4,3,2,1,0:T(8,128)(2,1)S(1)} %copy-done, bf16[4,2,64,384]{3,2,1,0:T(8,128)(2,1)S(1)} %copy-done.2, ...), custom_call_target="tpu_custom_call" | custom-call | flops 100000000 | bytes 351590 | tf_op jit(solution)/shard_map/pallas_call | solution.py:18
  17.9 0.6 %collective-permute-done.2.q_ref = bf16[2,64,384]{2,1,0:T(8,128)(2,1)S(1)} collective-permute-done((bf16[2,64,384]{2,1,0:T(8,128)(2,1)S(1)}, bf16[2,64,384]{2,1,0:T(8,128)(2,1)S(1)}, u32[]{:S(2)}, u32[]{:S(2)}) %collective-permute-start.2) | collective-permute-done | bytes 98336 | tf_op jit(solution)/shard_map/ppermute | solution.py:223
  18.5 0.0 collective-permute-done.5.ra_ref
  18.5 1.1 %shard_map.98.part_ref = f32[2,4,64,192]{3,2,1,0:T(8,128)S(1)} custom-call(bf16[2,64,384]{2,1,0:T(8,128)(2,1)S(1)} %collective-permute-done.5.ra_ref, f32[4,2,64,192]{3,2,1,0:T(8,128)S(1)} %get-tuple-element.26.own_ref, f32[1,192]{1,0:T(1,128)S(1)} %bitcast.12, f32[1,192]{1,0:T(1,128)S(1)} %bitcast.16, bf16[3,3,3,192,192]{4,3,2,1,0:T(8,128)(2,1)S(1)} %copy-done, ...), custom_call_target="tpu_custom_call" | custom-call | flops 100000000 | bytes 327014 | tf_op jit(solution)/shard_map/pallas_call | solution.py:18
  19.6 3.4 %collective-permute-done.4.rb_ref = bf16[2,64,384]{2,1,0:T(8,128)(2,1)S(1)} collective-permute-done((bf16[2,64,384]{2,1,0:T(8,128)(2,1)S(1)}, bf16[2,64,384]{2,1,0:T(8,128)(2,1)S(1)}, u32[]{:S(2)}, u32[]{:S(2)}) %collective-permute-start.4) | collective-permute-done | bytes 98336 | tf_op jit(solution)/shard_map/ppermute | solution.py:228
  23.0 1.8 %shard_map.99 = bf16[4,2,64,192]{3,2,1,0:T(8,128)(2,1)} custom-call(bf16[2,64,384]{2,1,0:T(8,128)(2,1)S(1)} %collective-permute-done.2.q_ref, bf16[2,64,384]{2,1,0:T(8,128)(2,1)S(1)} %collective-permute-done.4.rb_ref, f32[4,2,64,192]{3,2,1,0:T(8,128)S(1)} %get-tuple-element.26.own_ref, f32[2,4,64,192]{3,2,1,0:T(8,128)S(1)} %shard_map.98.part_ref, ...), custom_call_target="tpu_custom_call" | custom-call | flops 100000000 | bytes 317184 | tf_op jit(solution)/shard_map/pallas_call | solution.py:18
Async XLA Ops:
  0.0 4.7 %copy-start.1 = (bf16[3,3,3,384,192]{3,4,2,1,0:T(8,128)(2,1)S(1)}, bf16[3,3,3,384,192]{3,4,2,1,0:T(8,128)(2,1)}, u32[]{:S(2)}) copy-start(bf16[3,3,3,384,192]{3,4,2,1,0:T(8,128)(2,1)} %param.10) | copy-start | bytes 11943940
  1.9 13.5 %collective-permute-start.3 = (bf16[2,2,64,384]{3,2,1,0:T(8,128)(2,1)S(1)}, bf16[2,2,64,384]{3,2,1,0:T(8,128)(2,1)S(1)}, u32[]{:S(2)}, u32[]{:S(2)}) collective-permute-start(bf16[2,2,64,384]{3,2,1,0:T(8,128)(2,1)S(1)} %get-tuple-element.23), channel_id=1, source_target_pairs={{0,32},{32,64},{64,96},{96,128},{128,160},{160,192},{192,224},{224... | collective-permute-start | bytes 589832 | tf_op jit(solution)/shard_map/ppermute | solution.py:213
  6.5 1.4 %collective-permute-start.1 = (bf16[2,64,384]{2,1,0:T(8,128)(2,1)S(1)}, bf16[2,64,384]{2,1,0:T(8,128)(2,1)S(1)}, u32[]{:S(2)}, u32[]{:S(2)}) collective-permute-start(bf16[2,64,384]{2,1,0:T(8,128)(2,1)S(1)} %get-tuple-element.20), channel_id=1, source_target_pairs={{0,1},{1,0},{2,3},{3,2},{4,5},{5,4},{6,7},{7,6},{8,9},{9,8},{10,11... | collective-permute-start | bytes 294920 | tf_op jit(solution)/shard_map/ppermute | solution.py:216
  6.6 1.8 %copy-start = (bf16[3,3,3,192,192]{4,3,2,1,0:T(8,128)(2,1)S(1)}, bf16[3,3,3,192,192]{4,3,2,1,0:T(8,128)(2,1)}, u32[]{:S(2)}) copy-start(bf16[3,3,3,192,192]{4,3,2,1,0:T(8,128)(2,1)} %w_ref.9) | copy-start | bytes 5971972
  6.6 1.7 %copy-start.4 = (f32[192]{0:T(256)S(1)}, f32[192]{0:T(256)}, u32[]{:S(2)}) copy-start(f32[192]{0:T(256)} %param.11) | copy-start | bytes 2308
  6.6 1.7 %copy-start.5 = (f32[192]{0:T(256)S(1)}, f32[192]{0:T(256)}, u32[]{:S(2)}) copy-start(f32[192]{0:T(256)} %param.15) | copy-start | bytes 2308
  6.6 6.2 %collective-permute-start = (bf16[2,64,384]{2,1,0:T(8,128)(2,1)S(1)}, bf16[2,64,384]{2,1,0:T(8,128)(2,1)S(1)}, u32[]{:S(2)}, u32[]{:S(2)}) collective-permute-start(bf16[2,64,384]{2,1,0:T(8,128)(2,1)S(1)} %get-tuple-element.18), channel_id=1, source_target_pairs={{1,2},{2,1},{3,4},{4,3},{5,6},{6,5},{7,8},{8,7},{9,10},{10,9},{11,... | collective-permute-start | bytes 294920 | tf_op jit(solution)/shard_map/ppermute | solution.py:215
  13.7 3.2 %copy-start.2 = (bf16[4,2,64,384]{3,2,1,0:T(8,128)(2,1)S(1)}, bf16[4,2,64,384]{3,2,1,0:T(8,128)(2,1)}, u32[]{:S(2)}) copy-start(bf16[4,2,64,384]{3,2,1,0:T(8,128)(2,1)} %x_ref.1) | copy-start | bytes 1179652
  13.8 3.2 %copy-start.3 = (bf16[384,192]{0,1:T(8,128)(2,1)S(1)}, bf16[384,192]{0,1:T(8,128)(2,1)}, u32[]{:S(2)}) copy-start(bf16[384,192]{0,1:T(8,128)(2,1)} %param.16) | copy-start | bytes 442372
  13.8 3.1 %copy-start.6 = (f32[192]{0:T(256)S(1)}, f32[192]{0:T(256)}, u32[]{:S(2)}) copy-start(f32[192]{0:T(256)} %param.14) | copy-start | bytes 2308
  13.8 3.1 %copy-start.7 = (f32[192]{0:T(256)S(1)}, f32[192]{0:T(256)}, u32[]{:S(2)}) copy-start(f32[192]{0:T(256)} %param.17) | copy-start | bytes 2308
  13.8 4.7 %collective-permute-start.2 = (bf16[2,64,384]{2,1,0:T(8,128)(2,1)S(1)}, bf16[2,64,384]{2,1,0:T(8,128)(2,1)S(1)}, u32[]{:S(2)}, u32[]{:S(2)}) collective-permute-start(bf16[2,64,384]{2,1,0:T(8,128)(2,1)S(1)} %get-tuple-element.22), channel_id=1, source_target_pairs={{0,32},{32,64},{64,96},{96,128},{128,160},{160,192},{192,224},{224... | collective-permute-start | bytes 294920 | tf_op jit(solution)/shard_map/ppermute | solution.py:223
  16.7 1.8 %collective-permute-start.5 = (bf16[2,64,384]{2,1,0:T(8,128)(2,1)S(1)}, bf16[2,64,384]{2,1,0:T(8,128)(2,1)S(1)}, u32[]{:S(2)}, u32[]{:S(2)}) collective-permute-start(bf16[2,64,384]{2,1,0:T(8,128)(2,1)S(1)} %get-tuple-element.27), channel_id=1, source_target_pairs={{0,1},{1,0},{2,3},{3,2},{4,5},{5,4},{6,7},{7,6},{8,9},{9,8},{10,11... | collective-permute-start | bytes 294920 | tf_op jit(solution)/shard_map/ppermute | solution.py:229
  16.8 6.2 %collective-permute-start.4 = (bf16[2,64,384]{2,1,0:T(8,128)(2,1)S(1)}, bf16[2,64,384]{2,1,0:T(8,128)(2,1)S(1)}, u32[]{:S(2)}, u32[]{:S(2)}) collective-permute-start(bf16[2,64,384]{2,1,0:T(8,128)(2,1)S(1)} %get-tuple-element.25), channel_id=1, source_target_pairs={{1,2},{2,1},{3,4},{4,3},{5,6},{6,5},{7,8},{8,7},{9,10},{10,9},{11,... | collective-permute-start | bytes 294920 | tf_op jit(solution)/shard_map/ppermute | solution.py:228

commit v6 on v5

--- a/solution.py
+++ b/solution.py
@@ -33,7 +33,8 @@
 def act(values, gain):
     mean = jnp.mean(values * values, axis=-1, keepdims=True)
     scaled = values * lax.rsqrt(mean + 1e-06) * gain
-    return scaled / (1.0 + jnp.exp(-scaled))
+    half = 0.5 * scaled
+    return half + half * jnp.tanh(half)
 
 
 def taps(values):
@@ -45,14 +46,14 @@
     return jnp.concatenate([left, flat, right], axis=-1).astype(BF16).reshape(frames, COLS, 3 * channels)
 
 
-def first_sums(parts, w_ref, acc_ref):
-    for i, source, frames in parts:
-        count = source.shape[1]
-        a = source.reshape(2 * count * COLS, 1152)
-        for j in range(3):
-            w = jnp.concatenate([w_ref[i, j, k] for k in range(3)], axis=-1)
-            out = lax.dot_general(a, w, (((1,), (1,)), ((), ())), preferred_element_type=F32)
-            acc_ref[2 - j : 4 - j, frames] += out.reshape(2, count, COLS, 192)
+def first_sums(parts, w_ref):
+    a = jnp.concatenate([source.reshape(4 * COLS, 1152) for _, source in parts], axis=-1)
+    outs = []
+    for j in range(3):
+        w = jnp.concatenate([w_ref[i, j, k] for i, _ in parts for k in range(3)], axis=-1)
+        out = lax.dot_general(a, w, (((1,), (1,)), ((), ())), preferred_element_type=F32)
+        outs.append(out.reshape(2, 2, COLS, 192))
+    return outs[2][0], outs[2][1] + outs[1][0], outs[1][1] + outs[0][0], outs[0][1]
 
 
 def edge_rows(acc_ref, outer):
@@ -108,16 +109,17 @@
 
 
 def early_kernel(fa_ref, w_ref, own_ref, a_ref, b_ref):
-    own_ref[...] = jnp.zeros_like(own_ref)
-    first_sums([(i, fa_ref[:, i : i + 2], slice(0, 2)) for i in range(3)], w_ref, own_ref)
+    for row, total in enumerate(first_sums([(i, fa_ref[:, i : i + 2]) for i in range(3)], w_ref)):
+        own_ref[row] = total
     a_ref[...] = edge_rows(own_ref, False)
     b_ref[...] = edge_rows(own_ref, True)
 
 
 def between_kernel(fa_ref, w_ref, part_ref):
-    part_ref[...] = jnp.zeros_like(part_ref)
-    parts = [(2, fa_ref[:, 0:2], slice(0, 2)), (1, fa_ref[:, 0:1], slice(1, 2))]
-    first_sums(parts, w_ref, part_ref)
+    first = fa_ref[:, 0:1]
+    parts = [(2, fa_ref[:, 0:2]), (1, jnp.concatenate([jnp.zeros_like(first), first], axis=1))]
+    for row, total in enumerate(first_sums(parts, w_ref)):
+        part_ref[row] = total
 
 
 def late_kernel(t_ref, part_ref, w_ref, after_ref, own_ref, a_ref, b_ref, fa_ref):
@@ -125,9 +127,10 @@
     first = lax.axis_index("tm") == 0
     for row in range(2):
         fa_ref[row] = taps(jnp.where(first, 0.0, t_ref[row].astype(F32)))
-    own_ref[...] = part_ref[...]
-    parts = [(0, fa_ref[...], slice(0, 2)), (1, fa_ref[:, 1:2], slice(0, 1))]
-    first_sums(parts, w_ref, own_ref)
+    last = fa_ref[:, 1:2]
+    parts = [(0, fa_ref[...]), (1, jnp.concatenate([last, jnp.zeros_like(last)], axis=1))]
+    for row, total in enumerate(first_sums(parts, w_ref)):
+        own_ref[row] = part_ref[row] + total
     a_ref[...] = edge_rows(own_ref, False)
     b_ref[...] = edge_rows(own_ref, True)
 
@@ -214,20 +217,20 @@
     own23, edge_a, edge_b = call(early_kernel, [sums, edges, edges], fa, w1, flops=10**9)
     b23 = lax.ppermute(edge_b, ("tm", "rows"), outer)
     a23 = lax.ppermute(edge_a, "rows", inner)
-    part = call(between_kernel, [sums], fa, w1, flops=10**9)[0]
+    part = call(between_kernel, [sums], fa, w1, flops=16*10**9)[0]
     near, part_q = call(near_kernel, [half, shape((2, 2, COLS, 192), F32)], a23, own23, b1, g2, w2, flops=10**9)
     far, give = call(
         next_kernel, [half, edges], b23, own23, part_q, b1, g2, w2, flops=10**9,
         scratch=[pltpu.VMEM((2, 2, COLS, 192), F32)],
     )
-    q = lax.optimization_barrier(lax.ppermute(give, "tm", ring))
+    q = lax.ppermute(give, "tm", ring)
     own01, edge_a, edge_b = call(
         late_kernel, [sums, edges, edges], came, part, w1, far, flops=10**9,
         scratch=[pltpu.VMEM((2, 2, COLS, 1152), BF16)],
     )
     b01 = lax.ppermute(edge_b, ("tm", "rows"), outer)
     a01 = lax.ppermute(edge_a, "rows", inner)
-    rest = call(rest_kernel, [shape((2, 4, COLS, 192), F32)], near, far, w2, x, sw, b2, sb, flops=10**9)[0]
+    rest = call(rest_kernel, [shape((2, 4, COLS, 192), F32)], near, far, w2, x, sw, b2, sb, flops=16*10**9)[0]
     total = call(
         second_near_kernel, [shape((2, 4, COLS, 192), F32)], a01, own01, b1, g2, w2, rest, flops=10**9,
         scratch=[pltpu.VMEM((2, 2, COLS, 576), BF16)],

time: 24.9 us -> 24.5 us (0.984)
  the two profiles are of different devices: /device:TPU:152 before, /device:TPU:132 now
where the time goes in v6:
time: 24.5 us; the launch traced here: 24.4 us
  Pallas kernels  11.2 us (46%)
  waiting for transfers between devices  8.04 us (33%)
  starting transfers between devices  4.85 us (20%)
    pallas_call x9, Pallas kernels, call(): pl.pallas_call(body, out_shape=outs, in_specs=[HBM if n in in_hbm else VM...  11.2 us
    ppermute x1, waiting for transfers between devices, per_device(): q = lax.ppermute(give, 'tm', ring)  4.48 us
    ppermute x1, waiting for transfers between devices, per_device(): b23 = lax.ppermute(edge_b, ('tm', 'rows'), outer)  2.99 us
    ppermute x1, starting transfers between devices, per_device(): came = lax.ppermute(give, 'tm', ring)  1.65 us
    ppermute x1, starting transfers between devices, per_device(): q = lax.ppermute(give, 'tm', ring)  1.65 us
    ppermute x1, starting transfers between devices, per_device(): a23 = lax.ppermute(edge_a, 'rows', inner)  1.26 us
  transfers between devices with their start and end apart: 6, of which 4 were waited for; matrix products, arithmetic and copies ran while one was open for 0% of the time, Pallas kernels for 31%

profile of v6, /device:TPU:132, one launch (start us, length us, event | category | flops | bytes accessed | tf_op | source)
XLA Modules:
  0.0 24.4 jit_solution(3573931464629750753)
XLA Ops:
  0.0 0.0 copy-start.1
  0.0 1.8 %shard_map.91 = (bf16[2,4,64,1152]{3,2,1,0:T(8,128)(2,1)S(1)}, bf16[2,2,64,384]{3,2,1,0:T(8,128)(2,1)S(1)}) custom-call(bf16[4,2,64,384]{3,2,1,0:T(8,128)(2,1)} %x_ref.1, f32[384]{0:T(512)} %g_hbm.1), custom_call_target="tpu_custom_call" | custom-call | flops 4000000000 | bytes 177100 | tf_op jit(solution)/shard_map/pallas_call | solution.py:18
  1.8 1.7 %collective-permute-start.3 = (bf16[2,2,64,384]{3,2,1,0:T(8,128)(2,1)S(1)}, bf16[2,2,64,384]{3,2,1,0:T(8,128)(2,1)S(1)}, u32[]{:S(2)}, u32[]{:S(2)}) collective-permute-start(bf16[2,2,64,384]{3,2,1,0:T(8,128)(2,1)S(1)} %get-tuple-element.23), channel_id=1, source_target_pairs={{0,32},{32,64},{64,96},{96,128},{128,160},{160,192},{192,224},{224... | collective-permute-start | bytes 589832 | tf_op jit(solution)/shard_map/ppermute | solution.py:216
  3.5 0.0 copy-done.1
  3.5 1.7 %shard_map.92 = (f32[4,2,64,192]{3,2,1,0:T(8,128)S(1)}, bf16[2,64,384]{2,1,0:T(8,128)(2,1)S(1)}, bf16[2,64,384]{2,1,0:T(8,128)(2,1)S(1)}) custom-call(bf16[2,4,64,1152]{3,2,1,0:T(8,128)(2,1)S(1)} %get-tuple-element.17.fa_ref, bf16[3,3,3,192,384]{4,3,2,1,0:T(8,128)(2,1)S(1)} %bitcast.6), custom_call_target="tpu_custom_call" | custom-call | flops 100000000 | bytes 575078 | tf_op jit(solution)/shard_map/pallas_call | solution.py:18
  5.2 0.1 collective-permute-start
  5.3 0.0 copy-start
  5.3 0.0 copy-start.2
  5.4 0.0 copy-start.3
  5.4 1.3 %collective-permute-start.1 = (bf16[2,64,384]{2,1,0:T(8,128)(2,1)S(1)}, bf16[2,64,384]{2,1,0:T(8,128)(2,1)S(1)}, u32[]{:S(2)}, u32[]{:S(2)}) collective-permute-start(bf16[2,64,384]{2,1,0:T(8,128)(2,1)S(1)} %get-tuple-element.20), channel_id=1, source_target_pairs={{0,1},{1,0},{2,3},{3,2},{4,5},{5,4},{6,7},{7,6},{8,9},{9,8},{10,11... | collective-permute-start | bytes 294920 | tf_op jit(solution)/shard_map/ppermute | solution.py:219
  6.6 1.1 %shard_map.95.part_ref = f32[4,2,64,192]{3,2,1,0:T(8,128)S(1)} custom-call(bf16[2,4,64,1152]{3,2,1,0:T(8,128)(2,1)S(1)} %get-tuple-element.17.fa_ref, bf16[3,3,3,192,384]{4,3,2,1,0:T(8,128)(2,1)S(1)} %bitcast.7), custom_call_target="tpu_custom_call" | custom-call | flops 1600000000 | bytes 555417 | tf_op jit(solution)/shard_map/pallas_call | solution.py:18
  7.7 0.0 collective-permute-done.1.ra_ref
  7.7 0.0 copy-done
  7.7 0.0 copy-done.2
  7.8 0.0 copy-done.3
  7.8 0.7 %shard_map.93 = (bf16[2,2,64,576]{3,2,1,0:T(8,128)(2,1)S(1)}, f32[2,2,64,192]{3,2,1,0:T(8,128)S(1)}) custom-call(bf16[2,64,384]{2,1,0:T(8,128)(2,1)S(1)} %collective-permute-done.1.ra_ref, f32[4,2,64,192]{3,2,1,0:T(8,128)S(1)} %get-tuple-element.19.own_ref, f32[1,192]{1,0:T(1,128)S(1)} %bitcast.9, f32[1,192]{1,0:T(1,128)S(1)} %bitcast.13, ...), custom_call_target="tpu_custom_call" | custom-call | flops 100000000 | bytes 297523 | tf_op jit(solution)/shard_map/pallas_call | solution.py:18
  8.5 3.0 %collective-permute-done.rb_ref = bf16[2,64,384]{2,1,0:T(8,128)(2,1)S(1)} collective-permute-done((bf16[2,64,384]{2,1,0:T(8,128)(2,1)S(1)}, bf16[2,64,384]{2,1,0:T(8,128)(2,1)S(1)}, u32[]{:S(2)}, u32[]{:S(2)}) %collective-permute-start) | collective-permute-done | bytes 98336 | tf_op jit(solution)/shard_map/ppermute | solution.py:218
  11.5 0.9 %shard_map.94 = (bf16[2,2,64,576]{3,2,1,0:T(8,128)(2,1)S(1)}, bf16[2,64,384]{2,1,0:T(8,128)(2,1)S(1)}) custom-call(bf16[2,64,384]{2,1,0:T(8,128)(2,1)S(1)} %collective-permute-done.rb_ref, f32[4,2,64,192]{3,2,1,0:T(8,128)S(1)} %get-tuple-element.19.own_ref, f32[2,2,64,192]{3,2,1,0:T(8,128)S(1)} %get-tuple-element.21.part_ref, f32[1,192]{1,0:T(1,128)S(1)} %bitcast.10, ...), custom_call_target="tpu_custom_call" | custom-call | flops 100000000 | bytes 307353 | tf_op jit(solution)/shard_map/pallas_call | solution.py:18
  12.3 0.0 copy-start.4
  12.3 0.0 copy-start.5
  12.4 0.0 copy-start.6
  12.4 0.0 copy-start.7
  12.4 1.7 %collective-permute-start.2 = (bf16[2,64,384]{2,1,0:T(8,128)(2,1)S(1)}, bf16[2,64,384]{2,1,0:T(8,128)(2,1)S(1)}, u32[]{:S(2)}, u32[]{:S(2)}) collective-permute-start(bf16[2,64,384]{2,1,0:T(8,128)(2,1)S(1)} %get-tuple-element.22), channel_id=1, source_target_pairs={{0,32},{32,64},{64,96},{96,128},{128,160},{160,192},{192,224},{224... | collective-permute-start | bytes 294920 | tf_op jit(solution)/shard_map/ppermute | solution.py:226
  14.0 0.2 %collective-permute-done.3.t_ref = bf16[2,2,64,384]{3,2,1,0:T(8,128)(2,1)S(1)} collective-permute-done((bf16[2,2,64,384]{3,2,1,0:T(8,128)(2,1)S(1)}, bf16[2,2,64,384]{3,2,1,0:T(8,128)(2,1)S(1)}, u32[]{:S(2)}, u32[]{:S(2)}) %collective-permute-start.3) | collective-permute-done | bytes 196640 | tf_op jit(solution)/shard_map/ppermute | solution.py:216
  14.3 1.2 %shard_map.96 = (f32[4,2,64,192]{3,2,1,0:T(8,128)S(1)}, bf16[2,64,384]{2,1,0:T(8,128)(2,1)S(1)}, bf16[2,64,384]{2,1,0:T(8,128)(2,1)S(1)}) custom-call(bf16[2,2,64,384]{3,2,1,0:T(8,128)(2,1)S(1)} %collective-permute-done.3.t_ref, f32[4,2,64,192]{3,2,1,0:T(8,128)S(1)} %shard_map.95.part_ref, bf16[3,3,3,192,384]{4,3,2,1,0:T(8,128)(2,1)S(1)} %bitcast.8, ...), custom_call_target="tpu_custom_call" | custom-call | flops 100000000 | bytes 545587 | tf_op jit(solution)/shard_map/pallas_call | solution.py:18
  15.5 0.1 collective-permute-start.4
  15.6 0.1 collective-permute-start.5
  15.7 0.0 copy-done.4
  15.7 0.0 copy-done.5
  15.7 0.0 copy-done.6
  15.7 0.0 copy-done.7
  15.7 0.9 %shard_map.97.rest_ref = f32[2,4,64,192]{3,2,1,0:T(8,128)S(1)} custom-call(bf16[2,2,64,576]{3,2,1,0:T(8,128)(2,1)S(1)} %get-tuple-element.28.near_ref, bf16[2,2,64,576]{3,2,1,0:T(8,128)(2,1)S(1)} %get-tuple-element.24.after_ref.far_ref, bf16[3,3,3,192,192]{4,3,2,1,0:T(8,128)(2,1)S(1)} %copy-done, bf16[4,2,64,384]{3,2,1,0:T(8,128)(2,1)S(1)} %copy-done.4, ...), custom_call_target="tpu_custom_call" | custom-call | flops 1600000000 | bytes 351590 | tf_op jit(solution)/shard_map/pallas_call | solution.py:18
  16.7 0.3 %collective-permute-done.5.ra_ref = bf16[2,64,384]{2,1,0:T(8,128)(2,1)S(1)} collective-permute-done((bf16[2,64,384]{2,1,0:T(8,128)(2,1)S(1)}, bf16[2,64,384]{2,1,0:T(8,128)(2,1)S(1)}, u32[]{:S(2)}, u32[]{:S(2)}) %collective-permute-start.5) | collective-permute-done | bytes 98336 | tf_op jit(solution)/shard_map/ppermute | solution.py:232
  17.0 1.1 %shard_map.98.part_ref = f32[2,4,64,192]{3,2,1,0:T(8,128)S(1)} custom-call(bf16[2,64,384]{2,1,0:T(8,128)(2,1)S(1)} %collective-permute-done.5.ra_ref, f32[4,2,64,192]{3,2,1,0:T(8,128)S(1)} %get-tuple-element.26.own_ref, f32[1,192]{1,0:T(1,128)S(1)} %bitcast.11, f32[1,192]{1,0:T(1,128)S(1)} %bitcast.15, bf16[3,3,3,192,192]{4,3,2,1,0:T(8,128)(2,1)S(1)} %copy-done, ...), custom_call_target="tpu_custom_call" | custom-call | flops 100000000 | bytes 327014 | tf_op jit(solution)/shard_map/pallas_call | solution.py:18
  18.0 4.5 %collective-permute-done.2.q_ref = bf16[2,64,384]{2,1,0:T(8,128)(2,1)S(1)} collective-permute-done((bf16[2,64,384]{2,1,0:T(8,128)(2,1)S(1)}, bf16[2,64,384]{2,1,0:T(8,128)(2,1)S(1)}, u32[]{:S(2)}, u32[]{:S(2)}) %collective-permute-start.2) | collective-permute-done | bytes 98336 | tf_op jit(solution)/shard_map/ppermute | solution.py:226
  22.5 0.0 collective-permute-done.4.rb_ref
  22.5 1.8 %shard_map.99 = bf16[4,2,64,192]{3,2,1,0:T(8,128)(2,1)} custom-call(bf16[2,64,384]{2,1,0:T(8,128)(2,1)S(1)} %collective-permute-done.2.q_ref, bf16[2,64,384]{2,1,0:T(8,128)(2,1)S(1)} %collective-permute-done.4.rb_ref, f32[4,2,64,192]{3,2,1,0:T(8,128)S(1)} %get-tuple-element.26.own_ref, f32[2,4,64,192]{3,2,1,0:T(8,128)S(1)} %shard_map.98.part_ref, ...), custom_call_target="tpu_custom_call" | custom-call | flops 100000000 | bytes 317184 | tf_op jit(solution)/shard_map/pallas_call | solution.py:18
Async XLA Ops:
  0.0 3.5 %copy-start.1 = (bf16[3,3,3,384,192]{3,4,2,1,0:T(8,128)(2,1)S(1)}, bf16[3,3,3,384,192]{3,4,2,1,0:T(8,128)(2,1)}, u32[]{:S(2)}) copy-start(bf16[3,3,3,384,192]{3,4,2,1,0:T(8,128)(2,1)} %param.10) | copy-start | bytes 11943940
  1.8 12.4 %collective-permute-start.3 = (bf16[2,2,64,384]{3,2,1,0:T(8,128)(2,1)S(1)}, bf16[2,2,64,384]{3,2,1,0:T(8,128)(2,1)S(1)}, u32[]{:S(2)}, u32[]{:S(2)}) collective-permute-start(bf16[2,2,64,384]{3,2,1,0:T(8,128)(2,1)S(1)} %get-tuple-element.23), channel_id=1, source_target_pairs={{0,32},{32,64},{64,96},{96,128},{128,160},{160,192},{192,224},{224... | collective-permute-start | bytes 589832 | tf_op jit(solution)/shard_map/ppermute | solution.py:216
  5.2 6.2 %collective-permute-start = (bf16[2,64,384]{2,1,0:T(8,128)(2,1)S(1)}, bf16[2,64,384]{2,1,0:T(8,128)(2,1)S(1)}, u32[]{:S(2)}, u32[]{:S(2)}) collective-permute-start(bf16[2,64,384]{2,1,0:T(8,128)(2,1)S(1)} %get-tuple-element.18), channel_id=1, source_target_pairs={{1,2},{2,1},{3,4},{4,3},{5,6},{6,5},{7,8},{8,7},{9,10},{10,9},{11,... | collective-permute-start | bytes 294920 | tf_op jit(solution)/shard_map/ppermute | solution.py:218
  5.3 2.4 %copy-start = (bf16[3,3,3,192,192]{4,3,2,1,0:T(8,128)(2,1)S(1)}, bf16[3,3,3,192,192]{4,3,2,1,0:T(8,128)(2,1)}, u32[]{:S(2)}) copy-start(bf16[3,3,3,192,192]{4,3,2,1,0:T(8,128)(2,1)} %w_ref.9) | copy-start | bytes 5971972
  5.3 2.4 %copy-start.2 = (f32[192]{0:T(256)S(1)}, f32[192]{0:T(256)}, u32[]{:S(2)}) copy-start(f32[192]{0:T(256)} %param.11) | copy-start | bytes 2308
  5.4 2.4 %copy-start.3 = (f32[192]{0:T(256)S(1)}, f32[192]{0:T(256)}, u32[]{:S(2)}) copy-start(f32[192]{0:T(256)} %param.15) | copy-start | bytes 2308
  5.4 2.4 %collective-permute-start.1 = (bf16[2,64,384]{2,1,0:T(8,128)(2,1)S(1)}, bf16[2,64,384]{2,1,0:T(8,128)(2,1)S(1)}, u32[]{:S(2)}, u32[]{:S(2)}) collective-permute-start(bf16[2,64,384]{2,1,0:T(8,128)(2,1)S(1)} %get-tuple-element.20), channel_id=1, source_target_pairs={{0,1},{1,0},{2,3},{3,2},{4,5},{5,4},{6,7},{7,6},{8,9},{9,8},{10,11... | collective-permute-start | bytes 294920 | tf_op jit(solution)/shard_map/ppermute | solution.py:219
  12.3 3.4 %copy-start.4 = (bf16[4,2,64,384]{3,2,1,0:T(8,128)(2,1)S(1)}, bf16[4,2,64,384]{3,2,1,0:T(8,128)(2,1)}, u32[]{:S(2)}) copy-start(bf16[4,2,64,384]{3,2,1,0:T(8,128)(2,1)} %x_ref.1) | copy-start | bytes 1179652
  12.3 3.4 %copy-start.5 = (bf16[384,192]{0,1:T(8,128)(2,1)S(1)}, bf16[384,192]{0,1:T(8,128)(2,1)}, u32[]{:S(2)}) copy-start(bf16[384,192]{0,1:T(8,128)(2,1)} %param.16) | copy-start | bytes 442372
  12.4 3.4 %copy-start.6 = (f32[192]{0:T(256)S(1)}, f32[192]{0:T(256)}, u32[]{:S(2)}) copy-start(f32[192]{0:T(256)} %param.14) | copy-start | bytes 2308
  12.4 3.4 %copy-start.7 = (f32[192]{0:T(256)S(1)}, f32[192]{0:T(256)}, u32[]{:S(2)}) copy-start(f32[192]{0:T(256)} %param.17) | copy-start | bytes 2308
  12.4 10.1 %collective-permute-start.2 = (bf16[2,64,384]{2,1,0:T(8,128)(2,1)S(1)}, bf16[2,64,384]{2,1,0:T(8,128)(2,1)S(1)}, u32[]{:S(2)}, u32[]{:S(2)}) collective-permute-start(bf16[2,64,384]{2,1,0:T(8,128)(2,1)S(1)} %get-tuple-element.22), channel_id=1, source_target_pairs={{0,32},{32,64},{64,96},{96,128},{128,160},{160,192},{192,224},{224... | collective-permute-start | bytes 294920 | tf_op jit(solution)/shard_map/ppermute | solution.py:226
  15.5 7.0 %collective-permute-start.4 = (bf16[2,64,384]{2,1,0:T(8,128)(2,1)S(1)}, bf16[2,64,384]{2,1,0:T(8,128)(2,1)S(1)}, u32[]{:S(2)}, u32[]{:S(2)}) collective-permute-start(bf16[2,64,384]{2,1,0:T(8,128)(2,1)S(1)} %get-tuple-element.25), channel_id=1, source_target_pairs={{1,2},{2,1},{3,4},{4,3},{5,6},{6,5},{7,8},{8,7},{9,10},{10,9},{11,... | collective-permute-start | bytes 294920 | tf_op jit(solution)/shard_map/ppermute | solution.py:231
  15.6 1.4 %collective-permute-start.5 = (bf16[2,64,384]{2,1,0:T(8,128)(2,1)S(1)}, bf16[2,64,384]{2,1,0:T(8,128)(2,1)S(1)}, u32[]{:S(2)}, u32[]{:S(2)}) collective-permute-start(bf16[2,64,384]{2,1,0:T(8,128)(2,1)S(1)} %get-tuple-element.27), channel_id=1, source_target_pairs={{0,1},{1,0},{2,3},{3,2},{4,5},{5,4},{6,7},{7,6},{8,9},{9,8},{10,11... | collective-permute-start | bytes 294920 | tf_op jit(solution)/shard_map/ppermute | solution.py:232

commit v7 on v6

--- a/solution.py
+++ b/solution.py
@@ -46,21 +46,15 @@
     return jnp.concatenate([left, flat, right], axis=-1).astype(BF16).reshape(frames, COLS, 3 * channels)
 
 
-def first_sums(parts, w_ref):
+def first_dot(parts, w_ref, j):
     a = jnp.concatenate([source.reshape(4 * COLS, 1152) for _, source in parts], axis=-1)
-    outs = []
-    for j in range(3):
-        w = jnp.concatenate([w_ref[i, j, k] for i, _ in parts for k in range(3)], axis=-1)
-        out = lax.dot_general(a, w, (((1,), (1,)), ((), ())), preferred_element_type=F32)
-        outs.append(out.reshape(2, 2, COLS, 192))
-    return outs[2][0], outs[2][1] + outs[1][0], outs[1][1] + outs[0][0], outs[0][1]
-
-
-def edge_rows(acc_ref, outer):
-    odd = lax.axis_index("rows") % 2 == 1
-    up = jnp.concatenate([acc_ref[0], acc_ref[1]], axis=-1)
-    down = jnp.concatenate([acc_ref[2], acc_ref[3]], axis=-1)
-    return jnp.where(odd, down if outer else up, up if outer else down).astype(BF16)
+    w = jnp.concatenate([w_ref[i, j, k] for i, _ in parts for k in range(3)], axis=-1)
+    out = lax.dot_general(a, w, (((1,), (1,)), ((), ())), preferred_element_type=F32)
+    return out.reshape(2, 2, COLS, 192)
+
+
+def edge_rows(acc_ref):
+    return jnp.concatenate([acc_ref[0], acc_ref[1]], axis=-1).astype(BF16)
 
 
 def outer_side():
@@ -74,7 +68,7 @@
     if outer:
         came = jnp.where(edge, 0.0, came)
     for n in range(2):
-        hidden = own_ref[2 * side + n] + came[..., 192 * n : 192 * n + 192] + bias_ref[...]
+        hidden = own_ref[n] + came[..., 192 * n : 192 * n + 192] + bias_ref[...]
         second = act(hidden.astype(BF16).astype(F32), gain_ref[...])
         if outer:
             second = jnp.where(jnp.logical_and(edge, side == n), 0.0, second)
@@ -108,31 +102,48 @@
                 t_ref[row, t - 2] = value.astype(BF16)
 
 
-def early_kernel(fa_ref, w_ref, own_ref, a_ref, b_ref):
-    for row, total in enumerate(first_sums([(i, fa_ref[:, i : i + 2]) for i in range(3)], w_ref)):
-        own_ref[row] = total
-    a_ref[...] = edge_rows(own_ref, False)
-    b_ref[...] = edge_rows(own_ref, True)
+def early_kernel(fa_ref, w_ref, far_ref, near_ref, a_ref, b_ref, mid_ref):
+    side = outer_side()
+    parts = [(i, fa_ref[:, i : i + 2]) for i in range(3)]
+    far_ref[...] = first_dot(parts, w_ref, 2 - 2 * side)
+    mid_ref[...] = first_dot(parts, w_ref, 1)
+    near_ref[...] = first_dot(parts, w_ref, 2 * side)
+    far_ref[pl.ds(1 - side, 1)] += mid_ref[pl.ds(side, 1)]
+    near_ref[pl.ds(side, 1)] += mid_ref[pl.ds(1 - side, 1)]
+    a_ref[...] = edge_rows(near_ref)
+    b_ref[...] = edge_rows(far_ref)
 
 
 def between_kernel(fa_ref, w_ref, part_ref):
+    side = outer_side()
     first = fa_ref[:, 0:1]
     parts = [(2, fa_ref[:, 0:2]), (1, jnp.concatenate([jnp.zeros_like(first), first], axis=1))]
-    for row, total in enumerate(first_sums(parts, w_ref)):
-        part_ref[row] = total
-
-
-def late_kernel(t_ref, part_ref, w_ref, after_ref, own_ref, a_ref, b_ref, fa_ref):
+    for n, j in enumerate((2 - 2 * side, 1, 2 * side)):
+        part_ref[n] = first_dot(parts, w_ref, j)
+
+
+def before(fa_ref):
+    last = fa_ref[:, 1:2]
+    return [(0, fa_ref[...]), (1, jnp.concatenate([last, jnp.zeros_like(last)], axis=1))]
+
+
+def late_kernel(t_ref, part_ref, w_ref, after_ref, fa_ref, far_ref, mid_ref, b_ref):
     del after_ref
     first = lax.axis_index("tm") == 0
+    side = outer_side()
     for row in range(2):
         fa_ref[row] = taps(jnp.where(first, 0.0, t_ref[row].astype(F32)))
-    last = fa_ref[:, 1:2]
-    parts = [(0, fa_ref[...]), (1, jnp.concatenate([last, jnp.zeros_like(last)], axis=1))]
-    for row, total in enumerate(first_sums(parts, w_ref)):
-        own_ref[row] = part_ref[row] + total
-    a_ref[...] = edge_rows(own_ref, False)
-    b_ref[...] = edge_rows(own_ref, True)
+    far_ref[...] = part_ref[0] + first_dot(before(fa_ref), w_ref, 2 - 2 * side)
+    mid_ref[...] = part_ref[1] + first_dot(before(fa_ref), w_ref, 1)
+    far_ref[pl.ds(1 - side, 1)] += mid_ref[pl.ds(side, 1)]
+    b_ref[...] = edge_rows(far_ref)
+
+
+def inner_kernel(fa_ref, mid_ref, part_ref, w_ref, near_ref, a_ref):
+    side = outer_side()
+    near_ref[...] = part_ref[2] + first_dot(before(fa_ref), w_ref, 2 * side)
+    near_ref[pl.ds(side, 1)] += mid_ref[pl.ds(1 - side, 1)]
+    a_ref[...] = edge_rows(near_ref)
 
 
 NEXT = [(0, slice(0, 2), slice(0, 2)), (1, slice(1, 2), slice(0, 1))]
@@ -204,7 +215,7 @@
     sw = jnp.swapaxes(sw, 0, 1)
     b1, b2, g2, sb = (v.reshape(1, -1) for v in (b1, b2, g2, sb))
     half = shape((2, 2, COLS, 576))
-    sums, edges = shape((4, 2, COLS, 192), F32), shape((2, COLS, 384))
+    sums, edges = shape((2, 2, COLS, 192), F32), shape((2, COLS, 384))
 
     fa, give = call(
         act_kernel, [shape((2, 4, COLS, 1152)), shape((2, 2, COLS, 384))], x, g1, flops=4 * 10**10, in_hbm=(0, 1),
@@ -214,29 +225,31 @@
         ],
     )
     came = lax.ppermute(give, "tm", ring)
-    own23, edge_a, edge_b = call(early_kernel, [sums, edges, edges], fa, w1, flops=10**9)
+    far23, near23, edge_a, edge_b = call(
+        early_kernel, [sums, sums, edges, edges], fa, w1, flops=10**9, scratch=[pltpu.VMEM((2, 2, COLS, 192), F32)]
+    )
     b23 = lax.ppermute(edge_b, ("tm", "rows"), outer)
     a23 = lax.ppermute(edge_a, "rows", inner)
-    part = call(between_kernel, [sums], fa, w1, flops=16*10**9)[0]
-    near, part_q = call(near_kernel, [half, shape((2, 2, COLS, 192), F32)], a23, own23, b1, g2, w2, flops=10**9)
+    part = call(between_kernel, [shape((3, 2, 2, COLS, 192), F32)], fa, w1, flops=16 * 10**9)[0]
+    near, part_q = call(near_kernel, [half, shape((2, 2, COLS, 192), F32)], a23, near23, b1, g2, w2, flops=10**9)
     far, give = call(
-        next_kernel, [half, edges], b23, own23, part_q, b1, g2, w2, flops=10**9,
+        next_kernel, [half, edges], b23, far23, part_q, b1, g2, w2, flops=10**9,
         scratch=[pltpu.VMEM((2, 2, COLS, 192), F32)],
     )
     q = lax.ppermute(give, "tm", ring)
-    own01, edge_a, edge_b = call(
-        late_kernel, [sums, edges, edges], came, part, w1, far, flops=10**9,
-        scratch=[pltpu.VMEM((2, 2, COLS, 1152), BF16)],
-    )
-    b01 = lax.ppermute(edge_b, ("tm", "rows"), outer)
-    a01 = lax.ppermute(edge_a, "rows", inner)
+    frames, far01, mid, edge = call(
+        late_kernel, [shape((2, 2, COLS, 1152)), sums, sums, edges], came, part, w1, far, flops=10**9
+    )
+    b01 = lax.ppermute(edge, ("tm", "rows"), outer)
+    near01, edge = call(inner_kernel, [sums, edges], frames, mid, part, w1, flops=10**9)
+    a01 = lax.ppermute(edge, "rows", inner)
     rest = call(rest_kernel, [shape((2, 4, COLS, 192), F32)], near, far, w2, x, sw, b2, sb, flops=16*10**9)[0]
     total = call(
-        second_near_kernel, [shape((2, 4, COLS, 192), F32)], a01, own01, b1, g2, w2, rest, flops=10**9,
+        second_near_kernel, [shape((2, 4, COLS, 192), F32)], a01, near01, b1, g2, w2, rest, flops=10**9,
         scratch=[pltpu.VMEM((2, 2, COLS, 576), BF16)],
     )[0]
     return call(
-        second_kernel, [shape((4, 2, COLS, 192))], q, b01, own01, total, b1, g2, w2, flops=10**9,
+        second_kernel, [shape((4, 2, COLS, 192))], q, b01, far01, total, b1, g2, w2, flops=10**9,
         scratch=[pltpu.VMEM((2, 4, COLS, 192), F32), pltpu.VMEM((2, 2, COLS, 576), BF16)],
     )[0]
 

time: 24.5 us -> 24.7 us (level)
  Pallas kernels: 11.2 us -> 11.7 us
  waiting for transfers between devices: 8.04 us -> 7.66 us
    pallas_call x9 -> x10, Pallas kernels: 11.2 us -> 11.7 us  [call(): pl.pallas_call(body, out_shape=outs, in_specs=[HBM if n in in_hbm else VM...]
  transfers between devices with their start and end apart: 6 -> 6, of which waited for: 4 -> 4; matrix products, arithmetic and copies ran while one was open for 0% -> 0% of each run, Pallas kernels for 31% -> 33%
where the time goes in v7:
time: 24.7 us; the launch traced here: 24.6 us
  Pallas kernels  11.7 us (47%)
  waiting for transfers between devices  7.66 us (31%)
  starting transfers between devices  4.85 us (20%)
    pallas_call x10, Pallas kernels, call(): pl.pallas_call(body, out_shape=outs, in_specs=[HBM if n in in_hbm else VM...  11.7 us
    ppermute x1, waiting for transfers between devices, per_device(): q = lax.ppermute(give, 'tm', ring)  4.25 us
    ppermute x1, waiting for transfers between devices, per_device(): b23 = lax.ppermute(edge_b, ('tm', 'rows'), outer)  2.99 us
    ppermute x1, starting transfers between devices, per_device(): came = lax.ppermute(give, 'tm', ring)  1.65 us
    ppermute x1, starting transfers between devices, per_device(): q = lax.ppermute(give, 'tm', ring)  1.65 us
    ppermute x1, starting transfers between devices, per_device(): a23 = lax.ppermute(edge_a, 'rows', inner)  1.27 us
  transfers between devices with their start and end apart: 6, of which 4 were waited for; matrix products, arithmetic and copies ran while one was open for 0% of the time, Pallas kernels for 33%

profile of v7, /device:TPU:132, one launch (start us, length us, event | category | flops | bytes accessed | tf_op | source)
XLA Modules:
  0.0 24.6 jit_solution(26757589079027863)
XLA Ops:
  0.0 0.0 copy-start
  0.0 1.8 %shard_map.91 = (bf16[2,4,64,1152]{3,2,1,0:T(8,128)(2,1)S(1)}, bf16[2,2,64,384]{3,2,1,0:T(8,128)(2,1)S(1)}) custom-call(bf16[4,2,64,384]{3,2,1,0:T(8,128)(2,1)} %x_ref.1, f32[384]{0:T(512)} %g_hbm.1), custom_call_target="tpu_custom_call" | custom-call | flops 4000000000 | bytes 177100 | tf_op jit(solution)/shard_map/pallas_call | solution.py:18
  1.8 1.7 %collective-permute-start.3 = (bf16[2,2,64,384]{3,2,1,0:T(8,128)(2,1)S(1)}, bf16[2,2,64,384]{3,2,1,0:T(8,128)(2,1)S(1)}, u32[]{:S(2)}, u32[]{:S(2)}) collective-permute-start(bf16[2,2,64,384]{3,2,1,0:T(8,128)(2,1)S(1)} %get-tuple-element.28), channel_id=1, source_target_pairs={{0,32},{32,64},{64,96},{96,128},{128,160},{160,192},{192,224},{224... | collective-permute-start | bytes 589832 | tf_op jit(solution)/shard_map/ppermute | solution.py:227
  3.5 0.0 copy-done
  3.5 1.8 %shard_map.92 = (f32[2,2,64,192]{3,2,1,0:T(8,128)S(1)}, f32[2,2,64,192]{3,2,1,0:T(8,128)S(1)}, bf16[2,64,384]{2,1,0:T(8,128)(2,1)S(1)}, bf16[2,64,384]{2,1,0:T(8,128)(2,1)S(1)}) custom-call(bf16[2,4,64,1152]{3,2,1,0:T(8,128)(2,1)S(1)} %get-tuple-element.21.fa_ref, bf16[3,3,3,192,384]{4,3,2,1,0:T(8,128)(2,1)S(1)} %bitcast.6), custom_call_target="tpu_custom_call" | custom-call | flops 100000000 | bytes 575078 | tf_op jit(solution)/shard_map/pallas_call | solution.py:18
  5.3 0.1 collective-permute-start
  5.4 0.0 copy-start.1
  5.4 0.0 copy-start.2
  5.4 0.0 copy-start.3
  5.4 1.3 %collective-permute-start.1 = (bf16[2,64,384]{2,1,0:T(8,128)(2,1)S(1)}, bf16[2,64,384]{2,1,0:T(8,128)(2,1)S(1)}, u32[]{:S(2)}, u32[]{:S(2)}) collective-permute-start(bf16[2,64,384]{2,1,0:T(8,128)(2,1)S(1)} %get-tuple-element.24), channel_id=1, source_target_pairs={{0,1},{1,0},{2,3},{3,2},{4,5},{5,4},{6,7},{7,6},{8,9},{9,8},{10,11... | collective-permute-start | bytes 294920 | tf_op jit(solution)/shard_map/ppermute | solution.py:232
  6.7 1.1 %shard_map.95.part_ref = f32[3,2,2,64,192]{4,3,2,1,0:T(8,128)S(1)} custom-call(bf16[2,4,64,1152]{3,2,1,0:T(8,128)(2,1)S(1)} %get-tuple-element.21.fa_ref, bf16[3,3,3,192,384]{4,3,2,1,0:T(8,128)(2,1)S(1)} %bitcast.7), custom_call_target="tpu_custom_call" | custom-call | flops 1600000000 | bytes 575078 | tf_op jit(solution)/shard_map/pallas_call | solution.py:18
  7.8 0.0 collective-permute-done.1.ra_ref
  7.8 0.0 copy-done.1
  7.8 0.0 copy-done.2
  7.8 0.0 copy-done.3
  7.8 0.7 %shard_map.93 = (bf16[2,2,64,576]{3,2,1,0:T(8,128)(2,1)S(1)}, f32[2,2,64,192]{3,2,1,0:T(8,128)S(1)}) custom-call(bf16[2,64,384]{2,1,0:T(8,128)(2,1)S(1)} %collective-permute-done.1.ra_ref, f32[2,2,64,192]{3,2,1,0:T(8,128)S(1)} %get-tuple-element.25.own_ref, f32[1,192]{1,0:T(1,128)S(1)} %bitcast.10, f32[1,192]{1,0:T(1,128)S(1)} %bitcast.14, ...), custom_call_target="tpu_custom_call" | custom-call | flops 100000000 | bytes 277862 | tf_op jit(solution)/shard_map/pallas_call | solution.py:18
  8.5 3.0 %collective-permute-done.rb_ref = bf16[2,64,384]{2,1,0:T(8,128)(2,1)S(1)} collective-permute-done((bf16[2,64,384]{2,1,0:T(8,128)(2,1)S(1)}, bf16[2,64,384]{2,1,0:T(8,128)(2,1)S(1)}, u32[]{:S(2)}, u32[]{:S(2)}) %collective-permute-start) | collective-permute-done | bytes 98336 | tf_op jit(solution)/shard_map/ppermute | solution.py:231
  11.5 0.9 %shard_map.94 = (bf16[2,2,64,576]{3,2,1,0:T(8,128)(2,1)S(1)}, bf16[2,64,384]{2,1,0:T(8,128)(2,1)S(1)}) custom-call(bf16[2,64,384]{2,1,0:T(8,128)(2,1)S(1)} %collective-permute-done.rb_ref, f32[2,2,64,192]{3,2,1,0:T(8,128)S(1)} %get-tuple-element.23.own_ref, f32[2,2,64,192]{3,2,1,0:T(8,128)S(1)} %get-tuple-element.26.part_ref, f32[1,192]{1,0:T(1,128)S(1)} %bitcast.11, ...), custom_call_target="tpu_custom_call" | custom-call | flops 100000000 | bytes 287692 | tf_op jit(solution)/shard_map/pallas_call | solution.py:18
  12.4 1.7 %collective-permute-start.2 = (bf16[2,64,384]{2,1,0:T(8,128)(2,1)S(1)}, bf16[2,64,384]{2,1,0:T(8,128)(2,1)S(1)}, u32[]{:S(2)}, u32[]{:S(2)}) collective-permute-start(bf16[2,64,384]{2,1,0:T(8,128)(2,1)S(1)} %get-tuple-element.27), channel_id=1, source_target_pairs={{0,32},{32,64},{64,96},{96,128},{128,160},{160,192},{192,224},{224... | collective-permute-start | bytes 294920 | tf_op jit(solution)/shard_map/ppermute | solution.py:239
  14.0 0.3 %collective-permute-done.3.t_ref = bf16[2,2,64,384]{3,2,1,0:T(8,128)(2,1)S(1)} collective-permute-done((bf16[2,2,64,384]{3,2,1,0:T(8,128)(2,1)S(1)}, bf16[2,2,64,384]{3,2,1,0:T(8,128)(2,1)S(1)}, u32[]{:S(2)}, u32[]{:S(2)}) %collective-permute-start.3) | collective-permute-done | bytes 196640 | tf_op jit(solution)/shard_map/ppermute | solution.py:227
  14.3 1.0 %shard_map.96 = (bf16[2,2,64,1152]{3,2,1,0:T(8,128)(2,1)S(1)}, f32[2,2,64,192]{3,2,1,0:T(8,128)S(1)}, f32[2,2,64,192]{3,2,1,0:T(8,128)S(1)}, bf16[2,64,384]{2,1,0:T(8,128)(2,1)S(1)}) custom-call(bf16[2,2,64,384]{3,2,1,0:T(8,128)(2,1)S(1)} %collective-permute-done.3.t_ref, f32[3,2,2,64,192]{4,3,2,1,0:T(8,128)S(1)} %shard_map.95.part_ref, ...), custom_call_target="tpu_custom_call" | custom-call | flops 100000000 | bytes 614400 | tf_op jit(solution)/shard_map/pallas_call | solution.py:18
  15.2 0.1 collective-permute-start.4
  15.3 0.0 copy-start.4
  15.4 0.0 copy-start.5
  15.4 0.0 copy-start.6
  15.4 0.0 copy-start.7
  15.4 0.7 %shard_map.97 = (f32[2,2,64,192]{3,2,1,0:T(8,128)S(1)}, bf16[2,64,384]{2,1,0:T(8,128)(2,1)S(1)}) custom-call(bf16[2,2,64,1152]{3,2,1,0:T(8,128)(2,1)S(1)} %get-tuple-element.32.fa_ref, f32[2,2,64,192]{3,2,1,0:T(8,128)S(1)} %get-tuple-element.33.mid_ref, f32[3,2,2,64,192]{4,3,2,1,0:T(8,128)S(1)} %shard_map.95.part_ref, bf16[3,3,3,192,384]{4,3,2,1,0:T(8,128)(2,1)S(1)} %bitcast.9), custom_call_target="tpu_custom_call" | custom-call | flops 100000000 | bytes 565248 | tf_op jit(solution)/shard_map/pallas_call | solution.py:18
  16.1 0.1 collective-permute-start.5
  16.2 0.2 copy-done.4
  16.3 0.0 copy-done.5
  16.4 0.0 copy-done.6
  16.4 0.0 copy-done.7
  16.4 0.9 %shard_map.98.rest_ref = f32[2,4,64,192]{3,2,1,0:T(8,128)S(1)} custom-call(bf16[2,2,64,576]{3,2,1,0:T(8,128)(2,1)S(1)} %get-tuple-element.36.near_ref, bf16[2,2,64,576]{3,2,1,0:T(8,128)(2,1)S(1)} %get-tuple-element.29.after_ref.far_ref, bf16[3,3,3,192,192]{4,3,2,1,0:T(8,128)(2,1)S(1)} %copy-done.1, bf16[4,2,64,384]{3,2,1,0:T(8,128)(2,1)S(1)} %copy-done.4, ...), custom_call_target="tpu_custom_call" | custom-call | flops 1600000000 | bytes 351590 | tf_op jit(solution)/shard_map/pallas_call | solution.py:18
  17.3 0.2 collective-permute-done.5.ra_ref
  17.5 1.1 %shard_map.99.part_ref = f32[2,4,64,192]{3,2,1,0:T(8,128)S(1)} custom-call(bf16[2,64,384]{2,1,0:T(8,128)(2,1)S(1)} %collective-permute-done.5.ra_ref, f32[2,2,64,192]{3,2,1,0:T(8,128)S(1)} %get-tuple-element.35.own_ref, f32[1,192]{1,0:T(1,128)S(1)} %bitcast.12, f32[1,192]{1,0:T(1,128)S(1)} %bitcast.16, bf16[3,3,3,192,192]{4,3,2,1,0:T(8,128)(2,1)S(1)} %copy-done.1, ...), custom_call_target="tpu_custom_call" | custom-call | flops 100000000 | bytes 307353 | tf_op jit(solution)/shard_map/pallas_call | solution.py:18
  18.5 4.2 %collective-permute-done.2.q_ref = bf16[2,64,384]{2,1,0:T(8,128)(2,1)S(1)} collective-permute-done((bf16[2,64,384]{2,1,0:T(8,128)(2,1)S(1)}, bf16[2,64,384]{2,1,0:T(8,128)(2,1)S(1)}, u32[]{:S(2)}, u32[]{:S(2)}) %collective-permute-start.2) | collective-permute-done | bytes 98336 | tf_op jit(solution)/shard_map/ppermute | solution.py:239
  22.8 0.0 collective-permute-done.4.rb_ref
  22.8 1.8 %shard_map.100 = bf16[4,2,64,192]{3,2,1,0:T(8,128)(2,1)} custom-call(bf16[2,64,384]{2,1,0:T(8,128)(2,1)S(1)} %collective-permute-done.2.q_ref, bf16[2,64,384]{2,1,0:T(8,128)(2,1)S(1)} %collective-permute-done.4.rb_ref, f32[2,2,64,192]{3,2,1,0:T(8,128)S(1)} %get-tuple-element.31.own_ref, f32[2,4,64,192]{3,2,1,0:T(8,128)S(1)} %shard_map.99.part_ref, ...), custom_call_target="tpu_custom_call" | custom-call | flops 100000000 | bytes 297523 | tf_op jit(solution)/shard_map/pallas_call | solution.py:18
Async XLA Ops:
  0.0 3.5 %copy-start = (bf16[3,3,3,384,192]{3,4,2,1,0:T(8,128)(2,1)S(1)}, bf16[3,3,3,384,192]{3,4,2,1,0:T(8,128)(2,1)}, u32[]{:S(2)}) copy-start(bf16[3,3,3,384,192]{3,4,2,1,0:T(8,128)(2,1)} %param.10) | copy-start | bytes 11943940
  1.8 12.4 %collective-permute-start.3 = (bf16[2,2,64,384]{3,2,1,0:T(8,128)(2,1)S(1)}, bf16[2,2,64,384]{3,2,1,0:T(8,128)(2,1)S(1)}, u32[]{:S(2)}, u32[]{:S(2)}) collective-permute-start(bf16[2,2,64,384]{3,2,1,0:T(8,128)(2,1)S(1)} %get-tuple-element.28), channel_id=1, source_target_pairs={{0,32},{32,64},{64,96},{96,128},{128,160},{160,192},{192,224},{224... | collective-permute-start | bytes 589832 | tf_op jit(solution)/shard_map/ppermute | solution.py:227
  5.3 6.2 %collective-permute-start = (bf16[2,64,384]{2,1,0:T(8,128)(2,1)S(1)}, bf16[2,64,384]{2,1,0:T(8,128)(2,1)S(1)}, u32[]{:S(2)}, u32[]{:S(2)}) collective-permute-start(bf16[2,64,384]{2,1,0:T(8,128)(2,1)S(1)} %get-tuple-element.22), channel_id=1, source_target_pairs={{1,2},{2,1},{3,4},{4,3},{5,6},{6,5},{7,8},{8,7},{9,10},{10,9},{11,... | collective-permute-start | bytes 294920 | tf_op jit(solution)/shard_map/ppermute | solution.py:231
  5.4 2.4 %copy-start.1 = (bf16[3,3,3,192,192]{4,3,2,1,0:T(8,128)(2,1)S(1)}, bf16[3,3,3,192,192]{4,3,2,1,0:T(8,128)(2,1)}, u32[]{:S(2)}) copy-start(bf16[3,3,3,192,192]{4,3,2,1,0:T(8,128)(2,1)} %w_ref.9) | copy-start | bytes 5971972
  5.4 2.4 %copy-start.2 = (f32[192]{0:T(256)S(1)}, f32[192]{0:T(256)}, u32[]{:S(2)}) copy-start(f32[192]{0:T(256)} %param.11) | copy-start | bytes 2308
  5.4 2.4 %copy-start.3 = (f32[192]{0:T(256)S(1)}, f32[192]{0:T(256)}, u32[]{:S(2)}) copy-start(f32[192]{0:T(256)} %param.15) | copy-start | bytes 2308
  5.4 2.4 %collective-permute-start.1 = (bf16[2,64,384]{2,1,0:T(8,128)(2,1)S(1)}, bf16[2,64,384]{2,1,0:T(8,128)(2,1)S(1)}, u32[]{:S(2)}, u32[]{:S(2)}) collective-permute-start(bf16[2,64,384]{2,1,0:T(8,128)(2,1)S(1)} %get-tuple-element.24), channel_id=1, source_target_pairs={{0,1},{1,0},{2,3},{3,2},{4,5},{5,4},{6,7},{7,6},{8,9},{9,8},{10,11... | collective-permute-start | bytes 294920 | tf_op jit(solution)/shard_map/ppermute | solution.py:232
  12.4 10.4 %collective-permute-start.2 = (bf16[2,64,384]{2,1,0:T(8,128)(2,1)S(1)}, bf16[2,64,384]{2,1,0:T(8,128)(2,1)S(1)}, u32[]{:S(2)}, u32[]{:S(2)}) collective-permute-start(bf16[2,64,384]{2,1,0:T(8,128)(2,1)S(1)} %get-tuple-element.27), channel_id=1, source_target_pairs={{0,32},{32,64},{64,96},{96,128},{128,160},{160,192},{192,224},{224... | collective-permute-start | bytes 294920 | tf_op jit(solution)/shard_map/ppermute | solution.py:239
  15.2 7.5 %collective-permute-start.4 = (bf16[2,64,384]{2,1,0:T(8,128)(2,1)S(1)}, bf16[2,64,384]{2,1,0:T(8,128)(2,1)S(1)}, u32[]{:S(2)}, u32[]{:S(2)}) collective-permute-start(bf16[2,64,384]{2,1,0:T(8,128)(2,1)S(1)} %get-tuple-element.30), channel_id=1, source_target_pairs={{1,2},{2,1},{3,4},{4,3},{5,6},{6,5},{7,8},{8,7},{9,10},{10,9},{11,... | collective-permute-start | bytes 294920 | tf_op jit(solution)/shard_map/ppermute | solution.py:243
  15.3 1.0 %copy-start.4 = (bf16[4,2,64,384]{3,2,1,0:T(8,128)(2,1)S(1)}, bf16[4,2,64,384]{3,2,1,0:T(8,128)(2,1)}, u32[]{:S(2)}) copy-start(bf16[4,2,64,384]{3,2,1,0:T(8,128)(2,1)} %x_ref.1) | copy-start | bytes 1179652
  15.4 1.0 %copy-start.5 = (bf16[384,192]{0,1:T(8,128)(2,1)S(1)}, bf16[384,192]{0,1:T(8,128)(2,1)}, u32[]{:S(2)}) copy-start(bf16[384,192]{0,1:T(8,128)(2,1)} %param.16) | copy-start | bytes 442372
  15.4 1.0 %copy-start.6 = (f32[192]{0:T(256)S(1)}, f32[192]{0:T(256)}, u32[]{:S(2)}) copy-start(f32[192]{0:T(256)} %param.14) | copy-start | bytes 2308
  15.4 1.0 %copy-start.7 = (f32[192]{0:T(256)S(1)}, f32[192]{0:T(256)}, u32[]{:S(2)}) copy-start(f32[192]{0:T(256)} %param.17) | copy-start | bytes 2308
  16.1 1.4 %collective-permute-start.5 = (bf16[2,64,384]{2,1,0:T(8,128)(2,1)S(1)}, bf16[2,64,384]{2,1,0:T(8,128)(2,1)S(1)}, u32[]{:S(2)}, u32[]{:S(2)}) collective-permute-start(bf16[2,64,384]{2,1,0:T(8,128)(2,1)S(1)} %get-tuple-element.34), channel_id=1, source_target_pairs={{0,1},{1,0},{2,3},{3,2},{4,5},{5,4},{6,7},{7,6},{8,9},{9,8},{10,11... | collective-permute-start | bytes 294920 | tf_op jit(solution)/shard_map/ppermute | solution.py:245

commit v8 on v6

--- a/solution.py
+++ b/solution.py
@@ -78,13 +78,15 @@
         second = act(hidden.astype(BF16).astype(F32), gain_ref[...])
         if outer:
             second = jnp.where(jnp.logical_and(edge, side == n), 0.0, second)
-        sa_ref[n] = taps(second)
+        for k in range(3):
+            sa_ref[n, :, :, 256 * k : 256 * k + 192] = taps(second)[..., 192 * k : 192 * k + 192]
+            sa_ref[n, :, :, 256 * k + 192 : 256 * k + 256] = jnp.zeros((2, COLS, 64), BF16)
 
 
 def second_sums(sa_ref, w_ref, side, parts, acc_ref):
     def dot(a, w):
         count = a.shape[0] * a.shape[1]
-        out = jnp.dot(a.reshape(count * COLS, 576), w.reshape(576, 192), preferred_element_type=F32)
+        out = jnp.dot(a.reshape(count * COLS, 768), w, preferred_element_type=F32)
         return out.reshape(a.shape[0], a.shape[1], COLS, 192)
 
     for i, source, frames in parts:
@@ -140,6 +142,14 @@
 FIRST = [(i, slice(0, 2), slice(2 - i, 4 - i)) for i in range(3)]
 
 
+def widen_kernel(w_ref, wide_ref):
+    for i in range(3):
+        for j in range(3):
+            for k in range(3):
+                wide_ref[i, j, 256 * k : 256 * k + 192] = w_ref[i, j, k]
+                wide_ref[i, j, 256 * k + 192 : 256 * k + 256] = jnp.zeros((64, 192), BF16)
+
+
 def near_kernel(ra_ref, own_ref, bias_ref, gain_ref, w_ref, sa_ref, q_ref):
     side = 1 - outer_side()
     second_act(own_ref, ra_ref, bias_ref, gain_ref, side, False, sa_ref)
@@ -203,7 +213,7 @@
     w1 = jnp.swapaxes(w1, 3, 4)
     sw = jnp.swapaxes(sw, 0, 1)
     b1, b2, g2, sb = (v.reshape(1, -1) for v in (b1, b2, g2, sb))
-    half = shape((2, 2, COLS, 576))
+    half = shape((2, 2, COLS, 768))
     sums, edges = shape((4, 2, COLS, 192), F32), shape((2, COLS, 384))
 
     fa, give = call(
@@ -218,6 +228,7 @@
     b23 = lax.ppermute(edge_b, ("tm", "rows"), outer)
     a23 = lax.ppermute(edge_a, "rows", inner)
     part = call(between_kernel, [sums], fa, w1, flops=16*10**9)[0]
+    w2 = call(widen_kernel, [shape((3, 3, 768, 192))], w2)[0]
     near, part_q = call(near_kernel, [half, shape((2, 2, COLS, 192), F32)], a23, own23, b1, g2, w2, flops=10**9)
     far, give = call(
         next_kernel, [half, edges], b23, own23, part_q, b1, g2, w2, flops=10**9,
@@ -233,11 +244,11 @@
     rest = call(rest_kernel, [shape((2, 4, COLS, 192), F32)], near, far, w2, x, sw, b2, sb, flops=16*10**9)[0]
     total = call(
         second_near_kernel, [shape((2, 4, COLS, 192), F32)], a01, own01, b1, g2, w2, rest, flops=10**9,
-        scratch=[pltpu.VMEM((2, 2, COLS, 576), BF16)],
+        scratch=[pltpu.VMEM((2, 2, COLS, 768), BF16)],
     )[0]
     return call(
         second_kernel, [shape((4, 2, COLS, 192))], q, b01, own01, total, b1, g2, w2, flops=10**9,
-        scratch=[pltpu.VMEM((2, 4, COLS, 192), F32), pltpu.VMEM((2, 2, COLS, 576), BF16)],
+        scratch=[pltpu.VMEM((2, 4, COLS, 192), F32), pltpu.VMEM((2, 2, COLS, 768), BF16)],
     )[0]
 
 

time: 24.5 us -> 24.6 us (level)
  Pallas kernels: 11.2 us -> 11.7 us
  waiting for transfers between devices: 8.04 us -> 7.6 us
    pallas_call x9 -> x10, Pallas kernels: 11.2 us -> 11.7 us  [call(): pl.pallas_call(body, out_shape=outs, in_specs=[HBM if n in in_hbm else VM...]
    ppermute x1, waiting for transfers between devices: 2.99 us -> 2.64 us  [per_device(): b23 = lax.ppermute(edge_b, ('tm', 'rows'), outer)]
  transfers between devices with their start and end apart: 6 -> 6, of which waited for: 4 -> 4; matrix products, arithmetic and copies ran while one was open for 0% -> 0% of each run, Pallas kernels for 31% -> 33%
where the time goes in v8:
time: 24.6 us; the launch traced here: 24.4 us
  Pallas kernels  11.7 us (48%)
  waiting for transfers between devices  7.6 us (31%)
  starting transfers between devices  4.91 us (20%)
    pallas_call x10, Pallas kernels, call(): pl.pallas_call(body, out_shape=outs, in_specs=[HBM if n in in_hbm else VM...  11.7 us
    ppermute x1, waiting for transfers between devices, per_device(): q = lax.ppermute(give, 'tm', ring)  4.48 us
    ppermute x1, waiting for transfers between devices, per_device(): b23 = lax.ppermute(edge_b, ('tm', 'rows'), outer)  2.64 us
    ppermute x1, starting transfers between devices, per_device(): q = lax.ppermute(give, 'tm', ring)  1.66 us
    ppermute x1, starting transfers between devices, per_device(): came = lax.ppermute(give, 'tm', ring)  1.65 us
    ppermute x1, starting transfers between devices, per_device(): a23 = lax.ppermute(edge_a, 'rows', inner)  1.31 us
  transfers between devices with their start and end apart: 6, of which 4 were waited for; matrix products, arithmetic and copies ran while one was open for 0% of the time, Pallas kernels for 33%

profile of v8, /device:TPU:132, one launch (start us, length us, event | category | flops | bytes accessed | tf_op | source)
XLA Modules:
  0.0 24.4 jit_solution(16533140194754766845)
XLA Ops:
  0.0 0.0 copy-start
  0.0 1.8 %shard_map.91 = (bf16[2,4,64,1152]{3,2,1,0:T(8,128)(2,1)S(1)}, bf16[2,2,64,384]{3,2,1,0:T(8,128)(2,1)S(1)}) custom-call(bf16[4,2,64,384]{3,2,1,0:T(8,128)(2,1)} %x_ref.1, f32[384]{0:T(512)} %g_hbm.1), custom_call_target="tpu_custom_call" | custom-call | flops 4000000000 | bytes 177100 | tf_op jit(solution)/shard_map/pallas_call | solution.py:18
  1.8 0.0 copy-start.1
  1.9 1.7 %collective-permute-start.3 = (bf16[2,2,64,384]{3,2,1,0:T(8,128)(2,1)S(1)}, bf16[2,2,64,384]{3,2,1,0:T(8,128)(2,1)S(1)}, u32[]{:S(2)}, u32[]{:S(2)}) collective-permute-start(bf16[2,2,64,384]{3,2,1,0:T(8,128)(2,1)S(1)} %get-tuple-element.23), channel_id=1, source_target_pairs={{0,32},{32,64},{64,96},{96,128},{128,160},{160,192},{192,224},{224... | collective-permute-start | bytes 589832 | tf_op jit(solution)/shard_map/ppermute | solution.py:226
  3.5 0.0 copy-done
  3.5 1.7 %shard_map.92 = (f32[4,2,64,192]{3,2,1,0:T(8,128)S(1)}, bf16[2,64,384]{2,1,0:T(8,128)(2,1)S(1)}, bf16[2,64,384]{2,1,0:T(8,128)(2,1)S(1)}) custom-call(bf16[2,4,64,1152]{3,2,1,0:T(8,128)(2,1)S(1)} %get-tuple-element.17.fa_ref, bf16[3,3,3,192,384]{4,3,2,1,0:T(8,128)(2,1)S(1)} %bitcast.6), custom_call_target="tpu_custom_call" | custom-call | flops 100000000 | bytes 575078 | tf_op jit(solution)/shard_map/pallas_call | solution.py:18
  5.2 0.1 collective-permute-start
  5.3 1.3 %collective-permute-start.1 = (bf16[2,64,384]{2,1,0:T(8,128)(2,1)S(1)}, bf16[2,64,384]{2,1,0:T(8,128)(2,1)S(1)}, u32[]{:S(2)}, u32[]{:S(2)}) collective-permute-start(bf16[2,64,384]{2,1,0:T(8,128)(2,1)S(1)} %get-tuple-element.20), channel_id=1, source_target_pairs={{0,1},{1,0},{2,3},{3,2},{4,5},{5,4},{6,7},{7,6},{8,9},{9,8},{10,11... | collective-permute-start | bytes 294920 | tf_op jit(solution)/shard_map/ppermute | solution.py:229
  6.6 0.0 copy-done.1
  6.6 0.2 shard_map.93.w_ref
  6.9 0.0 copy-start.2
  6.9 0.0 copy-start.3
  6.9 1.1 %shard_map.96.part_ref = f32[4,2,64,192]{3,2,1,0:T(8,128)S(1)} custom-call(bf16[2,4,64,1152]{3,2,1,0:T(8,128)(2,1)S(1)} %get-tuple-element.17.fa_ref, bf16[3,3,3,192,384]{4,3,2,1,0:T(8,128)(2,1)S(1)} %bitcast.7), custom_call_target="tpu_custom_call" | custom-call | flops 1600000000 | bytes 555417 | tf_op jit(solution)/shard_map/pallas_call | solution.py:18
  8.0 0.0 collective-permute-done.1.ra_ref
  8.0 0.0 copy-done.2
  8.0 0.0 copy-done.3
  8.0 0.8 %shard_map.94 = (bf16[2,2,64,768]{3,2,1,0:T(8,128)(2,1)S(1)}, f32[2,2,64,192]{3,2,1,0:T(8,128)S(1)}) custom-call(bf16[2,64,384]{2,1,0:T(8,128)(2,1)S(1)} %collective-permute-done.1.ra_ref, f32[4,2,64,192]{3,2,1,0:T(8,128)S(1)} %get-tuple-element.19.own_ref, f32[1,192]{1,0:T(1,128)S(1)} %bitcast.9, f32[1,192]{1,0:T(1,128)S(1)} %bitcast.13, ...), custom_call_target="tpu_custom_call" | custom-call | flops 100000000 | bytes 373708 | tf_op jit(solution)/shard_map/pallas_call | solution.py:18
  8.8 2.6 %collective-permute-done.rb_ref = bf16[2,64,384]{2,1,0:T(8,128)(2,1)S(1)} collective-permute-done((bf16[2,64,384]{2,1,0:T(8,128)(2,1)S(1)}, bf16[2,64,384]{2,1,0:T(8,128)(2,1)S(1)}, u32[]{:S(2)}, u32[]{:S(2)}) %collective-permute-start) | collective-permute-done | bytes 98336 | tf_op jit(solution)/shard_map/ppermute | solution.py:228
  11.5 0.9 %shard_map.95 = (bf16[2,2,64,768]{3,2,1,0:T(8,128)(2,1)S(1)}, bf16[2,64,384]{2,1,0:T(8,128)(2,1)S(1)}) custom-call(bf16[2,64,384]{2,1,0:T(8,128)(2,1)S(1)} %collective-permute-done.rb_ref, f32[4,2,64,192]{3,2,1,0:T(8,128)S(1)} %get-tuple-element.19.own_ref, f32[2,2,64,192]{3,2,1,0:T(8,128)S(1)} %get-tuple-element.21.part_ref, f32[1,192]{1,0:T(1,128)S(1)} %bitcast.10, ...), custom_call_target="tpu_custom_call" | custom-call | flops 100000000 | bytes 383539 | tf_op jit(solution)/shard_map/pallas_call | solution.py:18
  12.4 0.0 copy-start.4
  12.4 0.0 copy-start.5
  12.4 0.0 copy-start.6
  12.4 0.0 copy-start.7
  12.4 1.7 %collective-permute-start.2 = (bf16[2,64,384]{2,1,0:T(8,128)(2,1)S(1)}, bf16[2,64,384]{2,1,0:T(8,128)(2,1)S(1)}, u32[]{:S(2)}, u32[]{:S(2)}) collective-permute-start(bf16[2,64,384]{2,1,0:T(8,128)(2,1)S(1)} %get-tuple-element.22), channel_id=1, source_target_pairs={{0,32},{32,64},{64,96},{96,128},{128,160},{160,192},{192,224},{224... | collective-permute-start | bytes 294920 | tf_op jit(solution)/shard_map/ppermute | solution.py:237
  14.1 0.2 collective-permute-done.3.t_ref
  14.3 1.2 %shard_map.97 = (f32[4,2,64,192]{3,2,1,0:T(8,128)S(1)}, bf16[2,64,384]{2,1,0:T(8,128)(2,1)S(1)}, bf16[2,64,384]{2,1,0:T(8,128)(2,1)S(1)}) custom-call(bf16[2,2,64,384]{3,2,1,0:T(8,128)(2,1)S(1)} %collective-permute-done.3.t_ref, f32[4,2,64,192]{3,2,1,0:T(8,128)S(1)} %shard_map.96.part_ref, bf16[3,3,3,192,384]{4,3,2,1,0:T(8,128)(2,1)S(1)} %bitcast.8, ...), custom_call_target="tpu_custom_call" | custom-call | flops 100000000 | bytes 555417 | tf_op jit(solution)/shard_map/pallas_call | solution.py:18
  15.5 0.1 collective-permute-start.4
  15.6 0.1 collective-permute-start.5
  15.7 0.0 copy-done.4
  15.7 0.0 copy-done.5
  15.7 0.0 copy-done.6
  15.7 0.0 copy-done.7
  15.7 1.0 %shard_map.98.rest_ref = f32[2,4,64,192]{3,2,1,0:T(8,128)S(1)} custom-call(bf16[2,2,64,768]{3,2,1,0:T(8,128)(2,1)S(1)} %get-tuple-element.28.near_ref, bf16[2,2,64,768]{3,2,1,0:T(8,128)(2,1)S(1)} %get-tuple-element.24.after_ref.far_ref, bf16[3,3,768,192]{3,2,1,0:T(8,128)(2,1)S(1)} %shard_map.93.w_ref, bf16[4,2,64,384]{3,2,1,0:T(8,128)(2,1)S(1)} %copy-done.4, ...), custom_call_target="tpu_custom_call" | custom-call | flops 1600000000 | bytes 437606 | tf_op jit(solution)/shard_map/pallas_call | solution.py:18
  16.7 0.3 %collective-permute-done.5.ra_ref = bf16[2,64,384]{2,1,0:T(8,128)(2,1)S(1)} collective-permute-done((bf16[2,64,384]{2,1,0:T(8,128)(2,1)S(1)}, bf16[2,64,384]{2,1,0:T(8,128)(2,1)S(1)}, u32[]{:S(2)}, u32[]{:S(2)}) %collective-permute-start.5) | collective-permute-done | bytes 98336 | tf_op jit(solution)/shard_map/ppermute | solution.py:243
  17.0 1.1 %shard_map.99.part_ref = f32[2,4,64,192]{3,2,1,0:T(8,128)S(1)} custom-call(bf16[2,64,384]{2,1,0:T(8,128)(2,1)S(1)} %collective-permute-done.5.ra_ref, f32[4,2,64,192]{3,2,1,0:T(8,128)S(1)} %get-tuple-element.26.own_ref, f32[1,192]{1,0:T(1,128)S(1)} %bitcast.11, f32[1,192]{1,0:T(1,128)S(1)} %bitcast.15, bf16[3,3,768,192]{3,2,1,0:T(8,128)(2,1)S(1)} %shard_map.93.w_ref, ...), custom_call_target="tpu_custom_call" | custom-call | flops 100000000 | bytes 393369 | tf_op jit(solution)/shard_map/pallas_call | solution.py:18
  18.1 4.5 %collective-permute-done.2.q_ref = bf16[2,64,384]{2,1,0:T(8,128)(2,1)S(1)} collective-permute-done((bf16[2,64,384]{2,1,0:T(8,128)(2,1)S(1)}, bf16[2,64,384]{2,1,0:T(8,128)(2,1)S(1)}, u32[]{:S(2)}, u32[]{:S(2)}) %collective-permute-start.2) | collective-permute-done | bytes 98336 | tf_op jit(solution)/shard_map/ppermute | solution.py:237
  22.6 0.0 collective-permute-done.4.rb_ref
  22.6 1.9 %shard_map.100 = bf16[4,2,64,192]{3,2,1,0:T(8,128)(2,1)} custom-call(bf16[2,64,384]{2,1,0:T(8,128)(2,1)S(1)} %collective-permute-done.2.q_ref, bf16[2,64,384]{2,1,0:T(8,128)(2,1)S(1)} %collective-permute-done.4.rb_ref, f32[4,2,64,192]{3,2,1,0:T(8,128)S(1)} %get-tuple-element.26.own_ref, f32[2,4,64,192]{3,2,1,0:T(8,128)S(1)} %shard_map.99.part_ref, ...), custom_call_target="tpu_custom_call" | custom-call | flops 100000000 | bytes 383539 | tf_op jit(solution)/shard_map/pallas_call | solution.py:18
Async XLA Ops:
  0.0 3.5 %copy-start = (bf16[3,3,3,384,192]{3,4,2,1,0:T(8,128)(2,1)S(1)}, bf16[3,3,3,384,192]{3,4,2,1,0:T(8,128)(2,1)}, u32[]{:S(2)}) copy-start(bf16[3,3,3,384,192]{3,4,2,1,0:T(8,128)(2,1)} %param.10) | copy-start | bytes 11943940
  1.8 4.8 %copy-start.1 = (bf16[3,3,3,192,192]{4,3,2,1,0:T(8,128)(2,1)S(1)}, bf16[3,3,3,192,192]{4,3,2,1,0:T(8,128)(2,1)}, u32[]{:S(2)}) copy-start(bf16[3,3,3,192,192]{4,3,2,1,0:T(8,128)(2,1)} %w_ref.1) | copy-start | bytes 5971972
  1.9 12.4 %collective-permute-start.3 = (bf16[2,2,64,384]{3,2,1,0:T(8,128)(2,1)S(1)}, bf16[2,2,64,384]{3,2,1,0:T(8,128)(2,1)S(1)}, u32[]{:S(2)}, u32[]{:S(2)}) collective-permute-start(bf16[2,2,64,384]{3,2,1,0:T(8,128)(2,1)S(1)} %get-tuple-element.23), channel_id=1, source_target_pairs={{0,32},{32,64},{64,96},{96,128},{128,160},{160,192},{192,224},{224... | collective-permute-start | bytes 589832 | tf_op jit(solution)/shard_map/ppermute | solution.py:226
  5.2 6.2 %collective-permute-start = (bf16[2,64,384]{2,1,0:T(8,128)(2,1)S(1)}, bf16[2,64,384]{2,1,0:T(8,128)(2,1)S(1)}, u32[]{:S(2)}, u32[]{:S(2)}) collective-permute-start(bf16[2,64,384]{2,1,0:T(8,128)(2,1)S(1)} %get-tuple-element.18), channel_id=1, source_target_pairs={{1,2},{2,1},{3,4},{4,3},{5,6},{6,5},{7,8},{8,7},{9,10},{10,9},{11,... | collective-permute-start | bytes 294920 | tf_op jit(solution)/shard_map/ppermute | solution.py:228
  5.3 2.7 %collective-permute-start.1 = (bf16[2,64,384]{2,1,0:T(8,128)(2,1)S(1)}, bf16[2,64,384]{2,1,0:T(8,128)(2,1)S(1)}, u32[]{:S(2)}, u32[]{:S(2)}) collective-permute-start(bf16[2,64,384]{2,1,0:T(8,128)(2,1)S(1)} %get-tuple-element.20), channel_id=1, source_target_pairs={{0,1},{1,0},{2,3},{3,2},{4,5},{5,4},{6,7},{7,6},{8,9},{9,8},{10,11... | collective-permute-start | bytes 294920 | tf_op jit(solution)/shard_map/ppermute | solution.py:229
  6.9 1.1 %copy-start.2 = (f32[192]{0:T(256)S(1)}, f32[192]{0:T(256)}, u32[]{:S(2)}) copy-start(f32[192]{0:T(256)} %param.11) | copy-start | bytes 2308
  6.9 1.1 %copy-start.3 = (f32[192]{0:T(256)S(1)}, f32[192]{0:T(256)}, u32[]{:S(2)}) copy-start(f32[192]{0:T(256)} %param.15) | copy-start | bytes 2308
  12.4 3.3 %copy-start.4 = (bf16[4,2,64,384]{3,2,1,0:T(8,128)(2,1)S(1)}, bf16[4,2,64,384]{3,2,1,0:T(8,128)(2,1)}, u32[]{:S(2)}) copy-start(bf16[4,2,64,384]{3,2,1,0:T(8,128)(2,1)} %x_ref.1) | copy-start | bytes 1179652
  12.4 3.3 %copy-start.5 = (bf16[384,192]{0,1:T(8,128)(2,1)S(1)}, bf16[384,192]{0,1:T(8,128)(2,1)}, u32[]{:S(2)}) copy-start(bf16[384,192]{0,1:T(8,128)(2,1)} %param.16) | copy-start | bytes 442372
  12.4 3.3 %copy-start.6 = (f32[192]{0:T(256)S(1)}, f32[192]{0:T(256)}, u32[]{:S(2)}) copy-start(f32[192]{0:T(256)} %param.14) | copy-start | bytes 2308
  12.4 3.3 %copy-start.7 = (f32[192]{0:T(256)S(1)}, f32[192]{0:T(256)}, u32[]{:S(2)}) copy-start(f32[192]{0:T(256)} %param.17) | copy-start | bytes 2308
  12.4 10.1 %collective-permute-start.2 = (bf16[2,64,384]{2,1,0:T(8,128)(2,1)S(1)}, bf16[2,64,384]{2,1,0:T(8,128)(2,1)S(1)}, u32[]{:S(2)}, u32[]{:S(2)}) collective-permute-start(bf16[2,64,384]{2,1,0:T(8,128)(2,1)S(1)} %get-tuple-element.22), channel_id=1, source_target_pairs={{0,32},{32,64},{64,96},{96,128},{128,160},{160,192},{192,224},{224... | collective-permute-start | bytes 294920 | tf_op jit(solution)/shard_map/ppermute | solution.py:237
  15.5 7.1 %collective-permute-start.4 = (bf16[2,64,384]{2,1,0:T(8,128)(2,1)S(1)}, bf16[2,64,384]{2,1,0:T(8,128)(2,1)S(1)}, u32[]{:S(2)}, u32[]{:S(2)}) collective-permute-start(bf16[2,64,384]{2,1,0:T(8,128)(2,1)S(1)} %get-tuple-element.25), channel_id=1, source_target_pairs={{1,2},{2,1},{3,4},{4,3},{5,6},{6,5},{7,8},{8,7},{9,10},{10,9},{11,... | collective-permute-start | bytes 294920 | tf_op jit(solution)/shard_map/ppermute | solution.py:242
  15.6 1.4 %collective-permute-start.5 = (bf16[2,64,384]{2,1,0:T(8,128)(2,1)S(1)}, bf16[2,64,384]{2,1,0:T(8,128)(2,1)S(1)}, u32[]{:S(2)}, u32[]{:S(2)}) collective-permute-start(bf16[2,64,384]{2,1,0:T(8,128)(2,1)S(1)} %get-tuple-element.27), channel_id=1, source_target_pairs={{0,1},{1,0},{2,3},{3,2},{4,5},{5,4},{6,7},{7,6},{8,9},{9,8},{10,11... | collective-permute-start | bytes 294920 | tf_op jit(solution)/shard_map/ppermute | solution.py:243
